TPU v7x, 128 devices: a whole 4x4x4 slice. The times are simulated.
128 devices in a mesh: blk: 8 (over x_lo, y), row: 16 (over x_hi, z, core).
Axes of the slice: x: 4 (x_hi: 2, x_lo: 2; x = x_hi * 2 + x_lo), y: 4, z: 4, core: 2. Of those that a mesh axis runs over, the one named last changes fastest.
Arguments:
- intersection: bfloat16 [4096, 4096], P('row', 'blk'), may hold values from -0.09375 to 0.09375
- inverse_dev: bfloat16 [4096, 4096], P('row', 'blk'), may hold values from -0.09375 to 0.09375
- hamiltonian: bfloat16 [4096, 4096], P('row', 'blk'), may hold values from -0.0625 to 0.0625
- chem_potential: float32 [1], replicated, may hold values from -0.4 to 0.4
- pattern_s: int32 [32, 32], replicated, may hold values 0 or 1
- pattern_z: int32 [32, 32], replicated, may hold values 0 or 1
- pattern_h: int32 [32, 32], replicated, may hold values 0 or 1
- fill_inverse: int32 [32, 32], replicated, may hold values 0 or 1
- fill_sign: int32 [32, 32], replicated, may hold values 0 or 1
Outputs:
- refined_inverse: bfloat16 [4096, 4096], P('row', 'blk')
- inverse_error: bfloat16 [4096, 4096], P('row', 'blk')
- sign_step: bfloat16 [4096, 4096], P('row', 'blk')
All inputs are finite; a program needn't handle non-finite values.
Results may differ from a plain program's by a relative error of at most 0.0067.
Values may be sent and summed in bfloat16 or wider, within the bound.
No kernel may reach another device: no remote copies, remote signals or barrier semaphores. Data moves between devices by JAX's collectives and lax.ppermute only.
A program may use at most 64 MiB of HBM per device.

v0:
```python
import jax
import jax.numpy as jnp
from jax import lax
from jax.sharding import PartitionSpec as P

BS = 128


def expand_local(pattern, row_start, rows, col_start, cols):
    count = pattern.shape[0]
    labels = jnp.arange(count, dtype=jnp.int32)
    row_blocks = (row_start + jnp.arange(rows, dtype=jnp.int32)) // BS
    col_blocks = (col_start + jnp.arange(cols, dtype=jnp.int32)) // BS
    row_pick = (row_blocks[:, None] == labels[None, :]).astype(jnp.float32)
    col_pick = (col_blocks[:, None] == labels[None, :]).astype(jnp.float32)
    inner = jnp.dot(row_pick, pattern.astype(jnp.float32), precision=lax.Precision.HIGHEST)
    return jnp.dot(inner, col_pick.T, precision=lax.Precision.HIGHEST)


def make_folder(panel, piece):
    return jnp.dot(panel, piece, preferred_element_type=jnp.float32)


def body(
    intersection,
    inverse_dev,
    hamiltonian,
    chem_potential,
    pattern_s,
    pattern_z,
    pattern_h,
    fill_inverse,
    fill_sign,
):
    rows, cols = intersection.shape
    row_start = lax.axis_index("row") * rows
    col_start = lax.axis_index("blk") * cols
    ident = (
        (row_start + jnp.arange(rows, dtype=jnp.int32))[:, None]
        == (col_start + jnp.arange(cols, dtype=jnp.int32))[None, :]
    ).astype(jnp.float32)
    seff = (
        ident
        + 0.35
        * expand_local(pattern_s, row_start, rows, col_start, cols)
        * intersection.astype(jnp.float32)
    ).astype(jnp.bfloat16)
    zeff = (
        ident
        - 0.35
        * expand_local(pattern_z, row_start, rows, col_start, cols)
        * inverse_dev.astype(jnp.float32)
    ).astype(jnp.bfloat16)
    heff = (
        expand_local(pattern_h, row_start, rows, col_start, cols) * hamiltonian.astype(jnp.float32)
    ).astype(jnp.bfloat16)
    z_rows = lax.all_gather(zeff, "blk", axis=1, tiled=True)
    s_cols = lax.all_gather(seff, "row", axis=0, tiled=True)
    first = jnp.dot(z_rows, s_cols, preferred_element_type=jnp.float32).astype(jnp.bfloat16)
    f_rows = lax.all_gather(first, "blk", axis=1, tiled=True)
    second = make_folder(f_rows, lax.all_gather(zeff, "row", axis=0, tiled=True))
    keep_inverse = expand_local(fill_inverse, row_start, rows, col_start, cols)
    refined = (keep_inverse * (2.0 * zeff.astype(jnp.float32) - second)).astype(jnp.bfloat16)
    r_rows = lax.all_gather(refined, "blk", axis=1, tiled=True)
    error = (ident - jnp.dot(r_rows, s_cols, preferred_element_type=jnp.float32)).astype(
        jnp.bfloat16
    )
    third = make_folder(r_rows, lax.all_gather(heff, "row", axis=0, tiled=True))
    keep_sign = expand_local(fill_sign, row_start, rows, col_start, cols)
    shifted = (keep_sign * third - chem_potential[0] * ident).astype(jnp.bfloat16)
    x_rows = lax.all_gather(shifted, "blk", axis=1, tiled=True)
    squared = make_folder(x_rows, lax.all_gather(shifted, "row", axis=0, tiled=True))
    square = (keep_sign * squared).astype(jnp.bfloat16)
    cube = make_folder(x_rows, lax.all_gather(square, "row", axis=0, tiled=True))
    sign = (0.5 * (3.0 * shifted.astype(jnp.float32) - cube)).astype(jnp.bfloat16)
    return (refined, error, sign)


def solution(mesh):
    placed = (P("row", "blk"), P("row", "blk"), P("row", "blk"), P(), P(), P(), P(), P(), P())
    return jax.shard_map(
        body,
        mesh=mesh,
        in_specs=placed,
        out_specs=(P("row", "blk"), P("row", "blk"), P("row", "blk")),
        check_vma=False,
    )
```

profile of v0, /device:TPU:1, one launch (start us, length us, event | category | flops | bytes accessed | tf_op | source)
XLA Modules:
  0.0 479.5 jit_solution(4841761674206644709)
XLA Ops:
  7.3 1.0 fusion.23
  8.3 2.2 fusion.10
  10.5 0.0 all-gather.12.cloned.1.call-start
  10.5 1.0 fusion.22
  11.5 2.2 fusion.9
  13.7 0.0 all-gather.16.cloned.1.call-start
  13.8 0.7 all-gather.16.cloned.1.call-update
  14.5 35.2 %all-gather.10.cloned.1.call-done = bf16[256,4096]{1,0:T(8,128)(2,1)} async-done(((bf16[256,512]{1,0:T(8,128)(2,1)}), bf16[256,4096]{1,0:T(8,128)(2,1)}) %all-gather.10.cloned.1.call-update) | async-done | bytes 2097168 | tf_op jit(solution)/shard_map/all_gather | solution.py:57
  49.7 63.2 %all-gather.12.cloned.1.call-done = bf16[4096,512]{1,0:T(8,128)(2,1)} async-done(((bf16[256,512]{1,0:T(8,128)(2,1)}), bf16[4096,512]{1,0:T(8,128)(2,1)}) %all-gather.12.cloned.1.call-update) | async-done | bytes 4194320 | tf_op jit(solution)/shard_map/all_gather | solution.py:58
  112.9 4.8 convolution_convert_fusion
  117.7 0.0 all-gather.20.cloned.1.call-start
  117.8 0.3 fusion.20
  118.0 1.2 fusion.12
  119.3 0.0 all-gather.18.cloned.1.call-start
  119.3 0.3 fusion.24
  119.6 49.1 %all-gather.16.cloned.1.call-done = bf16[4096,512]{1,0:T(8,128)(2,1)} async-done(((bf16[256,512]{1,0:T(8,128)(2,1)}), bf16[4096,512]{1,0:T(8,128)(2,1)}) %all-gather.16.cloned.1.call-update) | async-done | bytes 4194320 | tf_op jit(solution)/shard_map/all_gather | solution.py:61
  168.7 35.3 %all-gather.14.cloned.1.call-done = bf16[256,4096]{1,0:T(8,128)(2,1)} async-done(((bf16[256,512]{1,0:T(8,128)(2,1)}), bf16[256,4096]{1,0:T(8,128)(2,1)}) %all-gather.14.cloned.1.call-update) | async-done | bytes 2097168 | tf_op jit(solution)/shard_map/all_gather | solution.py:60
  204.0 4.1 convolution_subtract_fusion.2
  208.1 1.2 fusion.11
  209.3 0.0 all-gather.22.cloned.1.call-start
  210.0 0.3 fusion.21
  210.3 0.5 fusion.14
  210.8 55.7 %all-gather.20.cloned.1.call-done = bf16[4096,512]{1,0:T(8,128)(2,1)} async-done(((bf16[256,512]{1,0:T(8,128)(2,1)}), bf16[4096,512]{1,0:T(8,128)(2,1)}) %all-gather.20.cloned.1.call-update) | async-done | bytes 4194320 | tf_op jit(solution)/shard_map/all_gather | solution.py:68
  266.5 35.3 %all-gather.18.cloned.1.call-done = bf16[256,4096]{1,0:T(8,128)(2,1)} async-done(((bf16[256,512]{1,0:T(8,128)(2,1)}), bf16[256,4096]{1,0:T(8,128)(2,1)}) %all-gather.18.cloned.1.call-update) | async-done | bytes 2097168 | tf_op jit(solution)/shard_map/all_gather | solution.py:64
  301.8 4.8 fusion.6
  306.7 0.7 all-gather.24.cloned.1.call-update
  307.4 40.0 %all-gather.22.cloned.1.call-done = bf16[256,4096]{1,0:T(8,128)(2,1)} async-done(((bf16[256,512]{1,0:T(8,128)(2,1)}), bf16[256,4096]{1,0:T(8,128)(2,1)}) %all-gather.22.cloned.1.call-update) | async-done | bytes 2097168 | tf_op jit(solution)/shard_map/all_gather | solution.py:71
  347.4 63.2 %all-gather.24.cloned.1.call-done = bf16[4096,512]{1,0:T(8,128)(2,1)} async-done(((bf16[256,512]{1,0:T(8,128)(2,1)}), bf16[4096,512]{1,0:T(8,128)(2,1)}) %all-gather.24.cloned.1.call-update) | async-done | bytes 4194320 | tf_op jit(solution)/shard_map/all_gather | solution.py:72
  410.5 4.8 fusion.13
  415.4 4.2 fusion.7
  419.6 48.6 %all-gather.26.cloned.1.call-done = bf16[4096,512]{1,0:T(8,128)(2,1)} async-done(((bf16[256,512]{1,0:T(8,128)(2,1)}), bf16[4096,512]{1,0:T(8,128)(2,1)}) %all-gather.26.cloned.1.call-update) | async-done | bytes 4194320 | tf_op jit(solution)/shard_map/all_gather | solution.py:74
  468.2 4.8 fusion.8
  (29 shorter events, 0.3 us)
Async XLA Ops:
  7.2 42.6 %all-gather.10.cloned.1.call-start = ((), (), s32[]{:S(2)}) async-start(), calls=%async_computation | async-start | bytes 2359296 | tf_op jit(solution)/shard_map/all_gather | solution.py:57
  10.5 102.4 %all-gather.12.cloned.1.call-start = ((), (), s32[]{:S(2)}) async-start(), calls=%async_computation.1 | async-start | bytes 4456448 | tf_op jit(solution)/shard_map/all_gather | solution.py:58
  13.7 104.0 %copy-start.3 = (s32[32,32]{1,0:T(8,128)S(1)}, s32[32,32]{1,0:T(8,128)}, u32[]{:S(2)}) copy-start(s32[32,32]{1,0:T(8,128)} %param.15) | copy-start | bytes 12292
  13.7 104.3 %copy-start.2 = (bf16[256,512]{1,0:T(8,128)(2,1)S(1)}, bf16[256,512]{1,0:T(8,128)(2,1)}, u32[]{:S(2)}) copy-start(bf16[256,512]{1,0:T(8,128)(2,1)} %param.11) | copy-start | bytes 786436
  13.7 155.0 %all-gather.16.cloned.1.call-start = ((), (), s32[]{:S(2)}) async-start(), calls=%async_computation.3 | async-start | bytes 4456448 | tf_op jit(solution)/shard_map/all_gather | solution.py:61
  14.5 104.9 %copy-start.4 = (s32[32,32]{1,0:T(8,128)S(1)}, s32[32,32]{1,0:T(8,128)}, u32[]{:S(2)}) copy-start(s32[32,32]{1,0:T(8,128)} %param.16) | copy-start | bytes 12292
  14.5 189.5 %copy-start = (bf16[256,512]{1,0:T(8,128)(2,1)S(1)}, bf16[256,512]{1,0:T(8,128)(2,1)}, u32[]{:S(2)}) copy-start(bf16[256,512]{1,0:T(8,128)(2,1)} %fusion.10) | copy-start | bytes 786436
  14.5 189.5 %all-gather.14.cloned.1.call-start = ((), (), s32[]{:S(2)}) async-start(), calls=%async_computation.2 | async-start | bytes 2359296 | tf_op jit(solution)/shard_map/all_gather | solution.py:60
  117.7 148.8 %all-gather.20.cloned.1.call-start = ((), (), s32[]{:S(2)}) async-start(), calls=%async_computation.5 | async-start | bytes 4456448 | tf_op jit(solution)/shard_map/all_gather | solution.py:68
  119.3 182.5 %all-gather.18.cloned.1.call-start = ((), (), s32[]{:S(2)}) async-start(), calls=%async_computation.4 | async-start | bytes 2359296 | tf_op jit(solution)/shard_map/all_gather | solution.py:64
  119.6 90.4 %copy-start.5 = (s32[32,32]{1,0:T(8,128)S(1)}, s32[32,32]{1,0:T(8,128)}, u32[]{:S(2)}) copy-start(s32[32,32]{1,0:T(8,128)} %param.17) | copy-start | bytes 12292
  209.3 138.1 %all-gather.22.cloned.1.call-start = ((), (), s32[]{:S(2)}) async-start(), calls=%async_computation.6 | async-start | bytes 2359296 | tf_op jit(solution)/shard_map/all_gather | solution.py:71
  306.6 108.8 %copy-start.6 = (bf16[256,4096]{1,0:T(8,128)(2,1)S(1)}, bf16[256,4096]{1,0:T(8,128)(2,1)}, u32[]{:S(2)}) copy-start(bf16[256,4096]{1,0:T(8,128)(2,1)} %all-gather.18.cloned.1.call-done) | copy-start | bytes 6291460
  306.6 103.9 %all-gather.24.cloned.1.call-start = ((), (), s32[]{:S(2)}) async-start(), calls=%async_computation.7 | async-start | bytes 4456448 | tf_op jit(solution)/shard_map/all_gather | solution.py:72
  307.4 160.9 %all-gather.26.cloned.1.call-start = ((), (), s32[]{:S(2)}) async-start(), calls=%async_computation.8 | async-start | bytes 4456448 | tf_op jit(solution)/shard_map/all_gather | solution.py:74
  415.3 52.9 %copy-start.1 = (bf16[256,512]{1,0:T(8,128)(2,1)S(1)}, bf16[256,512]{1,0:T(8,128)(2,1)}, u32[]{:S(2)}) copy-start(bf16[256,512]{1,0:T(8,128)(2,1)} %fusion.6) | copy-start | bytes 786436
Sparse Core Ops, SparseCore 0:
  10.6 39.0 all-gather.9
  52.8 60.0 all-gather.11
  115.9 52.6 all-gather.15
  170.8 33.2 all-gather.13
  206.3 60.0 all-gather.19
  268.5 33.2 all-gather.17
  306.7 40.6 all-gather.21
  350.4 60.0 all-gather.23
  415.5 52.6 all-gather.25
where the time goes:
time: 480 us
  waiting for transfers between devices  427 us (89%)
  matrix products  37.4 us (8%)
  between operations  14.7 us (3%)
    all_gather x1, waiting for transfers between devices, body(): s_cols = lax.all_gather(seff, 'row', axis=0, tiled=True)  63.2 us
    all_gather x1, waiting for transfers between devices, body(): lax.all_gather(shifted, 'row', axis=0, tiled=True)  63.2 us
    all_gather x1, waiting for transfers between devices, body(): third = make_folder(r_rows, lax.all_gather(heff, 'row', axis=0, tiled=True))  55.7 us
    all_gather x1, waiting for transfers between devices, body(): lax.all_gather(zeff, 'row', axis=0, tiled=True)  49.1 us
    all_gather x1, waiting for transfers between devices, body(): lax.all_gather(square, 'row', axis=0, tiled=True)  48.6 us
    all_gather x1, waiting for transfers between devices, body(): x_rows = lax.all_gather(shifted, 'blk', axis=1, tiled=True)  40 us
    all_gather x1, waiting for transfers between devices, body(): f_rows = lax.all_gather(first, 'blk', axis=1, tiled=True)  35.3 us
    all_gather x1, waiting for transfers between devices, body(): r_rows = lax.all_gather(refined, 'blk', axis=1, tiled=True)  35.3 us
  transfers between devices with their start and end apart: 9, of which 9 were waited for; matrix products, arithmetic and copies ran while one was open for 4% of the time, Pallas kernels for 0%

commit v1 on v0

v1 whole, which is shorter than its diff:
```python
import functools

import jax
import jax.numpy as jnp
from jax import lax
from jax.experimental import pallas as pl
from jax.experimental.pallas import tpu as pltpu
from jax.sharding import PartitionSpec as P


BS = 128
AXES = ("blk", "row")
BF = jnp.bfloat16
F32 = jnp.float32
VMEM_LIMIT = 10 * 2**20


def flat(x, y, z, c):
    x, y, z = x % 4, y % 4, z % 4
    return ((x % 2) * 4 + y) * 16 + (x // 2) * 8 + z * 2 + c


def moves(step, step1=None):
    steps = (step, step1 or step)
    return [
        (flat(x, y, z, c), flat(*steps[c](x, y, z, c)))
        for x in range(4)
        for y in range(4)
        for z in range(4)
        for c in range(2)
    ]


def far(x, y, z, c):
    return (x ^ 2, y, z, c)


def z_up(x, y, z, c):
    return (x, y, z + 1, c)


def z_down(x, y, z, c):
    return (x, y, z - 1, c)


NEAR = moves(lambda x, y, z, c: (x ^ 1, y, z, c))
Y_UP = moves(lambda x, y, z, c: (x, y + 1, z, c))
Y_DOWN = moves(lambda x, y, z, c: (x, y - 1, z, c))
Y_TWICE = moves(lambda x, y, z, c: (x, y + 2, z, c))
CORE = moves(lambda x, y, z, c: (x, y, z, 1 - c))
FAR_TWICE = moves(far, lambda x, y, z, c: (x, y, z + 2, c))
UP_DOWN = moves(z_up, z_down)
UP_FAR = moves(z_up, far)
DOWN_STAY = moves(z_down, lambda x, y, z, c: (x, y, z, c))


def send(array, pairs):
    return lax.ppermute(array, AXES, pairs)


def gather_rows(own, relay):
    other = send(own, NEAR)
    below = send(own, Y_UP)
    above = send(own, Y_DOWN)
    other_below = send(other, Y_UP)
    other_above = send(other, Y_DOWN)
    if relay:
        below2 = send(below, Y_UP)
        other2 = send(other_above, Y_DOWN)
    else:
        below2 = send(own, Y_TWICE)
        other2 = send(below2, NEAR)
    return [
        (own, (0, 0)),
        (other, (1, 0)),
        (below, (0, -1)),
        (above, (0, 1)),
        (other_below, (1, -1)),
        (other_above, (1, 1)),
        (below2, (0, 2)),
        (other2, (1, 2)),
    ]


def gather_cols(own):
    half = send(own, CORE)
    block = jnp.concatenate([own, half], 0)
    d0 = send(block, FAR_TWICE)
    d1 = send(block, UP_DOWN)
    d2 = send(d0, UP_FAR)
    d3 = send(d0, DOWN_STAY)
    got = [send(d, CORE) for d in (d0, d1, d2, d3)]
    return [
        (own, half, (0, 0), (0, 0)),
        (d0, got[0], (1, 0), (0, 2)),
        (d1, got[1], (0, -1), (0, 1)),
        (d2, got[2], (1, -1), (1, 2)),
        (d3, got[3], (1, 1), None),
    ]


def place():
    row = lax.axis_index("row")
    blk = lax.axis_index("blk")
    return row, blk


def keep(pattern, row, blk, value):
    rows = []
    for i in range(2):
        cells = []
        for j in range(4):
            on = pattern[row * 2 + i, blk * 4 + j].astype(F32)
            cells.append(value[i * BS : (i + 1) * BS, j * BS : (j + 1) * BS] * on)
        rows.append(jnp.concatenate(cells, 1))
    return jnp.concatenate(rows, 0)


def identity(row, blk, shape):
    below = lax.broadcasted_iota(jnp.int32, shape, 0) + row * shape[0]
    along = lax.broadcasted_iota(jnp.int32, shape, 1) + blk * shape[1]
    return (below == along).astype(F32)


VMEM = pl.BlockSpec(memory_space=pltpu.VMEM)
ANY = pl.BlockSpec(memory_space=pl.ANY)


def fetch(given, held, sems):
    copies = [
        pltpu.make_async_copy(one, two, sems.at[k])
        for k, (one, two) in enumerate(zip(given, held))
    ]
    for copy in copies:
        copy.start()
    for copy in copies:
        copy.wait()


def prepare_body(*refs):
    given, outs, held, sems = refs[:4], refs[4:6], refs[6:10], refs[10]
    fetch(given, held, sems)
    ps, pz, s, z = held
    row, blk = place()
    ident = identity(row, blk, s.shape)
    outs[0][...] = (ident + 0.35 * keep(ps, row, blk, s[...].astype(F32))).astype(BF)
    outs[1][...] = (ident - 0.35 * keep(pz, row, blk, z[...].astype(F32))).astype(BF)


def prepare(ps, pz, s, z):
    out = jax.ShapeDtypeStruct(s.shape, BF)
    return pl.pallas_call(
        prepare_body,
        out_shape=(out, out),
        in_specs=[ANY] * 4,
        out_specs=[VMEM] * 2,
        scratch_shapes=[pltpu.SMEM(ps.shape, jnp.int32)] * 2
        + [pltpu.VMEM(s.shape, BF)] * 2
        + [pltpu.SemaphoreType.DMA((4,))],
        name="prepare",
    )(ps, pz, s, z)


def late_body(*refs):
    given, outs, held, sems = refs[:5], refs[5:9], refs[9:14], refs[14]
    fetch(given, held, sems)
    ph, fi, fs, mu, h = held
    row, blk = place()
    ones = jnp.ones(h.shape, F32)
    outs[0][...] = keep(ph, row, blk, h[...].astype(F32)).astype(BF)
    outs[1][...] = keep(fi, row, blk, ones).astype(BF)
    outs[2][...] = keep(fs, row, blk, ones).astype(BF)
    outs[3][...] = jnp.full(outs[3].shape, mu[0], F32)


def prepare_late(ph, fi, fs, mu, h):
    out = jax.ShapeDtypeStruct(h.shape, BF)
    return pl.pallas_call(
        late_body,
        out_shape=(out, out, out, jax.ShapeDtypeStruct((8, BS), F32)),
        in_specs=[ANY] * 5,
        out_specs=[VMEM] * 4,
        scratch_shapes=[pltpu.SMEM(ph.shape, jnp.int32)] * 3
        + [pltpu.SMEM((1,), F32), pltpu.VMEM(h.shape, BF)]
        + [pltpu.SemaphoreType.DMA((5,))],
        name="prepare_late",
    )(ph, fi, fs, mu, h)


def product_body(finish, n_extra, n_out, a_sources, b_sources, *refs):
    extras, refs = refs[:n_extra], refs[n_extra:]
    a_refs, refs = refs[: len(a_sources)], refs[len(a_sources) :]
    b_refs, refs = refs[: 2 * len(b_sources)], refs[2 * len(b_sources) :]
    outs, refs = refs[:n_out], refs[n_out:]
    b_held, sems = refs
    row, blk = place()
    core = row % 2
    xh, z = row // 8, (row // 2) % 4
    xl, y = blk // 4, blk % 4
    rows = a_refs[0].shape[0]

    def start_of(bit, ring, source):
        return (((bit + source[0]) % 2) * 4 + (ring + source[1] + 4) % 4) * (2 * rows)

    waits = []

    def bring(ref, fetcher, source):
        at = start_of(xh, z, source)
        for k in range(ref.shape[0] // rows):
            half = fetcher if k == 0 else 1 - fetcher
            copy = pltpu.make_async_copy(
                ref.at[pl.ds(k * rows, rows)],
                b_held.at[pl.ds(pl.multiple_of(at + half * rows, rows), rows)],
                sems.at[len(waits)],
            )
            copy.start()
            waits.append(copy)

    def bring_either(here, there, source):
        at = start_of(xh, z, source)
        for k in range(2):
            target = b_held.at[pl.ds(pl.multiple_of(at + k * rows, rows), rows)]
            for side, ref in enumerate((here, there)):
                copy = pltpu.make_async_copy(
                    ref.at[pl.ds(k * rows, rows)], target, sems.at[len(waits)]
                )
                pl.when(core == side)(copy.start)
            waits.append(copy)

    for k, (first, second) in enumerate(b_sources):
        here, there = b_refs[2 * k], b_refs[2 * k + 1]
        if second is None:
            bring_either(here, there, first)
        else:
            one = [jnp.where(core == 0, a, b) for a, b in zip(first, second)]
            two = [jnp.where(core == 0, b, a) for a, b in zip(first, second)]
            bring(here, core, one)
            bring(there, 1 - core, two)
    for copy in waits:
        copy.wait()
    total = None
    for ref, source in zip(a_refs, a_sources):
        at = pl.multiple_of(start_of(xl, y, source), 2 * rows)
        part = jnp.dot(ref[...], b_held[pl.ds(at, 2 * rows)], preferred_element_type=F32)
        total = part if total is None else total + part
    finish(row, blk, total, extras, outs)


def product(finish, a, b, extras=(), n_out=1):
    rows, cols = a[0][0].shape
    out = jax.ShapeDtypeStruct((rows, cols), BF)
    a_sources = [source for _, source in a]
    b_sources = [one[2:] for one in b]
    b_arrays = [array for one in b for array in one[:2]]
    got = pl.pallas_call(
        functools.partial(
            product_body, finish, len(extras), n_out, a_sources, b_sources
        ),
        out_shape=[out] * n_out,
        in_specs=[VMEM] * (len(extras) + len(a) + len(b_arrays)),
        out_specs=[VMEM] * n_out,
        scratch_shapes=[
            pltpu.VMEM((16 * rows, cols), BF),
            pltpu.SemaphoreType.DMA((16,)),
        ],
        compiler_params=pltpu.CompilerParams(vmem_limit_bytes=VMEM_LIMIT),
    )(*extras, *[one[0] for one in a], *b_arrays)
    return got if n_out > 1 else got[0]


def end_first(row, blk, total, extras, outs):
    outs[0][...] = total.astype(BF)


def end_refined(row, blk, total, extras, outs):
    mask, own = extras
    value = mask[...].astype(F32) * (2.0 * own[...].astype(F32) - total)
    outs[0][...] = value.astype(BF)


def end_error(row, blk, total, extras, outs):
    outs[0][...] = (identity(row, blk, total.shape) - total).astype(BF)
    outs[1][...] = extras[0][...]


def end_shifted(row, blk, total, extras, outs):
    mask, mu = extras
    shift = mu[0:1, 0:1] * identity(row, blk, total.shape)
    outs[0][...] = (mask[...].astype(F32) * total - shift).astype(BF)


def end_square(row, blk, total, extras, outs):
    outs[0][...] = (extras[0][...].astype(F32) * total).astype(BF)


def end_sign(row, blk, total, extras, outs):
    outs[0][...] = (0.5 * (3.0 * extras[0][...].astype(F32) - total)).astype(BF)


def body(s, z, h, mu, ps, pz, ph, fi, fs):
    seff, zeff = prepare(ps, pz, s, z)
    heff, keep_inverse, keep_sign, mu = prepare_late(ph, fi, fs, mu, h)
    z_rows = gather_rows(zeff, True)
    s_cols = gather_cols(seff)
    first = product(end_first, z_rows, s_cols)
    f_rows = gather_rows(first, False)
    z_cols = gather_cols(zeff)
    refined = product(end_refined, f_rows, z_cols, (keep_inverse, zeff))
    r_rows = gather_rows(refined, False)
    h_cols = gather_cols(heff)
    shifted = product(end_shifted, r_rows, h_cols, (keep_sign, mu))
    x_rows = gather_rows(shifted, True)
    x_cols = gather_cols(shifted)
    error, refined = product(end_error, r_rows, s_cols, (refined,), 2)
    square = product(end_square, x_rows, x_cols, (keep_sign,))
    q_cols = gather_cols(square)
    sign = product(end_sign, x_rows, q_cols, (shifted,))
    return refined, error, sign


def solution(mesh):
    placed = (P("row", "blk"), P("row", "blk"), P("row", "blk"), P(), P(), P(), P(), P(), P())
    return jax.shard_map(
        body,
        mesh=mesh,
        in_specs=placed,
        out_specs=(P("row", "blk"), P("row", "blk"), P("row", "blk")),
        check_vma=False,
    )
```

time: 480 us -> 210 us (0.44)
  waiting for transfers between devices: 427 us -> 71.4 us
  starting transfers between devices: 0.36 us -> 119 us
  matrix products: 37.4 us -> 0 us
  Pallas kernels: 0 us -> 16.9 us
  between operations: 14.7 us -> 1.85 us
    all_gather x9 -> x0, waiting for transfers between devices: 426 us -> none  [the longest x1 63.2 us: body(): s_cols = lax.all_gather(seff, 'row', axis=0, tiled=True)]
    ppermute x0 -> x73, starting transfers between devices: none -> 119 us  [send(): return lax.ppermute(array, AXES, pairs)]
    ppermute x0 -> x73, waiting for transfers between devices: none -> 71.4 us  [send(): return lax.ppermute(array, AXES, pairs)]
    dot_general x16 -> x0, matrix products: 37.4 us -> none  [the longest x4 18.4 us: make_folder(): return jnp.dot(panel, piece, preferred_element_type=jnp.float32)]
    pallas_call x0 -> x8, Pallas kernels: none -> 16.9 us  [the longest x6 12.3 us: product(): pl.pallas_call(functools.partial(product_body, finish, len(extras), n_out...]
  transfers between devices with their start and end apart: 9 -> 73, of which waited for: 9 -> 21; matrix products, arithmetic and copies ran while one was open for 4% -> 0% of each run, Pallas kernels for 0% -> 4%
where the time goes in v1:
time: 210 us; the launch traced here: 209 us
  starting transfers between devices  119 us (57%)
  waiting for transfers between devices  71.4 us (34%)
  Pallas kernels  16.9 us (8%)
    ppermute x73, starting transfers between devices, send(): return lax.ppermute(array, AXES, pairs)  119 us
    ppermute x73, waiting for transfers between devices, send(): return lax.ppermute(array, AXES, pairs)  71.4 us
    pallas_call x6, Pallas kernels, product(): pl.pallas_call(functools.partial(product_body, finish, len(extras), n_out...  12.3 us
  transfers between devices with their start and end apart: 73, of which 21 were waited for; matrix products, arithmetic and copies ran while one was open for 0% of the time, Pallas kernels for 4%

profile of v1, /device:TPU:1, one launch (start us, length us, event | category | flops | bytes accessed | tf_op | source)
XLA Modules:
  0.0 209.1 jit_solution(5957988798895284771)
XLA Ops:
  12.6 2.6 %collective-permute-start.4 = (bf16[256,512]{1,0:T(8,128)(2,1)S(1)}, bf16[256,512]{1,0:T(8,128)(2,1)S(1)}, u32[]{:S(2)}, u32[]{:S(2)}) collective-permute-start(bf16[256,512]{1,0:T(8,128)(2,1)S(1)} %collective-permute-done.refs_1_), channel_id=1, source_target_pairs={{0,48},{1,49},{2,50},{3,51},{4,52},{5,53},{6,54},{7,55},{16,0},{17... | collective-permute-start | bytes 786440 | tf_op jit(solution)/shard_map/ppermute | solution.py:58
  15.4 3.8 %collective-permute-start.26 = (bf16[512,512]{1,0:T(8,128)(2,1)S(1)}, bf16[512,512]{1,0:T(8,128)(2,1)S(1)}, u32[]{:S(2)}, u32[]{:S(2)}) collective-permute-start(bf16[512,512]{1,0:T(8,128)(2,1)S(1)} %constant_dynamic-update-slice_fusion.2), channel_id=1, source_target_pairs={{0,2},{1,7},{2,4},{3,1},{4,6},{5,3},{6,0},{7,5},{16,18},{17,23},{1... | collective-permute-start | bytes 1572872 | tf_op jit(solution)/shard_map/ppermute | solution.py:58
  23.3 5.4 %collective-permute-done.5.refs_6_ = bf16[256,512]{1,0:T(8,128)(2,1)S(1)} collective-permute-done((bf16[256,512]{1,0:T(8,128)(2,1)S(1)}, bf16[256,512]{1,0:T(8,128)(2,1)S(1)}, u32[]{:S(2)}, u32[]{:S(2)}) %collective-permute-start.5) | collective-permute-done | bytes 262176 | tf_op jit(solution)/shard_map/ppermute | solution.py:58
  28.7 3.8 %collective-permute-start.10 = (bf16[512,512]{1,0:T(8,128)(2,1)S(1)}, bf16[512,512]{1,0:T(8,128)(2,1)S(1)}, u32[]{:S(2)}, u32[]{:S(2)}) collective-permute-start(bf16[512,512]{1,0:T(8,128)(2,1)S(1)} %constant_dynamic-update-slice_fusion), channel_id=1, source_target_pairs={{0,2},{1,7},{2,4},{3,1},{4,6},{5,3},{6,0},{7,5},{16,18},{17,23},{1... | collective-permute-start | bytes 1572872 | tf_op jit(solution)/shard_map/ppermute | solution.py:58
  32.9 2.8 %collective-permute-start.40 = (bf16[512,512]{1,0:T(8,128)(2,1)S(1)}, bf16[512,512]{1,0:T(8,128)(2,1)S(1)}, u32[]{:S(2)}, u32[]{:S(2)}) collective-permute-start(bf16[512,512]{1,0:T(8,128)(2,1)S(1)} %constant_dynamic-update-slice_fusion.4), channel_id=1, source_target_pairs={{0,8},{1,5},{2,10},{3,7},{4,12},{5,1},{6,14},{7,3},{16,24},{17,21}... | collective-permute-start | bytes 1572872 | tf_op jit(solution)/shard_map/ppermute | solution.py:58
  35.7 2.6 %collective-permute-start.27 = (bf16[512,512]{1,0:T(8,128)(2,1)S(1)}, bf16[512,512]{1,0:T(8,128)(2,1)S(1)}, u32[]{:S(2)}, u32[]{:S(2)}) collective-permute-start(bf16[512,512]{1,0:T(8,128)(2,1)S(1)} %collective-permute-done.26.refs_14_), channel_id=1, source_target_pairs={{0,1},{1,0},{2,3},{3,2},{4,5},{5,4},{6,7},{7,6},{16,17},{17,16},{1... | collective-permute-start | bytes 1572872 | tf_op jit(solution)/shard_map/ppermute | solution.py:58
  38.3 5.9 %collective-permute-done.10.refs_12_.refs_13_ = bf16[512,512]{1,0:T(8,128)(2,1)S(1)} collective-permute-done((bf16[512,512]{1,0:T(8,128)(2,1)S(1)}, bf16[512,512]{1,0:T(8,128)(2,1)S(1)}, u32[]{:S(2)}, u32[]{:S(2)}) %collective-permute-start.10) | collective-permute-done | bytes 524320 | tf_op jit(solution)/shard_map/ppermute | solution.py:58
  47.9 9.6 %collective-permute-done.42.refs_14_ = bf16[512,512]{1,0:T(8,128)(2,1)S(1)} collective-permute-done((bf16[512,512]{1,0:T(8,128)(2,1)S(1)}, bf16[512,512]{1,0:T(8,128)(2,1)S(1)}, u32[]{:S(2)}, u32[]{:S(2)}) %collective-permute-start.42) | collective-permute-done | bytes 524320 | tf_op jit(solution)/shard_map/ppermute | solution.py:58
  57.5 2.7 %collective-permute-start.12 = (bf16[512,512]{1,0:T(8,128)(2,1)S(1)}, bf16[512,512]{1,0:T(8,128)(2,1)S(1)}, u32[]{:S(2)}, u32[]{:S(2)}) collective-permute-start(bf16[512,512]{1,0:T(8,128)(2,1)S(1)} %collective-permute-done.8.refs_10_.refs_11_), channel_id=1, source_target_pairs={{0,2},{1,9},{2,4},{3,11},{4,6},{5,13},{6,0},{7,15},{16,18},{17,25}... | collective-permute-start | bytes 1572872 | tf_op jit(solution)/shard_map/ppermute | solution.py:58
  61.5 5.6 %collective-permute-start.15 = (bf16[512,512]{1,0:T(8,128)(2,1)S(1)}, bf16[512,512]{1,0:T(8,128)(2,1)S(1)}, u32[]{:S(2)}, u32[]{:S(2)}) collective-permute-start(bf16[512,512]{1,0:T(8,128)(2,1)S(1)} %collective-permute-done.14.refs_16_.refs_17_), channel_id=1, source_target_pairs={{0,1},{1,0},{2,3},{3,2},{4,5},{5,4},{6,7},{7,6},{16,17},{17,16},{1... | collective-permute-start | bytes 1572872 | tf_op jit(solution)/shard_map/ppermute | solution.py:58
  69.3 3.4 %collective-permute-done.28.refs_16_ = bf16[512,512]{1,0:T(8,128)(2,1)S(1)} collective-permute-done((bf16[512,512]{1,0:T(8,128)(2,1)S(1)}, bf16[512,512]{1,0:T(8,128)(2,1)S(1)}, u32[]{:S(2)}, u32[]{:S(2)}) %collective-permute-start.28) | collective-permute-done | bytes 524320 | tf_op jit(solution)/shard_map/ppermute | solution.py:58
  75.6 2.8 %collective-permute-start.44 = (bf16[512,512]{1,0:T(8,128)(2,1)S(1)}, bf16[512,512]{1,0:T(8,128)(2,1)S(1)}, u32[]{:S(2)}, u32[]{:S(2)}) collective-permute-start(bf16[512,512]{1,0:T(8,128)(2,1)S(1)} %collective-permute-done.40.refs_12_), channel_id=1, source_target_pairs={{0,2},{1,9},{2,4},{3,11},{4,6},{5,13},{6,0},{7,15},{16,18},{17,25}... | collective-permute-start | bytes 1572872 | tf_op jit(solution)/shard_map/ppermute | solution.py:58
  86.7 3.2 %collective-permute-done.21.refs_8_ = bf16[256,512]{1,0:T(8,128)(2,1)S(1)} collective-permute-done((bf16[256,512]{1,0:T(8,128)(2,1)S(1)}, bf16[256,512]{1,0:T(8,128)(2,1)S(1)}, u32[]{:S(2)}, u32[]{:S(2)}) %collective-permute-start.21) | collective-permute-done | bytes 262176 | tf_op jit(solution)/shard_map/ppermute | solution.py:58
  95.9 2.7 %collective-permute-start.47 = (bf16[512,512]{1,0:T(8,128)(2,1)S(1)}, bf16[512,512]{1,0:T(8,128)(2,1)S(1)}, u32[]{:S(2)}, u32[]{:S(2)}) collective-permute-start(bf16[512,512]{1,0:T(8,128)(2,1)S(1)} %collective-permute-done.46.refs_18_), channel_id=1, source_target_pairs={{0,1},{1,0},{2,3},{3,2},{4,5},{5,4},{6,7},{7,6},{16,17},{17,16},{1... | collective-permute-start | bytes 1572872 | tf_op jit(solution)/shard_map/ppermute | solution.py:58
  98.6 2.7 %collective-permute-done.20.refs_7_ = bf16[256,512]{1,0:T(8,128)(2,1)S(1)} collective-permute-done((bf16[256,512]{1,0:T(8,128)(2,1)S(1)}, bf16[256,512]{1,0:T(8,128)(2,1)S(1)}, u32[]{:S(2)}, u32[]{:S(2)}) %collective-permute-start.20) | collective-permute-done | bytes 262176 | tf_op jit(solution)/shard_map/ppermute | solution.py:58
  108.9 2.8 %collective-permute-done.37.refs_7_.refs_8_ = bf16[256,512]{1,0:T(8,128)(2,1)S(1)} collective-permute-done((bf16[256,512]{1,0:T(8,128)(2,1)S(1)}, bf16[256,512]{1,0:T(8,128)(2,1)S(1)}, u32[]{:S(2)}, u32[]{:S(2)}) %collective-permute-start.37) | collective-permute-done | bytes 262176 | tf_op jit(solution)/shard_map/ppermute | solution.py:58
  119.3 2.7 %collective-permute-done.36.refs_6_.refs_7_ = bf16[256,512]{1,0:T(8,128)(2,1)S(1)} collective-permute-done((bf16[256,512]{1,0:T(8,128)(2,1)S(1)}, bf16[256,512]{1,0:T(8,128)(2,1)S(1)}, u32[]{:S(2)}, u32[]{:S(2)}) %collective-permute-start.36) | collective-permute-done | bytes 262176 | tf_op jit(solution)/shard_map/ppermute | solution.py:58
  125.2 4.4 %collective-permute-start.55 = (bf16[256,512]{1,0:T(8,128)(2,1)S(1)}, bf16[256,512]{1,0:T(8,128)(2,1)S(1)}, u32[]{:S(2)}, u32[]{:S(2)}) collective-permute-start(bf16[256,512]{1,0:T(8,128)(2,1)S(1)} %shard_map.115.refs_1_.refs_9_.refs_0_), channel_id=1, source_target_pairs={{0,1},{1,0},{2,3},{3,2},{4,5},{5,4},{6,7},{7,6},{16,17},{17,16},{1... | collective-permute-start | bytes 786440 | tf_op jit(solution)/shard_map/ppermute | solution.py:58
  135.7 5.1 %collective-permute-done.56.refs_11_ = bf16[512,512]{1,0:T(8,128)(2,1)S(1)} collective-permute-done((bf16[512,512]{1,0:T(8,128)(2,1)S(1)}, bf16[512,512]{1,0:T(8,128)(2,1)S(1)}, u32[]{:S(2)}, u32[]{:S(2)}) %collective-permute-start.56) | collective-permute-done | bytes 524320 | tf_op jit(solution)/shard_map/ppermute | solution.py:58
  143.8 2.6 %collective-permute-start.52 = (bf16[256,512]{1,0:T(8,128)(2,1)S(1)}, bf16[256,512]{1,0:T(8,128)(2,1)S(1)}, u32[]{:S(2)}, u32[]{:S(2)}) collective-permute-start(bf16[256,512]{1,0:T(8,128)(2,1)S(1)} %collective-permute-done.48.refs_2_), channel_id=1, source_target_pairs={{0,48},{1,49},{2,50},{3,51},{4,52},{5,53},{6,54},{7,55},{16,0},{17... | collective-permute-start | bytes 786440 | tf_op jit(solution)/shard_map/ppermute | solution.py:58
  146.4 3.8 %collective-permute-done.53.refs_7_ = bf16[256,512]{1,0:T(8,128)(2,1)S(1)} collective-permute-done((bf16[256,512]{1,0:T(8,128)(2,1)S(1)}, bf16[256,512]{1,0:T(8,128)(2,1)S(1)}, u32[]{:S(2)}, u32[]{:S(2)}) %collective-permute-start.53) | collective-permute-done | bytes 262176 | tf_op jit(solution)/shard_map/ppermute | solution.py:58
  150.2 9.9 %collective-permute-start.57 = (bf16[512,512]{1,0:T(8,128)(2,1)S(1)}, bf16[512,512]{1,0:T(8,128)(2,1)S(1)}, u32[]{:S(2)}, u32[]{:S(2)}) collective-permute-start(bf16[512,512]{1,0:T(8,128)(2,1)S(1)} %collective-permute-done.56.refs_11_), channel_id=1, source_target_pairs={{0,1},{1,0},{2,3},{3,2},{4,5},{5,4},{6,7},{7,6},{16,17},{17,16},{1... | collective-permute-start | bytes 1572872 | tf_op jit(solution)/shard_map/ppermute | solution.py:58
  160.8 3.2 %collective-permute-start.54 = (bf16[256,512]{1,0:T(8,128)(2,1)S(1)}, bf16[256,512]{1,0:T(8,128)(2,1)S(1)}, u32[]{:S(2)}, u32[]{:S(2)}) collective-permute-start(bf16[256,512]{1,0:T(8,128)(2,1)S(1)} %collective-permute-done.52.refs_6_), channel_id=1, source_target_pairs={{0,48},{1,49},{2,50},{3,51},{4,52},{5,53},{6,54},{7,55},{16,0},{17... | collective-permute-start | bytes 786440 | tf_op jit(solution)/shard_map/ppermute | solution.py:58
  163.9 3.3 %collective-permute-done.54.refs_8_ = bf16[256,512]{1,0:T(8,128)(2,1)S(1)} collective-permute-done((bf16[256,512]{1,0:T(8,128)(2,1)S(1)}, bf16[256,512]{1,0:T(8,128)(2,1)S(1)}, u32[]{:S(2)}, u32[]{:S(2)}) %collective-permute-start.54) | collective-permute-done | bytes 262176 | tf_op jit(solution)/shard_map/ppermute | solution.py:58
  169.1 6.9 %collective-permute-start.64 = (bf16[256,512]{1,0:T(8,128)(2,1)S(1)}, bf16[256,512]{1,0:T(8,128)(2,1)S(1)}, u32[]{:S(2)}, u32[]{:S(2)}) collective-permute-start(bf16[256,512]{1,0:T(8,128)(2,1)S(1)} %shard_map.116.refs_9_), channel_id=1, source_target_pairs={{0,1},{1,0},{2,3},{3,2},{4,5},{5,4},{6,7},{7,6},{16,17},{17,16},{1... | collective-permute-start | bytes 786440 | tf_op jit(solution)/shard_map/ppermute | solution.py:58
  177.3 2.9 %collective-permute-start.67 = (bf16[512,512]{1,0:T(8,128)(2,1)S(1)}, bf16[512,512]{1,0:T(8,128)(2,1)S(1)}, u32[]{:S(2)}, u32[]{:S(2)}) collective-permute-start(bf16[512,512]{1,0:T(8,128)(2,1)S(1)} %pad_maximum_fusion.1), channel_id=1, source_target_pairs={{0,2},{1,7},{2,4},{3,1},{4,6},{5,3},{6,0},{7,5},{16,18},{17,23},{1... | collective-permute-start | bytes 1572872 | tf_op jit(solution)/shard_map/ppermute | solution.py:58
  180.2 9.4 %collective-permute-done.65.refs_11_ = bf16[512,512]{1,0:T(8,128)(2,1)S(1)} collective-permute-done((bf16[512,512]{1,0:T(8,128)(2,1)S(1)}, bf16[512,512]{1,0:T(8,128)(2,1)S(1)}, u32[]{:S(2)}, u32[]{:S(2)}) %collective-permute-start.65) | collective-permute-done | bytes 524320 | tf_op jit(solution)/shard_map/ppermute | solution.py:58
  190.4 3.2 %collective-permute-start.66 = (bf16[512,512]{1,0:T(8,128)(2,1)S(1)}, bf16[512,512]{1,0:T(8,128)(2,1)S(1)}, u32[]{:S(2)}, u32[]{:S(2)}) collective-permute-start(bf16[512,512]{1,0:T(8,128)(2,1)S(1)} %collective-permute-done.65.refs_11_), channel_id=1, source_target_pairs={{0,1},{1,0},{2,3},{3,2},{4,5},{5,4},{6,7},{7,6},{16,17},{17,16},{1... | collective-permute-start | bytes 1572872 | tf_op jit(solution)/shard_map/ppermute | solution.py:58
  193.6 6.4 %collective-permute-start.72 = (bf16[512,512]{1,0:T(8,128)(2,1)S(1)}, bf16[512,512]{1,0:T(8,128)(2,1)S(1)}, u32[]{:S(2)}, u32[]{:S(2)}) collective-permute-start(bf16[512,512]{1,0:T(8,128)(2,1)S(1)} %collective-permute-done.71.refs_17_), channel_id=1, source_target_pairs={{0,1},{1,0},{2,3},{3,2},{4,5},{5,4},{6,7},{7,6},{16,17},{17,16},{1... | collective-permute-start | bytes 1572872 | tf_op jit(solution)/shard_map/ppermute | solution.py:58
  200.0 3.8 %collective-permute-start.70 = (bf16[512,512]{1,0:T(8,128)(2,1)S(1)}, bf16[512,512]{1,0:T(8,128)(2,1)S(1)}, u32[]{:S(2)}, u32[]{:S(2)}) collective-permute-start(bf16[512,512]{1,0:T(8,128)(2,1)S(1)} %collective-permute-done.69.refs_15_), channel_id=1, source_target_pairs={{0,1},{1,0},{2,3},{3,2},{4,5},{5,4},{6,7},{7,6},{16,17},{17,16},{1... | collective-permute-start | bytes 1572872 | tf_op jit(solution)/shard_map/ppermute | solution.py:58
  203.8 2.5 %shard_map.114 = (bf16[256,512]{1,0:T(8,128)(2,1)}, bf16[256,512]{1,0:T(8,128)(2,1)}) custom-call(bf16[256,512]{1,0:T(8,128)(2,1)S(1)} %shard_map.113.refs_0_.refs_1_.refs_2_, bf16[256,512]{1,0:T(8,128)(2,1)S(1)} %shard_map.113.refs_0_.refs_1_.refs_2_, bf16[256,512]{1,0:T(8,128)(2,1)S(1)} %collective-permute-done.32.refs_2_.refs_3_, ...), custom_call_target="tpu_custom_call" | custom-call | tf_op jit(solution)/shard_map/pallas_call | solution.py:255
  206.4 2.5 %shard_map.117 = bf16[256,512]{1,0:T(8,128)(2,1)} custom-call(bf16[256,512]{1,0:T(8,128)(2,1)S(1)} %shard_map.115.refs_1_.refs_9_.refs_0_, bf16[256,512]{1,0:T(8,128)(2,1)S(1)} %shard_map.115.refs_1_.refs_9_.refs_0_, bf16[256,512]{1,0:T(8,128)(2,1)S(1)} %collective-permute-done.48.refs_2_, bf16[256,512]{1,0:T(8,128)(2,1)S(1)} %collective-permute-done.49.refs_3_, ...), custom_call_target="tpu_custom_call" | custom-call | tf_op jit(solution)/shard_map/pallas_call | solution.py:255
  (142 shorter events, 72.0 us)
Async XLA Ops:
  15.2 17.3 %collective-permute-start.3 = (bf16[256,512]{1,0:T(8,128)(2,1)S(1)}, bf16[256,512]{1,0:T(8,128)(2,1)S(1)}, u32[]{:S(2)}, u32[]{:S(2)}) collective-permute-start(bf16[256,512]{1,0:T(8,128)(2,1)S(1)} %collective-permute-done.refs_1_), channel_id=1, source_target_pairs={{0,16},{1,17},{2,18},{3,19},{4,20},{5,21},{6,22},{7,23},{16,32},{1... | collective-permute-start | bytes 786440 | tf_op jit(solution)/shard_map/ppermute | solution.py:58
  15.3 13.4 %collective-permute-start.5 = (bf16[256,512]{1,0:T(8,128)(2,1)S(1)}, bf16[256,512]{1,0:T(8,128)(2,1)S(1)}, u32[]{:S(2)}, u32[]{:S(2)}) collective-permute-start(bf16[256,512]{1,0:T(8,128)(2,1)S(1)} %collective-permute-done.1.refs_2_), channel_id=1, source_target_pairs={{0,16},{1,17},{2,18},{3,19},{4,20},{5,21},{6,22},{7,23},{16,32},{1... | collective-permute-start | bytes 786440 | tf_op jit(solution)/shard_map/ppermute | solution.py:58
  15.4 17.5 %collective-permute-start.26 = (bf16[512,512]{1,0:T(8,128)(2,1)S(1)}, bf16[512,512]{1,0:T(8,128)(2,1)S(1)}, u32[]{:S(2)}, u32[]{:S(2)}) collective-permute-start(bf16[512,512]{1,0:T(8,128)(2,1)S(1)} %constant_dynamic-update-slice_fusion.2), channel_id=1, source_target_pairs={{0,2},{1,7},{2,4},{3,1},{4,6},{5,3},{6,0},{7,5},{16,18},{17,23},{1... | collective-permute-start | bytes 1572872 | tf_op jit(solution)/shard_map/ppermute | solution.py:58
  19.2 16.4 %collective-permute-start.24 = (bf16[512,512]{1,0:T(8,128)(2,1)S(1)}, bf16[512,512]{1,0:T(8,128)(2,1)S(1)}, u32[]{:S(2)}, u32[]{:S(2)}) collective-permute-start(bf16[512,512]{1,0:T(8,128)(2,1)S(1)} %constant_dynamic-update-slice_fusion.2), channel_id=1, source_target_pairs={{0,8},{1,5},{2,10},{3,7},{4,12},{5,1},{6,14},{7,3},{16,24},{17,21}... | collective-permute-start | bytes 1572872 | tf_op jit(solution)/shard_map/ppermute | solution.py:58
  20.9 11.7 %collective-permute-start.6 = (bf16[256,512]{1,0:T(8,128)(2,1)S(1)}, bf16[256,512]{1,0:T(8,128)(2,1)S(1)}, u32[]{:S(2)}, u32[]{:S(2)}) collective-permute-start(bf16[256,512]{1,0:T(8,128)(2,1)S(1)} %collective-permute-done.4.refs_5_), channel_id=1, source_target_pairs={{0,48},{1,49},{2,50},{3,51},{4,52},{5,53},{6,54},{7,55},{16,0},{17... | collective-permute-start | bytes 786440 | tf_op jit(solution)/shard_map/ppermute | solution.py:58
  28.7 15.5 %collective-permute-start.10 = (bf16[512,512]{1,0:T(8,128)(2,1)S(1)}, bf16[512,512]{1,0:T(8,128)(2,1)S(1)}, u32[]{:S(2)}, u32[]{:S(2)}) collective-permute-start(bf16[512,512]{1,0:T(8,128)(2,1)S(1)} %constant_dynamic-update-slice_fusion), channel_id=1, source_target_pairs={{0,2},{1,7},{2,4},{3,1},{4,6},{5,3},{6,0},{7,5},{16,18},{17,23},{1... | collective-permute-start | bytes 1572872 | tf_op jit(solution)/shard_map/ppermute | solution.py:58
  32.5 14.7 %collective-permute-start.8 = (bf16[512,512]{1,0:T(8,128)(2,1)S(1)}, bf16[512,512]{1,0:T(8,128)(2,1)S(1)}, u32[]{:S(2)}, u32[]{:S(2)}) collective-permute-start(bf16[512,512]{1,0:T(8,128)(2,1)S(1)} %constant_dynamic-update-slice_fusion), channel_id=1, source_target_pairs={{0,8},{1,5},{2,10},{3,7},{4,12},{5,1},{6,14},{7,3},{16,24},{17,21}... | collective-permute-start | bytes 1572872 | tf_op jit(solution)/shard_map/ppermute | solution.py:58
  32.5 25.0 %collective-permute-start.42 = (bf16[512,512]{1,0:T(8,128)(2,1)S(1)}, bf16[512,512]{1,0:T(8,128)(2,1)S(1)}, u32[]{:S(2)}, u32[]{:S(2)}) collective-permute-start(bf16[512,512]{1,0:T(8,128)(2,1)S(1)} %constant_dynamic-update-slice_fusion.4), channel_id=1, source_target_pairs={{0,2},{1,7},{2,4},{3,1},{4,6},{5,3},{6,0},{7,5},{16,18},{17,23},{1... | collective-permute-start | bytes 1572872 | tf_op jit(solution)/shard_map/ppermute | solution.py:58
  32.9 27.4 %collective-permute-start.40 = (bf16[512,512]{1,0:T(8,128)(2,1)S(1)}, bf16[512,512]{1,0:T(8,128)(2,1)S(1)}, u32[]{:S(2)}, u32[]{:S(2)}) collective-permute-start(bf16[512,512]{1,0:T(8,128)(2,1)S(1)} %constant_dynamic-update-slice_fusion.4), channel_id=1, source_target_pairs={{0,8},{1,5},{2,10},{3,7},{4,12},{5,1},{6,14},{7,3},{16,24},{17,21}... | collective-permute-start | bytes 1572872 | tf_op jit(solution)/shard_map/ppermute | solution.py:58
  35.7 25.2 %collective-permute-start.27 = (bf16[512,512]{1,0:T(8,128)(2,1)S(1)}, bf16[512,512]{1,0:T(8,128)(2,1)S(1)}, u32[]{:S(2)}, u32[]{:S(2)}) collective-permute-start(bf16[512,512]{1,0:T(8,128)(2,1)S(1)} %collective-permute-done.26.refs_14_), channel_id=1, source_target_pairs={{0,1},{1,0},{2,3},{3,2},{4,5},{5,4},{6,7},{7,6},{16,17},{17,16},{1... | collective-permute-start | bytes 1572872 | tf_op jit(solution)/shard_map/ppermute | solution.py:58
  44.2 16.6 %collective-permute-start.30 = (bf16[512,512]{1,0:T(8,128)(2,1)S(1)}, bf16[512,512]{1,0:T(8,128)(2,1)S(1)}, u32[]{:S(2)}, u32[]{:S(2)}) collective-permute-start(bf16[512,512]{1,0:T(8,128)(2,1)S(1)} %collective-permute-done.24.refs_12_), channel_id=1, source_target_pairs={{0,6},{1,1},{2,0},{3,3},{4,2},{5,5},{6,4},{7,7},{16,22},{17,17},{1... | collective-permute-start | bytes 1572872 | tf_op jit(solution)/shard_map/ppermute | solution.py:58
  47.2 14.3 %collective-permute-start.14 = (bf16[512,512]{1,0:T(8,128)(2,1)S(1)}, bf16[512,512]{1,0:T(8,128)(2,1)S(1)}, u32[]{:S(2)}, u32[]{:S(2)}) collective-permute-start(bf16[512,512]{1,0:T(8,128)(2,1)S(1)} %collective-permute-done.8.refs_10_.refs_11_), channel_id=1, source_target_pairs={{0,6},{1,1},{2,0},{3,3},{4,2},{5,5},{6,4},{7,7},{16,22},{17,17},{1... | collective-permute-start | bytes 1572872 | tf_op jit(solution)/shard_map/ppermute | solution.py:58
  60.3 12.4 %collective-permute-start.28 = (bf16[512,512]{1,0:T(8,128)(2,1)S(1)}, bf16[512,512]{1,0:T(8,128)(2,1)S(1)}, u32[]{:S(2)}, u32[]{:S(2)}) collective-permute-start(bf16[512,512]{1,0:T(8,128)(2,1)S(1)} %collective-permute-done.24.refs_12_), channel_id=1, source_target_pairs={{0,2},{1,9},{2,4},{3,11},{4,6},{5,13},{6,0},{7,15},{16,18},{17,25}... | collective-permute-start | bytes 1572872 | tf_op jit(solution)/shard_map/ppermute | solution.py:58
  60.9 14.0 %collective-permute-start.11 = (bf16[512,512]{1,0:T(8,128)(2,1)S(1)}, bf16[512,512]{1,0:T(8,128)(2,1)S(1)}, u32[]{:S(2)}, u32[]{:S(2)}) collective-permute-start(bf16[512,512]{1,0:T(8,128)(2,1)S(1)} %collective-permute-done.10.refs_12_.refs_13_), channel_id=1, source_target_pairs={{0,1},{1,0},{2,3},{3,2},{4,5},{5,4},{6,7},{7,6},{16,17},{17,16},{1... | collective-permute-start | bytes 1572872 | tf_op jit(solution)/shard_map/ppermute | solution.py:58
  60.9 14.7 %collective-permute-start.9 = (bf16[512,512]{1,0:T(8,128)(2,1)S(1)}, bf16[512,512]{1,0:T(8,128)(2,1)S(1)}, u32[]{:S(2)}, u32[]{:S(2)}) collective-permute-start(bf16[512,512]{1,0:T(8,128)(2,1)S(1)} %collective-permute-done.8.refs_10_.refs_11_), channel_id=1, source_target_pairs={{0,1},{1,0},{2,3},{3,2},{4,5},{5,4},{6,7},{7,6},{16,17},{17,16},{1... | collective-permute-start | bytes 1572872 | tf_op jit(solution)/shard_map/ppermute | solution.py:58
  61.5 16.9 %collective-permute-start.15 = (bf16[512,512]{1,0:T(8,128)(2,1)S(1)}, bf16[512,512]{1,0:T(8,128)(2,1)S(1)}, u32[]{:S(2)}, u32[]{:S(2)}) collective-permute-start(bf16[512,512]{1,0:T(8,128)(2,1)S(1)} %collective-permute-done.14.refs_16_.refs_17_), channel_id=1, source_target_pairs={{0,1},{1,0},{2,3},{3,2},{4,5},{5,4},{6,7},{7,6},{16,17},{17,16},{1... | collective-permute-start | bytes 1572872 | tf_op jit(solution)/shard_map/ppermute | solution.py:58
  67.1 11.9 %collective-permute-start.13 = (bf16[512,512]{1,0:T(8,128)(2,1)S(1)}, bf16[512,512]{1,0:T(8,128)(2,1)S(1)}, u32[]{:S(2)}, u32[]{:S(2)}) collective-permute-start(bf16[512,512]{1,0:T(8,128)(2,1)S(1)} %collective-permute-done.12.refs_14_.refs_15_), channel_id=1, source_target_pairs={{0,1},{1,0},{2,3},{3,2},{4,5},{5,4},{6,7},{7,6},{16,17},{17,16},{1... | collective-permute-start | bytes 1572872 | tf_op jit(solution)/shard_map/ppermute | solution.py:58
  79.0 12.1 %collective-permute-start.29 = (bf16[512,512]{1,0:T(8,128)(2,1)S(1)}, bf16[512,512]{1,0:T(8,128)(2,1)S(1)}, u32[]{:S(2)}, u32[]{:S(2)}) collective-permute-start(bf16[512,512]{1,0:T(8,128)(2,1)S(1)} %collective-permute-done.28.refs_16_), channel_id=1, source_target_pairs={{0,1},{1,0},{2,3},{3,2},{4,5},{5,4},{6,7},{7,6},{16,17},{17,16},{1... | collective-permute-start | bytes 1572872 | tf_op jit(solution)/shard_map/ppermute | solution.py:58
  91.1 14.5 %collective-permute-start.43 = (bf16[512,512]{1,0:T(8,128)(2,1)S(1)}, bf16[512,512]{1,0:T(8,128)(2,1)S(1)}, u32[]{:S(2)}, u32[]{:S(2)}) collective-permute-start(bf16[512,512]{1,0:T(8,128)(2,1)S(1)} %collective-permute-done.42.refs_14_), channel_id=1, source_target_pairs={{0,1},{1,0},{2,3},{3,2},{4,5},{5,4},{6,7},{7,6},{16,17},{17,16},{1... | collective-permute-start | bytes 1572872 | tf_op jit(solution)/shard_map/ppermute | solution.py:58
  94.2 12.7 %collective-permute-start.41 = (bf16[512,512]{1,0:T(8,128)(2,1)S(1)}, bf16[512,512]{1,0:T(8,128)(2,1)S(1)}, u32[]{:S(2)}, u32[]{:S(2)}) collective-permute-start(bf16[512,512]{1,0:T(8,128)(2,1)S(1)} %collective-permute-done.40.refs_12_), channel_id=1, source_target_pairs={{0,1},{1,0},{2,3},{3,2},{4,5},{5,4},{6,7},{7,6},{16,17},{17,16},{1... | collective-permute-start | bytes 1572872 | tf_op jit(solution)/shard_map/ppermute | solution.py:58
  95.9 13.0 %collective-permute-start.47 = (bf16[512,512]{1,0:T(8,128)(2,1)S(1)}, bf16[512,512]{1,0:T(8,128)(2,1)S(1)}, u32[]{:S(2)}, u32[]{:S(2)}) collective-permute-start(bf16[512,512]{1,0:T(8,128)(2,1)S(1)} %collective-permute-done.46.refs_18_), channel_id=1, source_target_pairs={{0,1},{1,0},{2,3},{3,2},{4,5},{5,4},{6,7},{7,6},{16,17},{17,16},{1... | collective-permute-start | bytes 1572872 | tf_op jit(solution)/shard_map/ppermute | solution.py:58
  101.3 14.1 %collective-permute-start.45 = (bf16[512,512]{1,0:T(8,128)(2,1)S(1)}, bf16[512,512]{1,0:T(8,128)(2,1)S(1)}, u32[]{:S(2)}, u32[]{:S(2)}) collective-permute-start(bf16[512,512]{1,0:T(8,128)(2,1)S(1)} %collective-permute-done.44.refs_16_), channel_id=1, source_target_pairs={{0,1},{1,0},{2,3},{3,2},{4,5},{5,4},{6,7},{7,6},{16,17},{17,16},{1... | collective-permute-start | bytes 1572872 | tf_op jit(solution)/shard_map/ppermute | solution.py:58
  132.4 11.4 %collective-permute-start.49 = (bf16[256,512]{1,0:T(8,128)(2,1)S(1)}, bf16[256,512]{1,0:T(8,128)(2,1)S(1)}, u32[]{:S(2)}, u32[]{:S(2)}) collective-permute-start(bf16[256,512]{1,0:T(8,128)(2,1)S(1)} %shard_map.115.refs_1_.refs_9_.refs_0_), channel_id=1, source_target_pairs={{0,16},{1,17},{2,18},{3,19},{4,20},{5,21},{6,22},{7,23},{16,32},{1... | collective-permute-start | bytes 786440 | tf_op jit(solution)/shard_map/ppermute | solution.py:58
  133.8 26.3 %collective-permute-start.58 = (bf16[512,512]{1,0:T(8,128)(2,1)S(1)}, bf16[512,512]{1,0:T(8,128)(2,1)S(1)}, u32[]{:S(2)}, u32[]{:S(2)}) collective-permute-start(bf16[512,512]{1,0:T(8,128)(2,1)S(1)} %pad_maximum_fusion), channel_id=1, source_target_pairs={{0,2},{1,7},{2,4},{3,1},{4,6},{5,3},{6,0},{7,5},{16,18},{17,23},{1... | collective-permute-start | bytes 1572872 | tf_op jit(solution)/shard_map/ppermute | solution.py:58
  140.7 19.5 %collective-permute-start.62 = (bf16[512,512]{1,0:T(8,128)(2,1)S(1)}, bf16[512,512]{1,0:T(8,128)(2,1)S(1)}, u32[]{:S(2)}, u32[]{:S(2)}) collective-permute-start(bf16[512,512]{1,0:T(8,128)(2,1)S(1)} %collective-permute-done.56.refs_11_), channel_id=1, source_target_pairs={{0,6},{1,1},{2,0},{3,3},{4,2},{5,5},{6,4},{7,7},{16,22},{17,17},{1... | collective-permute-start | bytes 1572872 | tf_op jit(solution)/shard_map/ppermute | solution.py:58
  141.4 19.2 %collective-permute-start.60 = (bf16[512,512]{1,0:T(8,128)(2,1)S(1)}, bf16[512,512]{1,0:T(8,128)(2,1)S(1)}, u32[]{:S(2)}, u32[]{:S(2)}) collective-permute-start(bf16[512,512]{1,0:T(8,128)(2,1)S(1)} %collective-permute-done.56.refs_11_), channel_id=1, source_target_pairs={{0,2},{1,9},{2,4},{3,11},{4,6},{5,13},{6,0},{7,15},{16,18},{17,25}... | collective-permute-start | bytes 1572872 | tf_op jit(solution)/shard_map/ppermute | solution.py:58
  150.2 17.0 %collective-permute-start.57 = (bf16[512,512]{1,0:T(8,128)(2,1)S(1)}, bf16[512,512]{1,0:T(8,128)(2,1)S(1)}, u32[]{:S(2)}, u32[]{:S(2)}) collective-permute-start(bf16[512,512]{1,0:T(8,128)(2,1)S(1)} %collective-permute-done.56.refs_11_), channel_id=1, source_target_pairs={{0,1},{1,0},{2,3},{3,2},{4,5},{5,4},{6,7},{7,6},{16,17},{17,16},{1... | collective-permute-start | bytes 1572872 | tf_op jit(solution)/shard_map/ppermute | solution.py:58
  177.2 12.3 %collective-permute-start.65 = (bf16[512,512]{1,0:T(8,128)(2,1)S(1)}, bf16[512,512]{1,0:T(8,128)(2,1)S(1)}, u32[]{:S(2)}, u32[]{:S(2)}) collective-permute-start(bf16[512,512]{1,0:T(8,128)(2,1)S(1)} %pad_maximum_fusion.1), channel_id=1, source_target_pairs={{0,8},{1,5},{2,10},{3,7},{4,12},{5,1},{6,14},{7,3},{16,24},{17,21}... | collective-permute-start | bytes 1572872 | tf_op jit(solution)/shard_map/ppermute | solution.py:58
  177.3 16.2 %collective-permute-start.67 = (bf16[512,512]{1,0:T(8,128)(2,1)S(1)}, bf16[512,512]{1,0:T(8,128)(2,1)S(1)}, u32[]{:S(2)}, u32[]{:S(2)}) collective-permute-start(bf16[512,512]{1,0:T(8,128)(2,1)S(1)} %pad_maximum_fusion.1), channel_id=1, source_target_pairs={{0,2},{1,7},{2,4},{3,1},{4,6},{5,3},{6,0},{7,5},{16,18},{17,23},{1... | collective-permute-start | bytes 1572872 | tf_op jit(solution)/shard_map/ppermute | solution.py:58
  190.4 16.0 %collective-permute-start.66 = (bf16[512,512]{1,0:T(8,128)(2,1)S(1)}, bf16[512,512]{1,0:T(8,128)(2,1)S(1)}, u32[]{:S(2)}, u32[]{:S(2)}) collective-permute-start(bf16[512,512]{1,0:T(8,128)(2,1)S(1)} %collective-permute-done.65.refs_11_), channel_id=1, source_target_pairs={{0,1},{1,0},{2,3},{3,2},{4,5},{5,4},{6,7},{7,6},{16,17},{17,16},{1... | collective-permute-start | bytes 1572872 | tf_op jit(solution)/shard_map/ppermute | solution.py:58
  193.5 12.8 %collective-permute-start.68 = (bf16[512,512]{1,0:T(8,128)(2,1)S(1)}, bf16[512,512]{1,0:T(8,128)(2,1)S(1)}, u32[]{:S(2)}, u32[]{:S(2)}) collective-permute-start(bf16[512,512]{1,0:T(8,128)(2,1)S(1)} %collective-permute-done.67.refs_13_), channel_id=1, source_target_pairs={{0,1},{1,0},{2,3},{3,2},{4,5},{5,4},{6,7},{7,6},{16,17},{17,16},{1... | collective-permute-start | bytes 1572872 | tf_op jit(solution)/shard_map/ppermute | solution.py:58
  193.6 12.7 %collective-permute-start.72 = (bf16[512,512]{1,0:T(8,128)(2,1)S(1)}, bf16[512,512]{1,0:T(8,128)(2,1)S(1)}, u32[]{:S(2)}, u32[]{:S(2)}) collective-permute-start(bf16[512,512]{1,0:T(8,128)(2,1)S(1)} %collective-permute-done.71.refs_17_), channel_id=1, source_target_pairs={{0,1},{1,0},{2,3},{3,2},{4,5},{5,4},{6,7},{7,6},{16,17},{17,16},{1... | collective-permute-start | bytes 1572872 | tf_op jit(solution)/shard_map/ppermute | solution.py:58
  (47 other events, 471.5 us)

commit v2 on v1

--- a/solution.py
+++ b/solution.py
@@ -13,6 +13,8 @@
 BF = jnp.bfloat16
 F32 = jnp.float32
 VMEM_LIMIT = 10 * 2**20
+TIGHT = 64 * 2**20 - 600 * 2**10
+TIGHT_LATE = 60 * 2**20
 
 
 def flat(x, y, z, c):
@@ -51,7 +53,7 @@
 FAR_TWICE = moves(far, lambda x, y, z, c: (x, y, z + 2, c))
 UP_DOWN = moves(z_up, z_down)
 UP_FAR = moves(z_up, far)
-DOWN_STAY = moves(z_down, lambda x, y, z, c: (x, y, z, c))
+DOWN_SWAP = moves(lambda x, y, z, c: (x, y, z - 1, 1), lambda x, y, z, c: (x, y, z, 0))
 
 
 def send(array, pairs):
@@ -88,14 +90,14 @@
     d0 = send(block, FAR_TWICE)
     d1 = send(block, UP_DOWN)
     d2 = send(d0, UP_FAR)
-    d3 = send(d0, DOWN_STAY)
+    d3 = send(d0, DOWN_SWAP)
     got = [send(d, CORE) for d in (d0, d1, d2, d3)]
     return [
         (own, half, (0, 0), (0, 0)),
         (d0, got[0], (1, 0), (0, 2)),
         (d1, got[1], (0, -1), (0, 1)),
         (d2, got[2], (1, -1), (1, 2)),
-        (d3, got[3], (1, 1), None),
+        (got[3], d3, (1, 1), None),
     ]
 
 
@@ -158,6 +160,7 @@
         + [pltpu.VMEM(s.shape, BF)] * 2
         + [pltpu.SemaphoreType.DMA((4,))],
         name="prepare",
+        compiler_params=pltpu.CompilerParams(vmem_limit_bytes=TIGHT),
     )(ps, pz, s, z)
 
 
@@ -184,6 +187,7 @@
         + [pltpu.SMEM((1,), F32), pltpu.VMEM(h.shape, BF)]
         + [pltpu.SemaphoreType.DMA((5,))],
         name="prepare_late",
+        compiler_params=pltpu.CompilerParams(vmem_limit_bytes=TIGHT_LATE),
     )(ph, fi, fs, mu, h)
 
 
@@ -300,7 +304,7 @@
 def body(s, z, h, mu, ps, pz, ph, fi, fs):
     seff, zeff = prepare(ps, pz, s, z)
     heff, keep_inverse, keep_sign, mu = prepare_late(ph, fi, fs, mu, h)
-    z_rows = gather_rows(zeff, True)
+    z_rows = gather_rows(zeff, False)
     s_cols = gather_cols(seff)
     first = product(end_first, z_rows, s_cols)
     f_rows = gather_rows(first, False)
@@ -309,7 +313,7 @@
     r_rows = gather_rows(refined, False)
     h_cols = gather_cols(heff)
     shifted = product(end_shifted, r_rows, h_cols, (keep_sign, mu))
-    x_rows = gather_rows(shifted, True)
+    x_rows = gather_rows(shifted, False)
     x_cols = gather_cols(shifted)
     error, refined = product(end_error, r_rows, s_cols, (refined,), 2)
     square = product(end_square, x_rows, x_cols, (keep_sign,))

time: 210 us -> 209 us (level)
  starting transfers between devices: 119 us -> 95.3 us
  waiting for transfers between devices: 71.4 us -> 93.7 us
    ppermute x73, starting transfers between devices: 119 us -> 95.3 us  [send(): return lax.ppermute(array, AXES, pairs)]
    ppermute x73, waiting for transfers between devices: 71.4 us -> 93.7 us  [send(): return lax.ppermute(array, AXES, pairs)]
  transfers between devices with their start and end apart: 73 -> 73, of which waited for: 21 -> 33; matrix products, arithmetic and copies ran while one was open for 0% -> 1% of each run, Pallas kernels for 4% -> 4%
where the time goes in v2:
time: 209 us
  starting transfers between devices  95.3 us (46%)
  waiting for transfers between devices  93.7 us (45%)
  Pallas kernels  17.1 us (8%)
    ppermute x73, starting transfers between devices, send(): return lax.ppermute(array, AXES, pairs)  95.3 us
    ppermute x73, waiting for transfers between devices, send(): return lax.ppermute(array, AXES, pairs)  93.7 us
    pallas_call x6, Pallas kernels, product(): pl.pallas_call(functools.partial(product_body, finish, len(extras), n_out...  12.5 us
  transfers between devices with their start and end apart: 73, of which 33 were waited for; matrix products, arithmetic and copies ran while one was open for 1% of the time, Pallas kernels for 4%

profile of v2, /device:TPU:1, one launch (start us, length us, event | category | flops | bytes accessed | tf_op | source)
XLA Modules:
  0.0 209.0 jit_solution(12224330953746527257)
XLA Ops:
  4.4 3.0 %collective-permute-start.5 = (bf16[256,512]{1,0:T(8,128)(2,1)}, bf16[256,512]{1,0:T(8,128)(2,1)S(1)}, u32[]{:S(2)}, u32[]{:S(2)}) collective-permute-start(bf16[256,512]{1,0:T(8,128)(2,1)} %get-tuple-element.12.refs_0_.refs_1_.refs_10_), channel_id=1, source_target_pairs={{0,32},{1,33},{2,34},{3,35},{4,36},{5,37},{6,38},{7,39},{16,48},{1... | collective-permute-start | bytes 786440 | tf_op jit(solution)/shard_map/ppermute | solution.py:60
  10.0 2.4 %prepare_late.1 = (bf16[256,512]{1,0:T(8,128)(2,1)}, bf16[256,512]{1,0:T(8,128)(2,1)}, bf16[256,512]{1,0:T(8,128)(2,1)}, f32[8,128]{1,0:T(8,128)}) custom-call(s32[32,32]{1,0:T(8,128)} %refs_0_.2, s32[32,32]{1,0:T(8,128)} %refs_1_.2, s32[32,32]{1,0:T(8,128)} %refs_2_.2, f32[1]{0:T(128)S(6)} %copy.15.refs_3_, bf16[256,512]{1,0:T(8,128)(2,1)} %refs_4_.1), custom_call_target="tpu_custom_call" | custom-call | tf_op jit(solution)/shard_map/prepare_late/pallas_call | solution.py:181
  19.7 3.8 %collective-permute-start.26 = (bf16[512,512]{1,0:T(8,128)(2,1)S(1)}, bf16[512,512]{1,0:T(8,128)(2,1)S(1)}, u32[]{:S(2)}, u32[]{:S(2)}) collective-permute-start(bf16[512,512]{1,0:T(8,128)(2,1)S(1)} %constant_dynamic-update-slice_fusion.2), channel_id=1, source_target_pairs={{0,2},{1,7},{2,4},{3,1},{4,6},{5,3},{6,0},{7,5},{16,18},{17,23},{1... | collective-permute-start | bytes 1572872 | tf_op jit(solution)/shard_map/ppermute | solution.py:60
  31.2 4.0 %collective-permute-done.26.refs_14_ = bf16[512,512]{1,0:T(8,128)(2,1)S(1)} collective-permute-done((bf16[512,512]{1,0:T(8,128)(2,1)S(1)}, bf16[512,512]{1,0:T(8,128)(2,1)S(1)}, u32[]{:S(2)}, u32[]{:S(2)}) %collective-permute-start.26) | collective-permute-done | bytes 524320 | tf_op jit(solution)/shard_map/ppermute | solution.py:60
  35.2 2.9 %collective-permute-done.24.refs_12_ = bf16[512,512]{1,0:T(8,128)(2,1)S(1)} collective-permute-done((bf16[512,512]{1,0:T(8,128)(2,1)S(1)}, bf16[512,512]{1,0:T(8,128)(2,1)S(1)}, u32[]{:S(2)}, u32[]{:S(2)}) %collective-permute-start.24) | collective-permute-done | bytes 524320 | tf_op jit(solution)/shard_map/ppermute | solution.py:60
  38.0 3.8 %collective-permute-start.27 = (bf16[512,512]{1,0:T(8,128)(2,1)S(1)}, bf16[512,512]{1,0:T(8,128)(2,1)S(1)}, u32[]{:S(2)}, u32[]{:S(2)}) collective-permute-start(bf16[512,512]{1,0:T(8,128)(2,1)S(1)} %collective-permute-done.26.refs_14_), channel_id=1, source_target_pairs={{0,1},{1,0},{2,3},{3,2},{4,5},{5,4},{6,7},{7,6},{16,17},{17,16},{1... | collective-permute-start | bytes 1572872 | tf_op jit(solution)/shard_map/ppermute | solution.py:60
  41.8 4.6 %collective-permute-done.10.refs_12_.refs_13_ = bf16[512,512]{1,0:T(8,128)(2,1)S(1)} collective-permute-done((bf16[512,512]{1,0:T(8,128)(2,1)S(1)}, bf16[512,512]{1,0:T(8,128)(2,1)S(1)}, u32[]{:S(2)}, u32[]{:S(2)}) %collective-permute-start.10) | collective-permute-done | bytes 524320 | tf_op jit(solution)/shard_map/ppermute | solution.py:60
  46.4 3.7 %collective-permute-start.30 = (bf16[512,512]{1,0:T(8,128)(2,1)S(1)}, bf16[512,512]{1,0:T(8,128)(2,1)S(1)}, u32[]{:S(2)}, u32[]{:S(2)}) collective-permute-start(bf16[512,512]{1,0:T(8,128)(2,1)S(1)} %collective-permute-done.24.refs_12_), channel_id=1, source_target_pairs={{0,7},{1,0},{2,1},{3,2},{4,3},{5,4},{6,5},{7,6},{16,23},{17,16},{1... | collective-permute-start | bytes 1572872 | tf_op jit(solution)/shard_map/ppermute | solution.py:60
  50.2 7.3 %collective-permute-done.42.refs_14_ = bf16[512,512]{1,0:T(8,128)(2,1)S(1)} collective-permute-done((bf16[512,512]{1,0:T(8,128)(2,1)S(1)}, bf16[512,512]{1,0:T(8,128)(2,1)S(1)}, u32[]{:S(2)}, u32[]{:S(2)}) %collective-permute-start.42) | collective-permute-done | bytes 524320 | tf_op jit(solution)/shard_map/ppermute | solution.py:60
  57.5 3.1 %collective-permute-start.12 = (bf16[512,512]{1,0:T(8,128)(2,1)S(1)}, bf16[512,512]{1,0:T(8,128)(2,1)S(1)}, u32[]{:S(2)}, u32[]{:S(2)}) collective-permute-start(bf16[512,512]{1,0:T(8,128)(2,1)S(1)} %collective-permute-done.8.refs_10_.refs_11_), channel_id=1, source_target_pairs={{0,2},{1,9},{2,4},{3,11},{4,6},{5,13},{6,0},{7,15},{16,18},{17,25}... | collective-permute-start | bytes 1572872 | tf_op jit(solution)/shard_map/ppermute | solution.py:60
  60.5 2.4 %collective-permute-start.28 = (bf16[512,512]{1,0:T(8,128)(2,1)S(1)}, bf16[512,512]{1,0:T(8,128)(2,1)S(1)}, u32[]{:S(2)}, u32[]{:S(2)}) collective-permute-start(bf16[512,512]{1,0:T(8,128)(2,1)S(1)} %collective-permute-done.24.refs_12_), channel_id=1, source_target_pairs={{0,2},{1,9},{2,4},{3,11},{4,6},{5,13},{6,0},{7,15},{16,18},{17,25}... | collective-permute-start | bytes 1572872 | tf_op jit(solution)/shard_map/ppermute | solution.py:60
  63.6 3.9 %collective-permute-done.14.refs_17_.refs_18_ = bf16[512,512]{1,0:T(8,128)(2,1)S(1)} collective-permute-done((bf16[512,512]{1,0:T(8,128)(2,1)S(1)}, bf16[512,512]{1,0:T(8,128)(2,1)S(1)}, u32[]{:S(2)}, u32[]{:S(2)}) %collective-permute-start.14) | collective-permute-done | bytes 524320 | tf_op jit(solution)/shard_map/ppermute | solution.py:60
  72.7 4.4 %collective-permute-start.25 = (bf16[512,512]{1,0:T(8,128)(2,1)S(1)}, bf16[512,512]{1,0:T(8,128)(2,1)S(1)}, u32[]{:S(2)}, u32[]{:S(2)}) collective-permute-start(bf16[512,512]{1,0:T(8,128)(2,1)S(1)} %collective-permute-done.24.refs_12_), channel_id=1, source_target_pairs={{0,1},{1,0},{2,3},{3,2},{4,5},{5,4},{6,7},{7,6},{16,17},{17,16},{1... | collective-permute-start | bytes 1572872 | tf_op jit(solution)/shard_map/ppermute | solution.py:60
  77.1 2.8 %collective-permute-start.44 = (bf16[512,512]{1,0:T(8,128)(2,1)S(1)}, bf16[512,512]{1,0:T(8,128)(2,1)S(1)}, u32[]{:S(2)}, u32[]{:S(2)}) collective-permute-start(bf16[512,512]{1,0:T(8,128)(2,1)S(1)} %collective-permute-done.40.refs_12_), channel_id=1, source_target_pairs={{0,2},{1,9},{2,4},{3,11},{4,6},{5,13},{6,0},{7,15},{16,18},{17,25}... | collective-permute-start | bytes 1572872 | tf_op jit(solution)/shard_map/ppermute | solution.py:60
  88.7 2.9 %collective-permute-done.21.refs_8_ = bf16[256,512]{1,0:T(8,128)(2,1)S(1)} collective-permute-done((bf16[256,512]{1,0:T(8,128)(2,1)S(1)}, bf16[256,512]{1,0:T(8,128)(2,1)S(1)}, u32[]{:S(2)}, u32[]{:S(2)}) %collective-permute-start.21) | collective-permute-done | bytes 262176 | tf_op jit(solution)/shard_map/ppermute | solution.py:60
  105.5 3.1 %collective-permute-start.37 = (bf16[256,512]{1,0:T(8,128)(2,1)S(1)}, bf16[256,512]{1,0:T(8,128)(2,1)S(1)}, u32[]{:S(2)}, u32[]{:S(2)}) collective-permute-start(bf16[256,512]{1,0:T(8,128)(2,1)S(1)} %shard_map.113.refs_0_.refs_1_.refs_2_), channel_id=1, source_target_pairs={{0,32},{1,33},{2,34},{3,35},{4,36},{5,37},{6,38},{7,39},{16,48},{1... | collective-permute-start | bytes 786440 | tf_op jit(solution)/shard_map/ppermute | solution.py:60
  110.1 2.8 %collective-permute-done.37.refs_7_.refs_8_ = bf16[256,512]{1,0:T(8,128)(2,1)S(1)} collective-permute-done((bf16[256,512]{1,0:T(8,128)(2,1)S(1)}, bf16[256,512]{1,0:T(8,128)(2,1)S(1)}, u32[]{:S(2)}, u32[]{:S(2)}) %collective-permute-start.37) | collective-permute-done | bytes 262176 | tf_op jit(solution)/shard_map/ppermute | solution.py:60
  114.7 2.8 %collective-permute-start.36 = (bf16[256,512]{1,0:T(8,128)(2,1)S(1)}, bf16[256,512]{1,0:T(8,128)(2,1)S(1)}, u32[]{:S(2)}, u32[]{:S(2)}) collective-permute-start(bf16[256,512]{1,0:T(8,128)(2,1)S(1)} %collective-permute-done.32.refs_2_.refs_3_), channel_id=1, source_target_pairs={{0,48},{1,49},{2,50},{3,51},{4,52},{5,53},{6,54},{7,55},{16,0},{17... | collective-permute-start | bytes 786440 | tf_op jit(solution)/shard_map/ppermute | solution.py:60
  120.3 3.5 %collective-permute-done.36.refs_6_.refs_7_ = bf16[256,512]{1,0:T(8,128)(2,1)S(1)} collective-permute-done((bf16[256,512]{1,0:T(8,128)(2,1)S(1)}, bf16[256,512]{1,0:T(8,128)(2,1)S(1)}, u32[]{:S(2)}, u32[]{:S(2)}) %collective-permute-start.36) | collective-permute-done | bytes 262176 | tf_op jit(solution)/shard_map/ppermute | solution.py:60
  126.0 4.7 %collective-permute-start.55 = (bf16[256,512]{1,0:T(8,128)(2,1)S(1)}, bf16[256,512]{1,0:T(8,128)(2,1)S(1)}, u32[]{:S(2)}, u32[]{:S(2)}) collective-permute-start(bf16[256,512]{1,0:T(8,128)(2,1)S(1)} %shard_map.115.refs_1_.refs_9_.refs_0_), channel_id=1, source_target_pairs={{0,1},{1,0},{2,3},{3,2},{4,5},{5,4},{6,7},{7,6},{16,17},{17,16},{1... | collective-permute-start | bytes 786440 | tf_op jit(solution)/shard_map/ppermute | solution.py:60
  135.7 3.5 %collective-permute-start.58 = (bf16[512,512]{1,0:T(8,128)(2,1)S(1)}, bf16[512,512]{1,0:T(8,128)(2,1)S(1)}, u32[]{:S(2)}, u32[]{:S(2)}) collective-permute-start(bf16[512,512]{1,0:T(8,128)(2,1)S(1)} %pad_maximum_fusion), channel_id=1, source_target_pairs={{0,2},{1,7},{2,4},{3,1},{4,6},{5,3},{6,0},{7,5},{16,18},{17,23},{1... | collective-permute-start | bytes 1572872 | tf_op jit(solution)/shard_map/ppermute | solution.py:60
  139.2 2.6 %collective-permute-done.56.refs_11_ = bf16[512,512]{1,0:T(8,128)(2,1)S(1)} collective-permute-done((bf16[512,512]{1,0:T(8,128)(2,1)S(1)}, bf16[512,512]{1,0:T(8,128)(2,1)S(1)}, u32[]{:S(2)}, u32[]{:S(2)}) %collective-permute-start.56) | collective-permute-done | bytes 524320 | tf_op jit(solution)/shard_map/ppermute | solution.py:60
  143.0 2.7 %collective-permute-start.60 = (bf16[512,512]{1,0:T(8,128)(2,1)S(1)}, bf16[512,512]{1,0:T(8,128)(2,1)S(1)}, u32[]{:S(2)}, u32[]{:S(2)}) collective-permute-start(bf16[512,512]{1,0:T(8,128)(2,1)S(1)} %collective-permute-done.56.refs_11_), channel_id=1, source_target_pairs={{0,2},{1,9},{2,4},{3,11},{4,6},{5,13},{6,0},{7,15},{16,18},{17,25}... | collective-permute-start | bytes 1572872 | tf_op jit(solution)/shard_map/ppermute | solution.py:60
  149.6 10.0 %collective-permute-done.48.refs_2_ = bf16[256,512]{1,0:T(8,128)(2,1)S(1)} collective-permute-done((bf16[256,512]{1,0:T(8,128)(2,1)S(1)}, bf16[256,512]{1,0:T(8,128)(2,1)S(1)}, u32[]{:S(2)}, u32[]{:S(2)}) %collective-permute-start.48) | collective-permute-done | bytes 262176 | tf_op jit(solution)/shard_map/ppermute | solution.py:60
  159.7 3.9 %collective-permute-done.54.refs_8_ = bf16[256,512]{1,0:T(8,128)(2,1)S(1)} collective-permute-done((bf16[256,512]{1,0:T(8,128)(2,1)S(1)}, bf16[256,512]{1,0:T(8,128)(2,1)S(1)}, u32[]{:S(2)}, u32[]{:S(2)}) %collective-permute-start.54) | collective-permute-done | bytes 262176 | tf_op jit(solution)/shard_map/ppermute | solution.py:60
  166.8 7.9 %collective-permute-done.51.refs_5_ = bf16[256,512]{1,0:T(8,128)(2,1)S(1)} collective-permute-done((bf16[256,512]{1,0:T(8,128)(2,1)S(1)}, bf16[256,512]{1,0:T(8,128)(2,1)S(1)}, u32[]{:S(2)}, u32[]{:S(2)}) %collective-permute-start.51) | collective-permute-done | bytes 262176 | tf_op jit(solution)/shard_map/ppermute | solution.py:60
  180.4 2.9 %collective-permute-start.67 = (bf16[512,512]{1,0:T(8,128)(2,1)S(1)}, bf16[512,512]{1,0:T(8,128)(2,1)S(1)}, u32[]{:S(2)}, u32[]{:S(2)}) collective-permute-start(bf16[512,512]{1,0:T(8,128)(2,1)S(1)} %pad_maximum_fusion.1), channel_id=1, source_target_pairs={{0,2},{1,7},{2,4},{3,1},{4,6},{5,3},{6,0},{7,5},{16,18},{17,23},{1... | collective-permute-start | bytes 1572872 | tf_op jit(solution)/shard_map/ppermute | solution.py:60
  183.2 8.5 %collective-permute-done.65.refs_11_ = bf16[512,512]{1,0:T(8,128)(2,1)S(1)} collective-permute-done((bf16[512,512]{1,0:T(8,128)(2,1)S(1)}, bf16[512,512]{1,0:T(8,128)(2,1)S(1)}, u32[]{:S(2)}, u32[]{:S(2)}) %collective-permute-start.65) | collective-permute-done | bytes 524320 | tf_op jit(solution)/shard_map/ppermute | solution.py:60
  193.9 3.1 %collective-permute-done.67.refs_13_ = bf16[512,512]{1,0:T(8,128)(2,1)S(1)} collective-permute-done((bf16[512,512]{1,0:T(8,128)(2,1)S(1)}, bf16[512,512]{1,0:T(8,128)(2,1)S(1)}, u32[]{:S(2)}, u32[]{:S(2)}) %collective-permute-start.67) | collective-permute-done | bytes 524320 | tf_op jit(solution)/shard_map/ppermute | solution.py:60
  197.0 4.8 %collective-permute-done.71.refs_18_ = bf16[512,512]{1,0:T(8,128)(2,1)S(1)} collective-permute-done((bf16[512,512]{1,0:T(8,128)(2,1)S(1)}, bf16[512,512]{1,0:T(8,128)(2,1)S(1)}, u32[]{:S(2)}, u32[]{:S(2)}) %collective-permute-start.71) | collective-permute-done | bytes 524320 | tf_op jit(solution)/shard_map/ppermute | solution.py:60
  203.7 2.5 %shard_map.114 = (bf16[256,512]{1,0:T(8,128)(2,1)}, bf16[256,512]{1,0:T(8,128)(2,1)}) custom-call(bf16[256,512]{1,0:T(8,128)(2,1)S(1)} %shard_map.113.refs_0_.refs_1_.refs_2_, bf16[256,512]{1,0:T(8,128)(2,1)S(1)} %shard_map.113.refs_0_.refs_1_.refs_2_, bf16[256,512]{1,0:T(8,128)(2,1)S(1)} %collective-permute-done.32.refs_2_.refs_3_, ...), custom_call_target="tpu_custom_call" | custom-call | tf_op jit(solution)/shard_map/pallas_call | solution.py:259
  206.3 2.5 %shard_map.117 = bf16[256,512]{1,0:T(8,128)(2,1)} custom-call(bf16[256,512]{1,0:T(8,128)(2,1)S(1)} %shard_map.115.refs_1_.refs_9_.refs_0_, bf16[256,512]{1,0:T(8,128)(2,1)S(1)} %shard_map.115.refs_1_.refs_9_.refs_0_, bf16[256,512]{1,0:T(8,128)(2,1)S(1)} %collective-permute-done.48.refs_2_, bf16[256,512]{1,0:T(8,128)(2,1)S(1)} %collective-permute-done.49.refs_3_, ...), custom_call_target="tpu_custom_call" | custom-call | tf_op jit(solution)/shard_map/pallas_call | solution.py:259
  (142 shorter events, 80.5 us)
Async XLA Ops:
  4.4 11.5 %collective-permute-start.5 = (bf16[256,512]{1,0:T(8,128)(2,1)}, bf16[256,512]{1,0:T(8,128)(2,1)S(1)}, u32[]{:S(2)}, u32[]{:S(2)}) collective-permute-start(bf16[256,512]{1,0:T(8,128)(2,1)} %get-tuple-element.12.refs_0_.refs_1_.refs_10_), channel_id=1, source_target_pairs={{0,32},{1,33},{2,34},{3,35},{4,36},{5,37},{6,38},{7,39},{16,48},{1... | collective-permute-start | bytes 786440 | tf_op jit(solution)/shard_map/ppermute | solution.py:60
  16.2 11.4 %collective-permute-start.4 = (bf16[256,512]{1,0:T(8,128)(2,1)S(1)}, bf16[256,512]{1,0:T(8,128)(2,1)S(1)}, u32[]{:S(2)}, u32[]{:S(2)}) collective-permute-start(bf16[256,512]{1,0:T(8,128)(2,1)S(1)} %collective-permute-done.refs_1_), channel_id=1, source_target_pairs={{0,48},{1,49},{2,50},{3,51},{4,52},{5,53},{6,54},{7,55},{16,0},{17... | collective-permute-start | bytes 786440 | tf_op jit(solution)/shard_map/ppermute | solution.py:60
  19.7 15.5 %collective-permute-start.26 = (bf16[512,512]{1,0:T(8,128)(2,1)S(1)}, bf16[512,512]{1,0:T(8,128)(2,1)S(1)}, u32[]{:S(2)}, u32[]{:S(2)}) collective-permute-start(bf16[512,512]{1,0:T(8,128)(2,1)S(1)} %constant_dynamic-update-slice_fusion.2), channel_id=1, source_target_pairs={{0,2},{1,7},{2,4},{3,1},{4,6},{5,3},{6,0},{7,5},{16,18},{17,23},{1... | collective-permute-start | bytes 1572872 | tf_op jit(solution)/shard_map/ppermute | solution.py:60
  23.4 14.6 %collective-permute-start.24 = (bf16[512,512]{1,0:T(8,128)(2,1)S(1)}, bf16[512,512]{1,0:T(8,128)(2,1)S(1)}, u32[]{:S(2)}, u32[]{:S(2)}) collective-permute-start(bf16[512,512]{1,0:T(8,128)(2,1)S(1)} %constant_dynamic-update-slice_fusion.2), channel_id=1, source_target_pairs={{0,8},{1,5},{2,10},{3,7},{4,12},{5,1},{6,14},{7,3},{16,24},{17,21}... | collective-permute-start | bytes 1572872 | tf_op jit(solution)/shard_map/ppermute | solution.py:60
  25.3 21.1 %collective-permute-start.10 = (bf16[512,512]{1,0:T(8,128)(2,1)S(1)}, bf16[512,512]{1,0:T(8,128)(2,1)S(1)}, u32[]{:S(2)}, u32[]{:S(2)}) collective-permute-start(bf16[512,512]{1,0:T(8,128)(2,1)S(1)} %constant_dynamic-update-slice_fusion), channel_id=1, source_target_pairs={{0,2},{1,7},{2,4},{3,1},{4,6},{5,3},{6,0},{7,5},{16,18},{17,23},{1... | collective-permute-start | bytes 1572872 | tf_op jit(solution)/shard_map/ppermute | solution.py:60
  27.5 22.5 %collective-permute-start.8 = (bf16[512,512]{1,0:T(8,128)(2,1)S(1)}, bf16[512,512]{1,0:T(8,128)(2,1)S(1)}, u32[]{:S(2)}, u32[]{:S(2)}) collective-permute-start(bf16[512,512]{1,0:T(8,128)(2,1)S(1)} %constant_dynamic-update-slice_fusion), channel_id=1, source_target_pairs={{0,8},{1,5},{2,10},{3,7},{4,12},{5,1},{6,14},{7,3},{16,24},{17,21}... | collective-permute-start | bytes 1572872 | tf_op jit(solution)/shard_map/ppermute | solution.py:60
  30.7 26.7 %collective-permute-start.42 = (bf16[512,512]{1,0:T(8,128)(2,1)S(1)}, bf16[512,512]{1,0:T(8,128)(2,1)S(1)}, u32[]{:S(2)}, u32[]{:S(2)}) collective-permute-start(bf16[512,512]{1,0:T(8,128)(2,1)S(1)} %constant_dynamic-update-slice_fusion.4), channel_id=1, source_target_pairs={{0,2},{1,7},{2,4},{3,1},{4,6},{5,3},{6,0},{7,5},{16,18},{17,23},{1... | collective-permute-start | bytes 1572872 | tf_op jit(solution)/shard_map/ppermute | solution.py:60
  35.2 25.4 %collective-permute-start.40 = (bf16[512,512]{1,0:T(8,128)(2,1)S(1)}, bf16[512,512]{1,0:T(8,128)(2,1)S(1)}, u32[]{:S(2)}, u32[]{:S(2)}) collective-permute-start(bf16[512,512]{1,0:T(8,128)(2,1)S(1)} %constant_dynamic-update-slice_fusion.4), channel_id=1, source_target_pairs={{0,8},{1,5},{2,10},{3,7},{4,12},{5,1},{6,14},{7,3},{16,24},{17,21}... | collective-permute-start | bytes 1572872 | tf_op jit(solution)/shard_map/ppermute | solution.py:60
  38.0 24.9 %collective-permute-start.27 = (bf16[512,512]{1,0:T(8,128)(2,1)S(1)}, bf16[512,512]{1,0:T(8,128)(2,1)S(1)}, u32[]{:S(2)}, u32[]{:S(2)}) collective-permute-start(bf16[512,512]{1,0:T(8,128)(2,1)S(1)} %collective-permute-done.26.refs_14_), channel_id=1, source_target_pairs={{0,1},{1,0},{2,3},{3,2},{4,5},{5,4},{6,7},{7,6},{16,17},{17,16},{1... | collective-permute-start | bytes 1572872 | tf_op jit(solution)/shard_map/ppermute | solution.py:60
  46.4 16.6 %collective-permute-start.30 = (bf16[512,512]{1,0:T(8,128)(2,1)S(1)}, bf16[512,512]{1,0:T(8,128)(2,1)S(1)}, u32[]{:S(2)}, u32[]{:S(2)}) collective-permute-start(bf16[512,512]{1,0:T(8,128)(2,1)S(1)} %collective-permute-done.24.refs_12_), channel_id=1, source_target_pairs={{0,7},{1,0},{2,1},{3,2},{4,3},{5,4},{6,5},{7,6},{16,23},{17,16},{1... | collective-permute-start | bytes 1572872 | tf_op jit(solution)/shard_map/ppermute | solution.py:60
  50.0 17.5 %collective-permute-start.14 = (bf16[512,512]{1,0:T(8,128)(2,1)S(1)}, bf16[512,512]{1,0:T(8,128)(2,1)S(1)}, u32[]{:S(2)}, u32[]{:S(2)}) collective-permute-start(bf16[512,512]{1,0:T(8,128)(2,1)S(1)} %collective-permute-done.8.refs_10_.refs_11_), channel_id=1, source_target_pairs={{0,7},{1,0},{2,1},{3,2},{4,3},{5,4},{6,5},{7,6},{16,23},{17,16},{1... | collective-permute-start | bytes 1572872 | tf_op jit(solution)/shard_map/ppermute | solution.py:60
  57.5 11.8 %collective-permute-start.12 = (bf16[512,512]{1,0:T(8,128)(2,1)S(1)}, bf16[512,512]{1,0:T(8,128)(2,1)S(1)}, u32[]{:S(2)}, u32[]{:S(2)}) collective-permute-start(bf16[512,512]{1,0:T(8,128)(2,1)S(1)} %collective-permute-done.8.refs_10_.refs_11_), channel_id=1, source_target_pairs={{0,2},{1,9},{2,4},{3,11},{4,6},{5,13},{6,0},{7,15},{16,18},{17,25}... | collective-permute-start | bytes 1572872 | tf_op jit(solution)/shard_map/ppermute | solution.py:60
  60.5 12.2 %collective-permute-start.28 = (bf16[512,512]{1,0:T(8,128)(2,1)S(1)}, bf16[512,512]{1,0:T(8,128)(2,1)S(1)}, u32[]{:S(2)}, u32[]{:S(2)}) collective-permute-start(bf16[512,512]{1,0:T(8,128)(2,1)S(1)} %collective-permute-done.24.refs_12_), channel_id=1, source_target_pairs={{0,2},{1,9},{2,4},{3,11},{4,6},{5,13},{6,0},{7,15},{16,18},{17,25}... | collective-permute-start | bytes 1572872 | tf_op jit(solution)/shard_map/ppermute | solution.py:60
  63.0 14.1 %collective-permute-start.11 = (bf16[512,512]{1,0:T(8,128)(2,1)S(1)}, bf16[512,512]{1,0:T(8,128)(2,1)S(1)}, u32[]{:S(2)}, u32[]{:S(2)}) collective-permute-start(bf16[512,512]{1,0:T(8,128)(2,1)S(1)} %collective-permute-done.10.refs_12_.refs_13_), channel_id=1, source_target_pairs={{0,1},{1,0},{2,3},{3,2},{4,5},{5,4},{6,7},{7,6},{16,17},{17,16},{1... | collective-permute-start | bytes 1572872 | tf_op jit(solution)/shard_map/ppermute | solution.py:60
  63.0 14.1 %collective-permute-start.9 = (bf16[512,512]{1,0:T(8,128)(2,1)S(1)}, bf16[512,512]{1,0:T(8,128)(2,1)S(1)}, u32[]{:S(2)}, u32[]{:S(2)}) collective-permute-start(bf16[512,512]{1,0:T(8,128)(2,1)S(1)} %collective-permute-done.8.refs_10_.refs_11_), channel_id=1, source_target_pairs={{0,1},{1,0},{2,3},{3,2},{4,5},{5,4},{6,7},{7,6},{16,17},{17,16},{1... | collective-permute-start | bytes 1572872 | tf_op jit(solution)/shard_map/ppermute | solution.py:60
  67.6 12.4 %collective-permute-start.15 = (bf16[512,512]{1,0:T(8,128)(2,1)S(1)}, bf16[512,512]{1,0:T(8,128)(2,1)S(1)}, u32[]{:S(2)}, u32[]{:S(2)}) collective-permute-start(bf16[512,512]{1,0:T(8,128)(2,1)S(1)} %collective-permute-done.14.refs_17_.refs_18_), channel_id=1, source_target_pairs={{0,1},{1,0},{2,3},{3,2},{4,5},{5,4},{6,7},{7,6},{16,17},{17,16},{1... | collective-permute-start | bytes 1572872 | tf_op jit(solution)/shard_map/ppermute | solution.py:60
  79.9 11.8 %collective-permute-start.29 = (bf16[512,512]{1,0:T(8,128)(2,1)S(1)}, bf16[512,512]{1,0:T(8,128)(2,1)S(1)}, u32[]{:S(2)}, u32[]{:S(2)}) collective-permute-start(bf16[512,512]{1,0:T(8,128)(2,1)S(1)} %collective-permute-done.28.refs_16_), channel_id=1, source_target_pairs={{0,1},{1,0},{2,3},{3,2},{4,5},{5,4},{6,7},{7,6},{16,17},{17,16},{1... | collective-permute-start | bytes 1572872 | tf_op jit(solution)/shard_map/ppermute | solution.py:60
  91.8 16.7 %collective-permute-start.43 = (bf16[512,512]{1,0:T(8,128)(2,1)S(1)}, bf16[512,512]{1,0:T(8,128)(2,1)S(1)}, u32[]{:S(2)}, u32[]{:S(2)}) collective-permute-start(bf16[512,512]{1,0:T(8,128)(2,1)S(1)} %collective-permute-done.42.refs_14_), channel_id=1, source_target_pairs={{0,1},{1,0},{2,3},{3,2},{4,5},{5,4},{6,7},{7,6},{16,17},{17,16},{1... | collective-permute-start | bytes 1572872 | tf_op jit(solution)/shard_map/ppermute | solution.py:60
  94.7 13.9 %collective-permute-start.41 = (bf16[512,512]{1,0:T(8,128)(2,1)S(1)}, bf16[512,512]{1,0:T(8,128)(2,1)S(1)}, u32[]{:S(2)}, u32[]{:S(2)}) collective-permute-start(bf16[512,512]{1,0:T(8,128)(2,1)S(1)} %collective-permute-done.40.refs_12_), channel_id=1, source_target_pairs={{0,1},{1,0},{2,3},{3,2},{4,5},{5,4},{6,7},{7,6},{16,17},{17,16},{1... | collective-permute-start | bytes 1572872 | tf_op jit(solution)/shard_map/ppermute | solution.py:60
  98.0 11.5 %collective-permute-start.47 = (bf16[512,512]{1,0:T(8,128)(2,1)S(1)}, bf16[512,512]{1,0:T(8,128)(2,1)S(1)}, u32[]{:S(2)}, u32[]{:S(2)}) collective-permute-start(bf16[512,512]{1,0:T(8,128)(2,1)S(1)} %collective-permute-done.46.refs_19_), channel_id=1, source_target_pairs={{0,1},{1,0},{2,3},{3,2},{4,5},{5,4},{6,7},{7,6},{16,17},{17,16},{1... | collective-permute-start | bytes 1572872 | tf_op jit(solution)/shard_map/ppermute | solution.py:60
  101.0 16.6 %collective-permute-start.45 = (bf16[512,512]{1,0:T(8,128)(2,1)S(1)}, bf16[512,512]{1,0:T(8,128)(2,1)S(1)}, u32[]{:S(2)}, u32[]{:S(2)}) collective-permute-start(bf16[512,512]{1,0:T(8,128)(2,1)S(1)} %collective-permute-done.44.refs_16_), channel_id=1, source_target_pairs={{0,1},{1,0},{2,3},{3,2},{4,5},{5,4},{6,7},{7,6},{16,17},{17,16},{1... | collective-permute-start | bytes 1572872 | tf_op jit(solution)/shard_map/ppermute | solution.py:60
  134.0 12.5 %collective-permute-start.50 = (bf16[256,512]{1,0:T(8,128)(2,1)S(1)}, bf16[256,512]{1,0:T(8,128)(2,1)S(1)}, u32[]{:S(2)}, u32[]{:S(2)}) collective-permute-start(bf16[256,512]{1,0:T(8,128)(2,1)S(1)} %shard_map.115.refs_1_.refs_9_.refs_0_), channel_id=1, source_target_pairs={{0,48},{1,49},{2,50},{3,51},{4,52},{5,53},{6,54},{7,55},{16,0},{17... | collective-permute-start | bytes 786440 | tf_op jit(solution)/shard_map/ppermute | solution.py:60
  135.7 13.1 %collective-permute-start.49 = (bf16[256,512]{1,0:T(8,128)(2,1)S(1)}, bf16[256,512]{1,0:T(8,128)(2,1)S(1)}, u32[]{:S(2)}, u32[]{:S(2)}) collective-permute-start(bf16[256,512]{1,0:T(8,128)(2,1)S(1)} %shard_map.115.refs_1_.refs_9_.refs_0_), channel_id=1, source_target_pairs={{0,16},{1,17},{2,18},{3,19},{4,20},{5,21},{6,22},{7,23},{16,32},{1... | collective-permute-start | bytes 786440 | tf_op jit(solution)/shard_map/ppermute | solution.py:60
  135.7 27.8 %collective-permute-start.58 = (bf16[512,512]{1,0:T(8,128)(2,1)S(1)}, bf16[512,512]{1,0:T(8,128)(2,1)S(1)}, u32[]{:S(2)}, u32[]{:S(2)}) collective-permute-start(bf16[512,512]{1,0:T(8,128)(2,1)S(1)} %pad_maximum_fusion), channel_id=1, source_target_pairs={{0,2},{1,7},{2,4},{3,1},{4,6},{5,3},{6,0},{7,5},{16,18},{17,23},{1... | collective-permute-start | bytes 1572872 | tf_op jit(solution)/shard_map/ppermute | solution.py:60
  141.8 22.2 %collective-permute-start.62 = (bf16[512,512]{1,0:T(8,128)(2,1)S(1)}, bf16[512,512]{1,0:T(8,128)(2,1)S(1)}, u32[]{:S(2)}, u32[]{:S(2)}) collective-permute-start(bf16[512,512]{1,0:T(8,128)(2,1)S(1)} %collective-permute-done.56.refs_11_), channel_id=1, source_target_pairs={{0,7},{1,0},{2,1},{3,2},{4,3},{5,4},{6,5},{7,6},{16,23},{17,16},{1... | collective-permute-start | bytes 1572872 | tf_op jit(solution)/shard_map/ppermute | solution.py:60
  143.0 21.1 %collective-permute-start.60 = (bf16[512,512]{1,0:T(8,128)(2,1)S(1)}, bf16[512,512]{1,0:T(8,128)(2,1)S(1)}, u32[]{:S(2)}, u32[]{:S(2)}) collective-permute-start(bf16[512,512]{1,0:T(8,128)(2,1)S(1)} %collective-permute-done.56.refs_11_), channel_id=1, source_target_pairs={{0,2},{1,9},{2,4},{3,11},{4,6},{5,13},{6,0},{7,15},{16,18},{17,25}... | collective-permute-start | bytes 1572872 | tf_op jit(solution)/shard_map/ppermute | solution.py:60
  146.5 13.2 %collective-permute-start.48 = (bf16[256,512]{1,0:T(8,128)(2,1)S(1)}, bf16[256,512]{1,0:T(8,128)(2,1)S(1)}, u32[]{:S(2)}, u32[]{:S(2)}) collective-permute-start(bf16[256,512]{1,0:T(8,128)(2,1)S(1)} %shard_map.115.refs_1_.refs_9_.refs_0_), channel_id=1, source_target_pairs={{0,64},{1,65},{2,66},{3,67},{4,68},{5,69},{6,70},{7,71},{16,80},{1... | collective-permute-start | bytes 786440 | tf_op jit(solution)/shard_map/ppermute | solution.py:60
  148.8 14.7 %collective-permute-start.54 = (bf16[256,512]{1,0:T(8,128)(2,1)S(1)}, bf16[256,512]{1,0:T(8,128)(2,1)S(1)}, u32[]{:S(2)}, u32[]{:S(2)}) collective-permute-start(bf16[256,512]{1,0:T(8,128)(2,1)S(1)} %collective-permute-done.53.refs_7_), channel_id=1, source_target_pairs={{0,64},{1,65},{2,66},{3,67},{4,68},{5,69},{6,70},{7,71},{16,80},{1... | collective-permute-start | bytes 786440 | tf_op jit(solution)/shard_map/ppermute | solution.py:60
  163.5 11.2 %collective-permute-start.57 = (bf16[512,512]{1,0:T(8,128)(2,1)S(1)}, bf16[512,512]{1,0:T(8,128)(2,1)S(1)}, u32[]{:S(2)}, u32[]{:S(2)}) collective-permute-start(bf16[512,512]{1,0:T(8,128)(2,1)S(1)} %collective-permute-done.56.refs_11_), channel_id=1, source_target_pairs={{0,1},{1,0},{2,3},{3,2},{4,5},{5,4},{6,7},{7,6},{16,17},{17,16},{1... | collective-permute-start | bytes 1572872 | tf_op jit(solution)/shard_map/ppermute | solution.py:60
  179.4 12.3 %collective-permute-start.65 = (bf16[512,512]{1,0:T(8,128)(2,1)S(1)}, bf16[512,512]{1,0:T(8,128)(2,1)S(1)}, u32[]{:S(2)}, u32[]{:S(2)}) collective-permute-start(bf16[512,512]{1,0:T(8,128)(2,1)S(1)} %pad_maximum_fusion.1), channel_id=1, source_target_pairs={{0,8},{1,5},{2,10},{3,7},{4,12},{5,1},{6,14},{7,3},{16,24},{17,21}... | collective-permute-start | bytes 1572872 | tf_op jit(solution)/shard_map/ppermute | solution.py:60
  180.4 16.6 %collective-permute-start.67 = (bf16[512,512]{1,0:T(8,128)(2,1)S(1)}, bf16[512,512]{1,0:T(8,128)(2,1)S(1)}, u32[]{:S(2)}, u32[]{:S(2)}) collective-permute-start(bf16[512,512]{1,0:T(8,128)(2,1)S(1)} %pad_maximum_fusion.1), channel_id=1, source_target_pairs={{0,2},{1,7},{2,4},{3,1},{4,6},{5,3},{6,0},{7,5},{16,18},{17,23},{1... | collective-permute-start | bytes 1572872 | tf_op jit(solution)/shard_map/ppermute | solution.py:60
  192.6 13.7 %collective-permute-start.66 = (bf16[512,512]{1,0:T(8,128)(2,1)S(1)}, bf16[512,512]{1,0:T(8,128)(2,1)S(1)}, u32[]{:S(2)}, u32[]{:S(2)}) collective-permute-start(bf16[512,512]{1,0:T(8,128)(2,1)S(1)} %collective-permute-done.65.refs_11_), channel_id=1, source_target_pairs={{0,1},{1,0},{2,3},{3,2},{4,5},{5,4},{6,7},{7,6},{16,17},{17,16},{1... | collective-permute-start | bytes 1572872 | tf_op jit(solution)/shard_map/ppermute | solution.py:60
  (47 other events, 539.3 us)

commit v3 on v2

--- a/solution.py
+++ b/solution.py
@@ -13,8 +13,7 @@
 BF = jnp.bfloat16
 F32 = jnp.float32
 VMEM_LIMIT = 10 * 2**20
-TIGHT = 64 * 2**20 - 600 * 2**10
-TIGHT_LATE = 60 * 2**20
+TIGHT = 60 * 2**20
 
 
 def flat(x, y, z, c):
@@ -150,7 +149,7 @@
 
 
 def prepare(ps, pz, s, z):
-    out = jax.ShapeDtypeStruct(s.shape, BF)
+    out = pltpu.VMEM(s.shape, BF)
     return pl.pallas_call(
         prepare_body,
         out_shape=(out, out),
@@ -177,17 +176,17 @@
 
 
 def prepare_late(ph, fi, fs, mu, h):
-    out = jax.ShapeDtypeStruct(h.shape, BF)
+    out = pltpu.VMEM(h.shape, BF)
     return pl.pallas_call(
         late_body,
-        out_shape=(out, out, out, jax.ShapeDtypeStruct((8, BS), F32)),
+        out_shape=(out, out, out, pltpu.VMEM((8, BS), F32)),
         in_specs=[ANY] * 5,
         out_specs=[VMEM] * 4,
         scratch_shapes=[pltpu.SMEM(ph.shape, jnp.int32)] * 3
         + [pltpu.SMEM((1,), F32), pltpu.VMEM(h.shape, BF)]
         + [pltpu.SemaphoreType.DMA((5,))],
         name="prepare_late",
-        compiler_params=pltpu.CompilerParams(vmem_limit_bytes=TIGHT_LATE),
+        compiler_params=pltpu.CompilerParams(vmem_limit_bytes=TIGHT),
     )(ph, fi, fs, mu, h)
 
 

time: 209 us -> 208 us (level)
  transfers between devices with their start and end apart: 73 -> 73, of which waited for: 33 -> 33; matrix products, arithmetic and copies ran while one was open for 1% -> 0% of each run, Pallas kernels for 4% -> 4%
where the time goes in v3:
time: 208 us
  starting transfers between devices  95.8 us (46%)
  waiting for transfers between devices  94.8 us (46%)
  Pallas kernels  15.5 us (7%)
    ppermute x73, starting transfers between devices, send(): return lax.ppermute(array, AXES, pairs)  95.8 us
    ppermute x73, waiting for transfers between devices, send(): return lax.ppermute(array, AXES, pairs)  94.8 us
    pallas_call x6, Pallas kernels, product(): pl.pallas_call(functools.partial(product_body, finish, len(extras), n_out...  12.5 us
  transfers between devices with their start and end apart: 73, of which 33 were waited for; matrix products, arithmetic and copies ran while one was open for 0% of the time, Pallas kernels for 4%

profile of v3, /device:TPU:1, one launch (start us, length us, event | category | flops | bytes accessed | tf_op | source)
XLA Modules:
  0.0 208.0 jit_solution(5962635032667626449)
XLA Ops:
  3.6 3.0 %collective-permute-start.5 = (bf16[256,512]{1,0:T(8,128)(2,1)S(1)}, bf16[256,512]{1,0:T(8,128)(2,1)S(1)}, u32[]{:S(2)}, u32[]{:S(2)}) collective-permute-start(bf16[256,512]{1,0:T(8,128)(2,1)S(1)} %get-tuple-element.12.refs_0_.refs_1_.refs_10_), channel_id=1, source_target_pairs={{0,32},{1,33},{2,34},{3,35},{4,36},{5,37},{6,38},{7,39},{16,48},{1... | collective-permute-start | bytes 786440 | tf_op jit(solution)/shard_map/ppermute | solution.py:59
  13.9 2.8 %collective-permute-start.4 = (bf16[256,512]{1,0:T(8,128)(2,1)S(1)}, bf16[256,512]{1,0:T(8,128)(2,1)S(1)}, u32[]{:S(2)}, u32[]{:S(2)}) collective-permute-start(bf16[256,512]{1,0:T(8,128)(2,1)S(1)} %collective-permute-done.refs_1_), channel_id=1, source_target_pairs={{0,48},{1,49},{2,50},{3,51},{4,52},{5,53},{6,54},{7,55},{16,0},{17... | collective-permute-start | bytes 786440 | tf_op jit(solution)/shard_map/ppermute | solution.py:59
  18.7 3.8 %collective-permute-start.26 = (bf16[512,512]{1,0:T(8,128)(2,1)S(1)}, bf16[512,512]{1,0:T(8,128)(2,1)S(1)}, u32[]{:S(2)}, u32[]{:S(2)}) collective-permute-start(bf16[512,512]{1,0:T(8,128)(2,1)S(1)} %constant_dynamic-update-slice_fusion.2), channel_id=1, source_target_pairs={{0,2},{1,7},{2,4},{3,1},{4,6},{5,3},{6,0},{7,5},{16,18},{17,23},{1... | collective-permute-start | bytes 1572872 | tf_op jit(solution)/shard_map/ppermute | solution.py:59
  24.6 3.4 %collective-permute-start.8 = (bf16[512,512]{1,0:T(8,128)(2,1)S(1)}, bf16[512,512]{1,0:T(8,128)(2,1)S(1)}, u32[]{:S(2)}, u32[]{:S(2)}) collective-permute-start(bf16[512,512]{1,0:T(8,128)(2,1)S(1)} %constant_dynamic-update-slice_fusion), channel_id=1, source_target_pairs={{0,8},{1,5},{2,10},{3,7},{4,12},{5,1},{6,14},{7,3},{16,24},{17,21}... | collective-permute-start | bytes 1572872 | tf_op jit(solution)/shard_map/ppermute | solution.py:59
  29.9 4.3 %collective-permute-done.26.refs_14_ = bf16[512,512]{1,0:T(8,128)(2,1)S(1)} collective-permute-done((bf16[512,512]{1,0:T(8,128)(2,1)S(1)}, bf16[512,512]{1,0:T(8,128)(2,1)S(1)}, u32[]{:S(2)}, u32[]{:S(2)}) %collective-permute-start.26) | collective-permute-done | bytes 524320 | tf_op jit(solution)/shard_map/ppermute | solution.py:59
  34.2 2.9 %collective-permute-done.24.refs_12_ = bf16[512,512]{1,0:T(8,128)(2,1)S(1)} collective-permute-done((bf16[512,512]{1,0:T(8,128)(2,1)S(1)}, bf16[512,512]{1,0:T(8,128)(2,1)S(1)}, u32[]{:S(2)}, u32[]{:S(2)}) %collective-permute-start.24) | collective-permute-done | bytes 524320 | tf_op jit(solution)/shard_map/ppermute | solution.py:59
  37.1 3.8 %collective-permute-start.27 = (bf16[512,512]{1,0:T(8,128)(2,1)S(1)}, bf16[512,512]{1,0:T(8,128)(2,1)S(1)}, u32[]{:S(2)}, u32[]{:S(2)}) collective-permute-start(bf16[512,512]{1,0:T(8,128)(2,1)S(1)} %collective-permute-done.26.refs_14_), channel_id=1, source_target_pairs={{0,1},{1,0},{2,3},{3,2},{4,5},{5,4},{6,7},{7,6},{16,17},{17,16},{1... | collective-permute-start | bytes 1572872 | tf_op jit(solution)/shard_map/ppermute | solution.py:59
  40.8 4.6 %collective-permute-done.10.refs_12_.refs_13_ = bf16[512,512]{1,0:T(8,128)(2,1)S(1)} collective-permute-done((bf16[512,512]{1,0:T(8,128)(2,1)S(1)}, bf16[512,512]{1,0:T(8,128)(2,1)S(1)}, u32[]{:S(2)}, u32[]{:S(2)}) %collective-permute-start.10) | collective-permute-done | bytes 524320 | tf_op jit(solution)/shard_map/ppermute | solution.py:59
  45.4 3.6 %collective-permute-start.30 = (bf16[512,512]{1,0:T(8,128)(2,1)S(1)}, bf16[512,512]{1,0:T(8,128)(2,1)S(1)}, u32[]{:S(2)}, u32[]{:S(2)}) collective-permute-start(bf16[512,512]{1,0:T(8,128)(2,1)S(1)} %collective-permute-done.24.refs_12_), channel_id=1, source_target_pairs={{0,7},{1,0},{2,1},{3,2},{4,3},{5,4},{6,5},{7,6},{16,23},{17,16},{1... | collective-permute-start | bytes 1572872 | tf_op jit(solution)/shard_map/ppermute | solution.py:59
  49.2 7.4 %collective-permute-done.42.refs_14_ = bf16[512,512]{1,0:T(8,128)(2,1)S(1)} collective-permute-done((bf16[512,512]{1,0:T(8,128)(2,1)S(1)}, bf16[512,512]{1,0:T(8,128)(2,1)S(1)}, u32[]{:S(2)}, u32[]{:S(2)}) %collective-permute-start.42) | collective-permute-done | bytes 524320 | tf_op jit(solution)/shard_map/ppermute | solution.py:59
  56.7 2.9 %collective-permute-start.12 = (bf16[512,512]{1,0:T(8,128)(2,1)S(1)}, bf16[512,512]{1,0:T(8,128)(2,1)S(1)}, u32[]{:S(2)}, u32[]{:S(2)}) collective-permute-start(bf16[512,512]{1,0:T(8,128)(2,1)S(1)} %collective-permute-done.8.refs_10_.refs_11_), channel_id=1, source_target_pairs={{0,2},{1,9},{2,4},{3,11},{4,6},{5,13},{6,0},{7,15},{16,18},{17,25}... | collective-permute-start | bytes 1572872 | tf_op jit(solution)/shard_map/ppermute | solution.py:59
  62.7 3.9 %collective-permute-done.14.refs_17_.refs_18_ = bf16[512,512]{1,0:T(8,128)(2,1)S(1)} collective-permute-done((bf16[512,512]{1,0:T(8,128)(2,1)S(1)}, bf16[512,512]{1,0:T(8,128)(2,1)S(1)}, u32[]{:S(2)}, u32[]{:S(2)}) %collective-permute-start.14) | collective-permute-done | bytes 524320 | tf_op jit(solution)/shard_map/ppermute | solution.py:59
  71.8 4.3 %collective-permute-start.25 = (bf16[512,512]{1,0:T(8,128)(2,1)S(1)}, bf16[512,512]{1,0:T(8,128)(2,1)S(1)}, u32[]{:S(2)}, u32[]{:S(2)}) collective-permute-start(bf16[512,512]{1,0:T(8,128)(2,1)S(1)} %collective-permute-done.24.refs_12_), channel_id=1, source_target_pairs={{0,1},{1,0},{2,3},{3,2},{4,5},{5,4},{6,7},{7,6},{16,17},{17,16},{1... | collective-permute-start | bytes 1572872 | tf_op jit(solution)/shard_map/ppermute | solution.py:59
  76.1 2.8 %collective-permute-start.44 = (bf16[512,512]{1,0:T(8,128)(2,1)S(1)}, bf16[512,512]{1,0:T(8,128)(2,1)S(1)}, u32[]{:S(2)}, u32[]{:S(2)}) collective-permute-start(bf16[512,512]{1,0:T(8,128)(2,1)S(1)} %collective-permute-done.40.refs_12_), channel_id=1, source_target_pairs={{0,2},{1,9},{2,4},{3,11},{4,6},{5,13},{6,0},{7,15},{16,18},{17,25}... | collective-permute-start | bytes 1572872 | tf_op jit(solution)/shard_map/ppermute | solution.py:59
  87.7 2.9 %collective-permute-done.21.refs_8_ = bf16[256,512]{1,0:T(8,128)(2,1)S(1)} collective-permute-done((bf16[256,512]{1,0:T(8,128)(2,1)S(1)}, bf16[256,512]{1,0:T(8,128)(2,1)S(1)}, u32[]{:S(2)}, u32[]{:S(2)}) %collective-permute-start.21) | collective-permute-done | bytes 262176 | tf_op jit(solution)/shard_map/ppermute | solution.py:59
  104.5 3.0 %collective-permute-start.37 = (bf16[256,512]{1,0:T(8,128)(2,1)S(1)}, bf16[256,512]{1,0:T(8,128)(2,1)S(1)}, u32[]{:S(2)}, u32[]{:S(2)}) collective-permute-start(bf16[256,512]{1,0:T(8,128)(2,1)S(1)} %shard_map.113.refs_0_.refs_1_.refs_2_), channel_id=1, source_target_pairs={{0,32},{1,33},{2,34},{3,35},{4,36},{5,37},{6,38},{7,39},{16,48},{1... | collective-permute-start | bytes 786440 | tf_op jit(solution)/shard_map/ppermute | solution.py:59
  109.1 2.8 %collective-permute-done.37.refs_7_.refs_8_ = bf16[256,512]{1,0:T(8,128)(2,1)S(1)} collective-permute-done((bf16[256,512]{1,0:T(8,128)(2,1)S(1)}, bf16[256,512]{1,0:T(8,128)(2,1)S(1)}, u32[]{:S(2)}, u32[]{:S(2)}) %collective-permute-start.37) | collective-permute-done | bytes 262176 | tf_op jit(solution)/shard_map/ppermute | solution.py:59
  113.8 2.9 %collective-permute-start.36 = (bf16[256,512]{1,0:T(8,128)(2,1)S(1)}, bf16[256,512]{1,0:T(8,128)(2,1)S(1)}, u32[]{:S(2)}, u32[]{:S(2)}) collective-permute-start(bf16[256,512]{1,0:T(8,128)(2,1)S(1)} %collective-permute-done.32.refs_2_.refs_3_), channel_id=1, source_target_pairs={{0,48},{1,49},{2,50},{3,51},{4,52},{5,53},{6,54},{7,55},{16,0},{17... | collective-permute-start | bytes 786440 | tf_op jit(solution)/shard_map/ppermute | solution.py:59
  119.3 3.5 %collective-permute-done.36.refs_6_.refs_7_ = bf16[256,512]{1,0:T(8,128)(2,1)S(1)} collective-permute-done((bf16[256,512]{1,0:T(8,128)(2,1)S(1)}, bf16[256,512]{1,0:T(8,128)(2,1)S(1)}, u32[]{:S(2)}, u32[]{:S(2)}) %collective-permute-start.36) | collective-permute-done | bytes 262176 | tf_op jit(solution)/shard_map/ppermute | solution.py:59
  125.0 4.7 %collective-permute-start.55 = (bf16[256,512]{1,0:T(8,128)(2,1)S(1)}, bf16[256,512]{1,0:T(8,128)(2,1)S(1)}, u32[]{:S(2)}, u32[]{:S(2)}) collective-permute-start(bf16[256,512]{1,0:T(8,128)(2,1)S(1)} %shard_map.115.refs_1_.refs_9_.refs_0_), channel_id=1, source_target_pairs={{0,1},{1,0},{2,3},{3,2},{4,5},{5,4},{6,7},{7,6},{16,17},{17,16},{1... | collective-permute-start | bytes 786440 | tf_op jit(solution)/shard_map/ppermute | solution.py:59
  134.7 3.6 %collective-permute-start.58 = (bf16[512,512]{1,0:T(8,128)(2,1)S(1)}, bf16[512,512]{1,0:T(8,128)(2,1)S(1)}, u32[]{:S(2)}, u32[]{:S(2)}) collective-permute-start(bf16[512,512]{1,0:T(8,128)(2,1)S(1)} %pad_maximum_fusion), channel_id=1, source_target_pairs={{0,2},{1,7},{2,4},{3,1},{4,6},{5,3},{6,0},{7,5},{16,18},{17,23},{1... | collective-permute-start | bytes 1572872 | tf_op jit(solution)/shard_map/ppermute | solution.py:59
  138.3 2.6 %collective-permute-done.56.refs_11_ = bf16[512,512]{1,0:T(8,128)(2,1)S(1)} collective-permute-done((bf16[512,512]{1,0:T(8,128)(2,1)S(1)}, bf16[512,512]{1,0:T(8,128)(2,1)S(1)}, u32[]{:S(2)}, u32[]{:S(2)}) %collective-permute-start.56) | collective-permute-done | bytes 524320 | tf_op jit(solution)/shard_map/ppermute | solution.py:59
  142.1 2.7 %collective-permute-start.60 = (bf16[512,512]{1,0:T(8,128)(2,1)S(1)}, bf16[512,512]{1,0:T(8,128)(2,1)S(1)}, u32[]{:S(2)}, u32[]{:S(2)}) collective-permute-start(bf16[512,512]{1,0:T(8,128)(2,1)S(1)} %collective-permute-done.56.refs_11_), channel_id=1, source_target_pairs={{0,2},{1,9},{2,4},{3,11},{4,6},{5,13},{6,0},{7,15},{16,18},{17,25}... | collective-permute-start | bytes 1572872 | tf_op jit(solution)/shard_map/ppermute | solution.py:59
  148.6 10.0 %collective-permute-done.48.refs_2_ = bf16[256,512]{1,0:T(8,128)(2,1)S(1)} collective-permute-done((bf16[256,512]{1,0:T(8,128)(2,1)S(1)}, bf16[256,512]{1,0:T(8,128)(2,1)S(1)}, u32[]{:S(2)}, u32[]{:S(2)}) %collective-permute-start.48) | collective-permute-done | bytes 262176 | tf_op jit(solution)/shard_map/ppermute | solution.py:59
  158.7 3.9 %collective-permute-done.54.refs_8_ = bf16[256,512]{1,0:T(8,128)(2,1)S(1)} collective-permute-done((bf16[256,512]{1,0:T(8,128)(2,1)S(1)}, bf16[256,512]{1,0:T(8,128)(2,1)S(1)}, u32[]{:S(2)}, u32[]{:S(2)}) %collective-permute-start.54) | collective-permute-done | bytes 262176 | tf_op jit(solution)/shard_map/ppermute | solution.py:59
  165.8 8.0 %collective-permute-done.51.refs_5_ = bf16[256,512]{1,0:T(8,128)(2,1)S(1)} collective-permute-done((bf16[256,512]{1,0:T(8,128)(2,1)S(1)}, bf16[256,512]{1,0:T(8,128)(2,1)S(1)}, u32[]{:S(2)}, u32[]{:S(2)}) %collective-permute-start.51) | collective-permute-done | bytes 262176 | tf_op jit(solution)/shard_map/ppermute | solution.py:59
  179.4 2.9 %collective-permute-start.67 = (bf16[512,512]{1,0:T(8,128)(2,1)S(1)}, bf16[512,512]{1,0:T(8,128)(2,1)S(1)}, u32[]{:S(2)}, u32[]{:S(2)}) collective-permute-start(bf16[512,512]{1,0:T(8,128)(2,1)S(1)} %pad_maximum_fusion.1), channel_id=1, source_target_pairs={{0,2},{1,7},{2,4},{3,1},{4,6},{5,3},{6,0},{7,5},{16,18},{17,23},{1... | collective-permute-start | bytes 1572872 | tf_op jit(solution)/shard_map/ppermute | solution.py:59
  182.3 8.5 %collective-permute-done.65.refs_11_ = bf16[512,512]{1,0:T(8,128)(2,1)S(1)} collective-permute-done((bf16[512,512]{1,0:T(8,128)(2,1)S(1)}, bf16[512,512]{1,0:T(8,128)(2,1)S(1)}, u32[]{:S(2)}, u32[]{:S(2)}) %collective-permute-start.65) | collective-permute-done | bytes 524320 | tf_op jit(solution)/shard_map/ppermute | solution.py:59
  192.9 3.0 %collective-permute-done.67.refs_13_ = bf16[512,512]{1,0:T(8,128)(2,1)S(1)} collective-permute-done((bf16[512,512]{1,0:T(8,128)(2,1)S(1)}, bf16[512,512]{1,0:T(8,128)(2,1)S(1)}, u32[]{:S(2)}, u32[]{:S(2)}) %collective-permute-start.67) | collective-permute-done | bytes 524320 | tf_op jit(solution)/shard_map/ppermute | solution.py:59
  195.9 4.8 %collective-permute-done.71.refs_18_ = bf16[512,512]{1,0:T(8,128)(2,1)S(1)} collective-permute-done((bf16[512,512]{1,0:T(8,128)(2,1)S(1)}, bf16[512,512]{1,0:T(8,128)(2,1)S(1)}, u32[]{:S(2)}, u32[]{:S(2)}) %collective-permute-start.71) | collective-permute-done | bytes 524320 | tf_op jit(solution)/shard_map/ppermute | solution.py:59
  202.7 2.5 %shard_map.114 = (bf16[256,512]{1,0:T(8,128)(2,1)}, bf16[256,512]{1,0:T(8,128)(2,1)}) custom-call(bf16[256,512]{1,0:T(8,128)(2,1)S(1)} %shard_map.113.refs_0_.refs_1_.refs_2_, bf16[256,512]{1,0:T(8,128)(2,1)S(1)} %shard_map.113.refs_0_.refs_1_.refs_2_, bf16[256,512]{1,0:T(8,128)(2,1)S(1)} %collective-permute-done.32.refs_2_.refs_3_, ...), custom_call_target="tpu_custom_call" | custom-call | tf_op jit(solution)/shard_map/pallas_call | solution.py:258
  205.3 2.5 %shard_map.117 = bf16[256,512]{1,0:T(8,128)(2,1)} custom-call(bf16[256,512]{1,0:T(8,128)(2,1)S(1)} %shard_map.115.refs_1_.refs_9_.refs_0_, bf16[256,512]{1,0:T(8,128)(2,1)S(1)} %shard_map.115.refs_1_.refs_9_.refs_0_, bf16[256,512]{1,0:T(8,128)(2,1)S(1)} %collective-permute-done.48.refs_2_, bf16[256,512]{1,0:T(8,128)(2,1)S(1)} %collective-permute-done.49.refs_3_, ...), custom_call_target="tpu_custom_call" | custom-call | tf_op jit(solution)/shard_map/pallas_call | solution.py:258
  (130 shorter events, 78.0 us)
Async XLA Ops:
  10.9 11.5 %collective-permute-start.1 = (bf16[256,512]{1,0:T(8,128)(2,1)S(1)}, bf16[256,512]{1,0:T(8,128)(2,1)S(1)}, u32[]{:S(2)}, u32[]{:S(2)}) collective-permute-start(bf16[256,512]{1,0:T(8,128)(2,1)S(1)} %get-tuple-element.12.refs_0_.refs_1_.refs_10_), channel_id=1, source_target_pairs={{0,16},{1,17},{2,18},{3,19},{4,20},{5,21},{6,22},{7,23},{16,32},{1... | collective-permute-start | bytes 786440 | tf_op jit(solution)/shard_map/ppermute | solution.py:59
  18.7 15.5 %collective-permute-start.26 = (bf16[512,512]{1,0:T(8,128)(2,1)S(1)}, bf16[512,512]{1,0:T(8,128)(2,1)S(1)}, u32[]{:S(2)}, u32[]{:S(2)}) collective-permute-start(bf16[512,512]{1,0:T(8,128)(2,1)S(1)} %constant_dynamic-update-slice_fusion.2), channel_id=1, source_target_pairs={{0,2},{1,7},{2,4},{3,1},{4,6},{5,3},{6,0},{7,5},{16,18},{17,23},{1... | collective-permute-start | bytes 1572872 | tf_op jit(solution)/shard_map/ppermute | solution.py:59
  22.5 14.6 %collective-permute-start.24 = (bf16[512,512]{1,0:T(8,128)(2,1)S(1)}, bf16[512,512]{1,0:T(8,128)(2,1)S(1)}, u32[]{:S(2)}, u32[]{:S(2)}) collective-permute-start(bf16[512,512]{1,0:T(8,128)(2,1)S(1)} %constant_dynamic-update-slice_fusion.2), channel_id=1, source_target_pairs={{0,8},{1,5},{2,10},{3,7},{4,12},{5,1},{6,14},{7,3},{16,24},{17,21}... | collective-permute-start | bytes 1572872 | tf_op jit(solution)/shard_map/ppermute | solution.py:59
  24.3 21.1 %collective-permute-start.10 = (bf16[512,512]{1,0:T(8,128)(2,1)S(1)}, bf16[512,512]{1,0:T(8,128)(2,1)S(1)}, u32[]{:S(2)}, u32[]{:S(2)}) collective-permute-start(bf16[512,512]{1,0:T(8,128)(2,1)S(1)} %constant_dynamic-update-slice_fusion), channel_id=1, source_target_pairs={{0,2},{1,7},{2,4},{3,1},{4,6},{5,3},{6,0},{7,5},{16,18},{17,23},{1... | collective-permute-start | bytes 1572872 | tf_op jit(solution)/shard_map/ppermute | solution.py:59
  24.6 24.5 %collective-permute-start.8 = (bf16[512,512]{1,0:T(8,128)(2,1)S(1)}, bf16[512,512]{1,0:T(8,128)(2,1)S(1)}, u32[]{:S(2)}, u32[]{:S(2)}) collective-permute-start(bf16[512,512]{1,0:T(8,128)(2,1)S(1)} %constant_dynamic-update-slice_fusion), channel_id=1, source_target_pairs={{0,8},{1,5},{2,10},{3,7},{4,12},{5,1},{6,14},{7,3},{16,24},{17,21}... | collective-permute-start | bytes 1572872 | tf_op jit(solution)/shard_map/ppermute | solution.py:59
  29.7 26.9 %collective-permute-start.42 = (bf16[512,512]{1,0:T(8,128)(2,1)S(1)}, bf16[512,512]{1,0:T(8,128)(2,1)S(1)}, u32[]{:S(2)}, u32[]{:S(2)}) collective-permute-start(bf16[512,512]{1,0:T(8,128)(2,1)S(1)} %constant_dynamic-update-slice_fusion.4), channel_id=1, source_target_pairs={{0,2},{1,7},{2,4},{3,1},{4,6},{5,3},{6,0},{7,5},{16,18},{17,23},{1... | collective-permute-start | bytes 1572872 | tf_op jit(solution)/shard_map/ppermute | solution.py:59
  34.2 25.4 %collective-permute-start.40 = (bf16[512,512]{1,0:T(8,128)(2,1)S(1)}, bf16[512,512]{1,0:T(8,128)(2,1)S(1)}, u32[]{:S(2)}, u32[]{:S(2)}) collective-permute-start(bf16[512,512]{1,0:T(8,128)(2,1)S(1)} %constant_dynamic-update-slice_fusion.4), channel_id=1, source_target_pairs={{0,8},{1,5},{2,10},{3,7},{4,12},{5,1},{6,14},{7,3},{16,24},{17,21}... | collective-permute-start | bytes 1572872 | tf_op jit(solution)/shard_map/ppermute | solution.py:59
  37.1 24.9 %collective-permute-start.27 = (bf16[512,512]{1,0:T(8,128)(2,1)S(1)}, bf16[512,512]{1,0:T(8,128)(2,1)S(1)}, u32[]{:S(2)}, u32[]{:S(2)}) collective-permute-start(bf16[512,512]{1,0:T(8,128)(2,1)S(1)} %collective-permute-done.26.refs_14_), channel_id=1, source_target_pairs={{0,1},{1,0},{2,3},{3,2},{4,5},{5,4},{6,7},{7,6},{16,17},{17,16},{1... | collective-permute-start | bytes 1572872 | tf_op jit(solution)/shard_map/ppermute | solution.py:59
  45.4 16.6 %collective-permute-start.30 = (bf16[512,512]{1,0:T(8,128)(2,1)S(1)}, bf16[512,512]{1,0:T(8,128)(2,1)S(1)}, u32[]{:S(2)}, u32[]{:S(2)}) collective-permute-start(bf16[512,512]{1,0:T(8,128)(2,1)S(1)} %collective-permute-done.24.refs_12_), channel_id=1, source_target_pairs={{0,7},{1,0},{2,1},{3,2},{4,3},{5,4},{6,5},{7,6},{16,23},{17,16},{1... | collective-permute-start | bytes 1572872 | tf_op jit(solution)/shard_map/ppermute | solution.py:59
  49.1 17.6 %collective-permute-start.14 = (bf16[512,512]{1,0:T(8,128)(2,1)S(1)}, bf16[512,512]{1,0:T(8,128)(2,1)S(1)}, u32[]{:S(2)}, u32[]{:S(2)}) collective-permute-start(bf16[512,512]{1,0:T(8,128)(2,1)S(1)} %collective-permute-done.8.refs_10_.refs_11_), channel_id=1, source_target_pairs={{0,7},{1,0},{2,1},{3,2},{4,3},{5,4},{6,5},{7,6},{16,23},{17,16},{1... | collective-permute-start | bytes 1572872 | tf_op jit(solution)/shard_map/ppermute | solution.py:59
  56.7 11.6 %collective-permute-start.12 = (bf16[512,512]{1,0:T(8,128)(2,1)S(1)}, bf16[512,512]{1,0:T(8,128)(2,1)S(1)}, u32[]{:S(2)}, u32[]{:S(2)}) collective-permute-start(bf16[512,512]{1,0:T(8,128)(2,1)S(1)} %collective-permute-done.8.refs_10_.refs_11_), channel_id=1, source_target_pairs={{0,2},{1,9},{2,4},{3,11},{4,6},{5,13},{6,0},{7,15},{16,18},{17,25}... | collective-permute-start | bytes 1572872 | tf_op jit(solution)/shard_map/ppermute | solution.py:59
  59.6 12.3 %collective-permute-start.28 = (bf16[512,512]{1,0:T(8,128)(2,1)S(1)}, bf16[512,512]{1,0:T(8,128)(2,1)S(1)}, u32[]{:S(2)}, u32[]{:S(2)}) collective-permute-start(bf16[512,512]{1,0:T(8,128)(2,1)S(1)} %collective-permute-done.24.refs_12_), channel_id=1, source_target_pairs={{0,2},{1,9},{2,4},{3,11},{4,6},{5,13},{6,0},{7,15},{16,18},{17,25}... | collective-permute-start | bytes 1572872 | tf_op jit(solution)/shard_map/ppermute | solution.py:59
  62.0 14.1 %collective-permute-start.11 = (bf16[512,512]{1,0:T(8,128)(2,1)S(1)}, bf16[512,512]{1,0:T(8,128)(2,1)S(1)}, u32[]{:S(2)}, u32[]{:S(2)}) collective-permute-start(bf16[512,512]{1,0:T(8,128)(2,1)S(1)} %collective-permute-done.10.refs_12_.refs_13_), channel_id=1, source_target_pairs={{0,1},{1,0},{2,3},{3,2},{4,5},{5,4},{6,7},{7,6},{16,17},{17,16},{1... | collective-permute-start | bytes 1572872 | tf_op jit(solution)/shard_map/ppermute | solution.py:59
  62.0 14.1 %collective-permute-start.9 = (bf16[512,512]{1,0:T(8,128)(2,1)S(1)}, bf16[512,512]{1,0:T(8,128)(2,1)S(1)}, u32[]{:S(2)}, u32[]{:S(2)}) collective-permute-start(bf16[512,512]{1,0:T(8,128)(2,1)S(1)} %collective-permute-done.8.refs_10_.refs_11_), channel_id=1, source_target_pairs={{0,1},{1,0},{2,3},{3,2},{4,5},{5,4},{6,7},{7,6},{16,17},{17,16},{1... | collective-permute-start | bytes 1572872 | tf_op jit(solution)/shard_map/ppermute | solution.py:59
  66.6 12.4 %collective-permute-start.15 = (bf16[512,512]{1,0:T(8,128)(2,1)S(1)}, bf16[512,512]{1,0:T(8,128)(2,1)S(1)}, u32[]{:S(2)}, u32[]{:S(2)}) collective-permute-start(bf16[512,512]{1,0:T(8,128)(2,1)S(1)} %collective-permute-done.14.refs_17_.refs_18_), channel_id=1, source_target_pairs={{0,1},{1,0},{2,3},{3,2},{4,5},{5,4},{6,7},{7,6},{16,17},{17,16},{1... | collective-permute-start | bytes 1572872 | tf_op jit(solution)/shard_map/ppermute | solution.py:59
  79.0 11.8 %collective-permute-start.29 = (bf16[512,512]{1,0:T(8,128)(2,1)S(1)}, bf16[512,512]{1,0:T(8,128)(2,1)S(1)}, u32[]{:S(2)}, u32[]{:S(2)}) collective-permute-start(bf16[512,512]{1,0:T(8,128)(2,1)S(1)} %collective-permute-done.28.refs_16_), channel_id=1, source_target_pairs={{0,1},{1,0},{2,3},{3,2},{4,5},{5,4},{6,7},{7,6},{16,17},{17,16},{1... | collective-permute-start | bytes 1572872 | tf_op jit(solution)/shard_map/ppermute | solution.py:59
  90.8 16.7 %collective-permute-start.43 = (bf16[512,512]{1,0:T(8,128)(2,1)S(1)}, bf16[512,512]{1,0:T(8,128)(2,1)S(1)}, u32[]{:S(2)}, u32[]{:S(2)}) collective-permute-start(bf16[512,512]{1,0:T(8,128)(2,1)S(1)} %collective-permute-done.42.refs_14_), channel_id=1, source_target_pairs={{0,1},{1,0},{2,3},{3,2},{4,5},{5,4},{6,7},{7,6},{16,17},{17,16},{1... | collective-permute-start | bytes 1572872 | tf_op jit(solution)/shard_map/ppermute | solution.py:59
  93.7 13.8 %collective-permute-start.41 = (bf16[512,512]{1,0:T(8,128)(2,1)S(1)}, bf16[512,512]{1,0:T(8,128)(2,1)S(1)}, u32[]{:S(2)}, u32[]{:S(2)}) collective-permute-start(bf16[512,512]{1,0:T(8,128)(2,1)S(1)} %collective-permute-done.40.refs_12_), channel_id=1, source_target_pairs={{0,1},{1,0},{2,3},{3,2},{4,5},{5,4},{6,7},{7,6},{16,17},{17,16},{1... | collective-permute-start | bytes 1572872 | tf_op jit(solution)/shard_map/ppermute | solution.py:59
  97.0 11.6 %collective-permute-start.47 = (bf16[512,512]{1,0:T(8,128)(2,1)S(1)}, bf16[512,512]{1,0:T(8,128)(2,1)S(1)}, u32[]{:S(2)}, u32[]{:S(2)}) collective-permute-start(bf16[512,512]{1,0:T(8,128)(2,1)S(1)} %collective-permute-done.46.refs_19_), channel_id=1, source_target_pairs={{0,1},{1,0},{2,3},{3,2},{4,5},{5,4},{6,7},{7,6},{16,17},{17,16},{1... | collective-permute-start | bytes 1572872 | tf_op jit(solution)/shard_map/ppermute | solution.py:59
  100.0 16.6 %collective-permute-start.45 = (bf16[512,512]{1,0:T(8,128)(2,1)S(1)}, bf16[512,512]{1,0:T(8,128)(2,1)S(1)}, u32[]{:S(2)}, u32[]{:S(2)}) collective-permute-start(bf16[512,512]{1,0:T(8,128)(2,1)S(1)} %collective-permute-done.44.refs_16_), channel_id=1, source_target_pairs={{0,1},{1,0},{2,3},{3,2},{4,5},{5,4},{6,7},{7,6},{16,17},{17,16},{1... | collective-permute-start | bytes 1572872 | tf_op jit(solution)/shard_map/ppermute | solution.py:59
  132.9 12.5 %collective-permute-start.50 = (bf16[256,512]{1,0:T(8,128)(2,1)S(1)}, bf16[256,512]{1,0:T(8,128)(2,1)S(1)}, u32[]{:S(2)}, u32[]{:S(2)}) collective-permute-start(bf16[256,512]{1,0:T(8,128)(2,1)S(1)} %shard_map.115.refs_1_.refs_9_.refs_0_), channel_id=1, source_target_pairs={{0,48},{1,49},{2,50},{3,51},{4,52},{5,53},{6,54},{7,55},{16,0},{17... | collective-permute-start | bytes 786440 | tf_op jit(solution)/shard_map/ppermute | solution.py:59
  134.7 13.2 %collective-permute-start.49 = (bf16[256,512]{1,0:T(8,128)(2,1)S(1)}, bf16[256,512]{1,0:T(8,128)(2,1)S(1)}, u32[]{:S(2)}, u32[]{:S(2)}) collective-permute-start(bf16[256,512]{1,0:T(8,128)(2,1)S(1)} %shard_map.115.refs_1_.refs_9_.refs_0_), channel_id=1, source_target_pairs={{0,16},{1,17},{2,18},{3,19},{4,20},{5,21},{6,22},{7,23},{16,32},{1... | collective-permute-start | bytes 786440 | tf_op jit(solution)/shard_map/ppermute | solution.py:59
  134.7 27.9 %collective-permute-start.58 = (bf16[512,512]{1,0:T(8,128)(2,1)S(1)}, bf16[512,512]{1,0:T(8,128)(2,1)S(1)}, u32[]{:S(2)}, u32[]{:S(2)}) collective-permute-start(bf16[512,512]{1,0:T(8,128)(2,1)S(1)} %pad_maximum_fusion), channel_id=1, source_target_pairs={{0,2},{1,7},{2,4},{3,1},{4,6},{5,3},{6,0},{7,5},{16,18},{17,23},{1... | collective-permute-start | bytes 1572872 | tf_op jit(solution)/shard_map/ppermute | solution.py:59
  140.8 22.2 %collective-permute-start.62 = (bf16[512,512]{1,0:T(8,128)(2,1)S(1)}, bf16[512,512]{1,0:T(8,128)(2,1)S(1)}, u32[]{:S(2)}, u32[]{:S(2)}) collective-permute-start(bf16[512,512]{1,0:T(8,128)(2,1)S(1)} %collective-permute-done.56.refs_11_), channel_id=1, source_target_pairs={{0,7},{1,0},{2,1},{3,2},{4,3},{5,4},{6,5},{7,6},{16,23},{17,16},{1... | collective-permute-start | bytes 1572872 | tf_op jit(solution)/shard_map/ppermute | solution.py:59
  142.1 21.1 %collective-permute-start.60 = (bf16[512,512]{1,0:T(8,128)(2,1)S(1)}, bf16[512,512]{1,0:T(8,128)(2,1)S(1)}, u32[]{:S(2)}, u32[]{:S(2)}) collective-permute-start(bf16[512,512]{1,0:T(8,128)(2,1)S(1)} %collective-permute-done.56.refs_11_), channel_id=1, source_target_pairs={{0,2},{1,9},{2,4},{3,11},{4,6},{5,13},{6,0},{7,15},{16,18},{17,25}... | collective-permute-start | bytes 1572872 | tf_op jit(solution)/shard_map/ppermute | solution.py:59
  145.5 13.2 %collective-permute-start.48 = (bf16[256,512]{1,0:T(8,128)(2,1)S(1)}, bf16[256,512]{1,0:T(8,128)(2,1)S(1)}, u32[]{:S(2)}, u32[]{:S(2)}) collective-permute-start(bf16[256,512]{1,0:T(8,128)(2,1)S(1)} %shard_map.115.refs_1_.refs_9_.refs_0_), channel_id=1, source_target_pairs={{0,64},{1,65},{2,66},{3,67},{4,68},{5,69},{6,70},{7,71},{16,80},{1... | collective-permute-start | bytes 786440 | tf_op jit(solution)/shard_map/ppermute | solution.py:59
  147.8 14.7 %collective-permute-start.54 = (bf16[256,512]{1,0:T(8,128)(2,1)S(1)}, bf16[256,512]{1,0:T(8,128)(2,1)S(1)}, u32[]{:S(2)}, u32[]{:S(2)}) collective-permute-start(bf16[256,512]{1,0:T(8,128)(2,1)S(1)} %collective-permute-done.53.refs_7_), channel_id=1, source_target_pairs={{0,64},{1,65},{2,66},{3,67},{4,68},{5,69},{6,70},{7,71},{16,80},{1... | collective-permute-start | bytes 786440 | tf_op jit(solution)/shard_map/ppermute | solution.py:59
  162.5 11.2 %collective-permute-start.57 = (bf16[512,512]{1,0:T(8,128)(2,1)S(1)}, bf16[512,512]{1,0:T(8,128)(2,1)S(1)}, u32[]{:S(2)}, u32[]{:S(2)}) collective-permute-start(bf16[512,512]{1,0:T(8,128)(2,1)S(1)} %collective-permute-done.56.refs_11_), channel_id=1, source_target_pairs={{0,1},{1,0},{2,3},{3,2},{4,5},{5,4},{6,7},{7,6},{16,17},{17,16},{1... | collective-permute-start | bytes 1572872 | tf_op jit(solution)/shard_map/ppermute | solution.py:59
  162.5 11.2 %collective-permute-start.59 = (bf16[512,512]{1,0:T(8,128)(2,1)S(1)}, bf16[512,512]{1,0:T(8,128)(2,1)S(1)}, u32[]{:S(2)}, u32[]{:S(2)}) collective-permute-start(bf16[512,512]{1,0:T(8,128)(2,1)S(1)} %collective-permute-done.58.refs_13_), channel_id=1, source_target_pairs={{0,1},{1,0},{2,3},{3,2},{4,5},{5,4},{6,7},{7,6},{16,17},{17,16},{1... | collective-permute-start | bytes 1572872 | tf_op jit(solution)/shard_map/ppermute | solution.py:59
  178.5 12.3 %collective-permute-start.65 = (bf16[512,512]{1,0:T(8,128)(2,1)S(1)}, bf16[512,512]{1,0:T(8,128)(2,1)S(1)}, u32[]{:S(2)}, u32[]{:S(2)}) collective-permute-start(bf16[512,512]{1,0:T(8,128)(2,1)S(1)} %pad_maximum_fusion.1), channel_id=1, source_target_pairs={{0,8},{1,5},{2,10},{3,7},{4,12},{5,1},{6,14},{7,3},{16,24},{17,21}... | collective-permute-start | bytes 1572872 | tf_op jit(solution)/shard_map/ppermute | solution.py:59
  179.4 16.5 %collective-permute-start.67 = (bf16[512,512]{1,0:T(8,128)(2,1)S(1)}, bf16[512,512]{1,0:T(8,128)(2,1)S(1)}, u32[]{:S(2)}, u32[]{:S(2)}) collective-permute-start(bf16[512,512]{1,0:T(8,128)(2,1)S(1)} %pad_maximum_fusion.1), channel_id=1, source_target_pairs={{0,2},{1,7},{2,4},{3,1},{4,6},{5,3},{6,0},{7,5},{16,18},{17,23},{1... | collective-permute-start | bytes 1572872 | tf_op jit(solution)/shard_map/ppermute | solution.py:59
  191.5 13.7 %collective-permute-start.66 = (bf16[512,512]{1,0:T(8,128)(2,1)S(1)}, bf16[512,512]{1,0:T(8,128)(2,1)S(1)}, u32[]{:S(2)}, u32[]{:S(2)}) collective-permute-start(bf16[512,512]{1,0:T(8,128)(2,1)S(1)} %collective-permute-done.65.refs_11_), channel_id=1, source_target_pairs={{0,1},{1,0},{2,3},{3,2},{4,5},{5,4},{6,7},{7,6},{16,17},{17,16},{1... | collective-permute-start | bytes 1572872 | tf_op jit(solution)/shard_map/ppermute | solution.py:59
  (41 other events, 346.3 us)

commit v4 on v3

--- a/solution.py
+++ b/solution.py
@@ -190,81 +190,78 @@
     )(ph, fi, fs, mu, h)
 
 
-def product_body(finish, n_extra, n_out, a_sources, b_sources, *refs):
+def product_body(finish, n_extra, n_out, a_sources, b_sources, carry, *refs):
     extras, refs = refs[:n_extra], refs[n_extra:]
     a_refs, refs = refs[: len(a_sources)], refs[len(a_sources) :]
     b_refs, refs = refs[: 2 * len(b_sources)], refs[2 * len(b_sources) :]
     outs, refs = refs[:n_out], refs[n_out:]
-    b_held, sems = refs
+    a_held, spare, sems = refs
     row, blk = place()
     core = row % 2
     xh, z = row // 8, (row // 2) % 4
     xl, y = blk // 4, blk % 4
     rows = a_refs[0].shape[0]
 
-    def start_of(bit, ring, source):
-        return (((bit + source[0]) % 2) * 4 + (ring + source[1] + 4) % 4) * (2 * rows)
+    def chunk(bit, ring, source):
+        return ((bit + source[0]) % 2) * 4 + (ring + source[1] + 4) % 4
 
     waits = []
-
-    def bring(ref, fetcher, source):
-        at = start_of(xh, z, source)
-        for k in range(ref.shape[0] // rows):
-            half = fetcher if k == 0 else 1 - fetcher
+    for ref, source in zip(a_refs, a_sources):
+        at = 2 * chunk(xl, y, source)
+        for k in range(2):
             copy = pltpu.make_async_copy(
-                ref.at[pl.ds(k * rows, rows)],
-                b_held.at[pl.ds(pl.multiple_of(at + half * rows, rows), rows)],
-                sems.at[len(waits)],
+                ref.at[:, pl.ds(k * rows, rows)], a_held.at[at + k], sems.at[len(waits)]
             )
             copy.start()
             waits.append(copy)
 
-    def bring_either(here, there, source):
-        at = start_of(xh, z, source)
-        for k in range(2):
-            target = b_held.at[pl.ds(pl.multiple_of(at + k * rows, rows), rows)]
-            for side, ref in enumerate((here, there)):
-                copy = pltpu.make_async_copy(
-                    ref.at[pl.ds(k * rows, rows)], target, sems.at[len(waits)]
-                )
-                pl.when(core == side)(copy.start)
-            waits.append(copy)
-
+    split = b_sources[-1][1] is None
+    if split:
+        for side in range(2):
+            copy = pltpu.make_async_copy(b_refs[side - 2], spare, sems.at[len(waits)])
+            pl.when(core == side)(copy.start)
+        waits.append(copy)
+    for copy in waits:
+        copy.wait()
+
+    def part(right, first_half, source):
+        at = 2 * chunk(xh, z, source)
+        left = jnp.concatenate([a_held[at + first_half], a_held[at + 1 - first_half]], 1)
+        return jnp.dot(left, right, preferred_element_type=F32)
+
+    parts = [extras[-1][...]] if carry else []
     for k, (first, second) in enumerate(b_sources):
         here, there = b_refs[2 * k], b_refs[2 * k + 1]
         if second is None:
-            bring_either(here, there, first)
+            parts.append(part(spare[...], 0, first))
+        elif here.shape[0] == rows:
+            parts.append(part(jnp.concatenate([here[...], there[...]], 0), core, first))
         else:
             one = [jnp.where(core == 0, a, b) for a, b in zip(first, second)]
             two = [jnp.where(core == 0, b, a) for a, b in zip(first, second)]
-            bring(here, core, one)
-            bring(there, 1 - core, two)
-    for copy in waits:
-        copy.wait()
-    total = None
-    for ref, source in zip(a_refs, a_sources):
-        at = pl.multiple_of(start_of(xl, y, source), 2 * rows)
-        part = jnp.dot(ref[...], b_held[pl.ds(at, 2 * rows)], preferred_element_type=F32)
-        total = part if total is None else total + part
+            parts.append(part(here[...], core, one))
+            parts.append(part(there[...], 1 - core, two))
+    total = functools.reduce(lambda a, b: a + b, parts)
     finish(row, blk, total, extras, outs)
 
 
-def product(finish, a, b, extras=(), n_out=1):
+def product(finish, a, b, extras=(), n_out=1, kind=BF, carry=False):
     rows, cols = a[0][0].shape
-    out = jax.ShapeDtypeStruct((rows, cols), BF)
+    out = jax.ShapeDtypeStruct((rows, cols), kind)
     a_sources = [source for _, source in a]
     b_sources = [one[2:] for one in b]
     b_arrays = [array for one in b for array in one[:2]]
     got = pl.pallas_call(
         functools.partial(
-            product_body, finish, len(extras), n_out, a_sources, b_sources
+            product_body, finish, len(extras), n_out, a_sources, b_sources, carry
         ),
         out_shape=[out] * n_out,
         in_specs=[VMEM] * (len(extras) + len(a) + len(b_arrays)),
         out_specs=[VMEM] * n_out,
         scratch_shapes=[
-            pltpu.VMEM((16 * rows, cols), BF),
-            pltpu.SemaphoreType.DMA((16,)),
+            pltpu.VMEM((16, rows, cols // 2), BF),
+            pltpu.VMEM((2 * rows, cols), BF),
+            pltpu.SemaphoreType.DMA((17,)),
         ],
         compiler_params=pltpu.CompilerParams(vmem_limit_bytes=VMEM_LIMIT),
     )(*extras, *[one[0] for one in a], *b_arrays)
@@ -273,6 +270,10 @@
 
 def end_first(row, blk, total, extras, outs):
     outs[0][...] = total.astype(BF)
+
+
+def end_early(row, blk, total, extras, outs):
+    outs[0][...] = total
 
 
 def end_refined(row, blk, total, extras, outs):
@@ -317,7 +318,8 @@
     error, refined = product(end_error, r_rows, s_cols, (refined,), 2)
     square = product(end_square, x_rows, x_cols, (keep_sign,))
     q_cols = gather_cols(square)
-    sign = product(end_sign, x_rows, q_cols, (shifted,))
+    partial = product(end_early, x_rows, q_cols[:3], kind=F32)
+    sign = product(end_sign, x_rows, q_cols[3:], (shifted, partial), carry=True)
     return refined, error, sign
 
 

time: 208 us -> 208 us (level)
    pallas_call x6 -> x7, Pallas kernels: 12.5 us -> 12.3 us  [product(): pl.pallas_call(functools.partial(product_body, finish, len(extras), n_out...]
where the time goes in v4:
time: 208 us
  starting transfers between devices  96.5 us (46%)
  waiting for transfers between devices  93.9 us (45%)
  Pallas kernels  15.3 us (7%)
    ppermute x73, starting transfers between devices, send(): return lax.ppermute(array, AXES, pairs)  96.5 us
    ppermute x73, waiting for transfers between devices, send(): return lax.ppermute(array, AXES, pairs)  93.9 us
    pallas_call x7, Pallas kernels, product(): pl.pallas_call(functools.partial(product_body, finish, len(extras), n_out...  12.3 us
  transfers between devices with their start and end apart: 73, of which 33 were waited for; matrix products, arithmetic and copies ran while one was open for 0% of the time, Pallas kernels for 4%

profile of v4, /device:TPU:1, one launch (start us, length us, event | category | flops | bytes accessed | tf_op | source)
XLA Modules:
  0.0 207.6 jit_solution(9320827197623030474)
XLA Ops:
  3.6 3.0 %collective-permute-start.5 = (bf16[256,512]{1,0:T(8,128)(2,1)S(1)}, bf16[256,512]{1,0:T(8,128)(2,1)S(1)}, u32[]{:S(2)}, u32[]{:S(2)}) collective-permute-start(bf16[256,512]{1,0:T(8,128)(2,1)S(1)} %get-tuple-element.12.refs_0_.refs_1_.refs_10_), channel_id=1, source_target_pairs={{0,32},{1,33},{2,34},{3,35},{4,36},{5,37},{6,38},{7,39},{16,48},{1... | collective-permute-start | bytes 786440 | tf_op jit(solution)/shard_map/ppermute | solution.py:59
  13.9 2.8 %collective-permute-start.4 = (bf16[256,512]{1,0:T(8,128)(2,1)S(1)}, bf16[256,512]{1,0:T(8,128)(2,1)S(1)}, u32[]{:S(2)}, u32[]{:S(2)}) collective-permute-start(bf16[256,512]{1,0:T(8,128)(2,1)S(1)} %collective-permute-done.refs_1_), channel_id=1, source_target_pairs={{0,48},{1,49},{2,50},{3,51},{4,52},{5,53},{6,54},{7,55},{16,0},{17... | collective-permute-start | bytes 786440 | tf_op jit(solution)/shard_map/ppermute | solution.py:59
  18.7 3.8 %collective-permute-start.26 = (bf16[512,512]{1,0:T(8,128)(2,1)S(1)}, bf16[512,512]{1,0:T(8,128)(2,1)S(1)}, u32[]{:S(2)}, u32[]{:S(2)}) collective-permute-start(bf16[512,512]{1,0:T(8,128)(2,1)S(1)} %constant_dynamic-update-slice_fusion.2), channel_id=1, source_target_pairs={{0,2},{1,7},{2,4},{3,1},{4,6},{5,3},{6,0},{7,5},{16,18},{17,23},{1... | collective-permute-start | bytes 1572872 | tf_op jit(solution)/shard_map/ppermute | solution.py:59
  24.6 3.4 %collective-permute-start.8 = (bf16[512,512]{1,0:T(8,128)(2,1)S(1)}, bf16[512,512]{1,0:T(8,128)(2,1)S(1)}, u32[]{:S(2)}, u32[]{:S(2)}) collective-permute-start(bf16[512,512]{1,0:T(8,128)(2,1)S(1)} %constant_dynamic-update-slice_fusion), channel_id=1, source_target_pairs={{0,8},{1,5},{2,10},{3,7},{4,12},{5,1},{6,14},{7,3},{16,24},{17,21}... | collective-permute-start | bytes 1572872 | tf_op jit(solution)/shard_map/ppermute | solution.py:59
  29.9 4.3 %collective-permute-done.26.refs_14_ = bf16[512,512]{1,0:T(8,128)(2,1)S(1)} collective-permute-done((bf16[512,512]{1,0:T(8,128)(2,1)S(1)}, bf16[512,512]{1,0:T(8,128)(2,1)S(1)}, u32[]{:S(2)}, u32[]{:S(2)}) %collective-permute-start.26) | collective-permute-done | bytes 524320 | tf_op jit(solution)/shard_map/ppermute | solution.py:59
  34.2 2.9 %collective-permute-done.24.refs_12_ = bf16[512,512]{1,0:T(8,128)(2,1)S(1)} collective-permute-done((bf16[512,512]{1,0:T(8,128)(2,1)S(1)}, bf16[512,512]{1,0:T(8,128)(2,1)S(1)}, u32[]{:S(2)}, u32[]{:S(2)}) %collective-permute-start.24) | collective-permute-done | bytes 524320 | tf_op jit(solution)/shard_map/ppermute | solution.py:59
  37.1 3.8 %collective-permute-start.27 = (bf16[512,512]{1,0:T(8,128)(2,1)S(1)}, bf16[512,512]{1,0:T(8,128)(2,1)S(1)}, u32[]{:S(2)}, u32[]{:S(2)}) collective-permute-start(bf16[512,512]{1,0:T(8,128)(2,1)S(1)} %collective-permute-done.26.refs_14_), channel_id=1, source_target_pairs={{0,1},{1,0},{2,3},{3,2},{4,5},{5,4},{6,7},{7,6},{16,17},{17,16},{1... | collective-permute-start | bytes 1572872 | tf_op jit(solution)/shard_map/ppermute | solution.py:59
  40.8 4.6 %collective-permute-done.10.refs_12_.refs_13_ = bf16[512,512]{1,0:T(8,128)(2,1)S(1)} collective-permute-done((bf16[512,512]{1,0:T(8,128)(2,1)S(1)}, bf16[512,512]{1,0:T(8,128)(2,1)S(1)}, u32[]{:S(2)}, u32[]{:S(2)}) %collective-permute-start.10) | collective-permute-done | bytes 524320 | tf_op jit(solution)/shard_map/ppermute | solution.py:59
  45.4 3.6 %collective-permute-start.30 = (bf16[512,512]{1,0:T(8,128)(2,1)S(1)}, bf16[512,512]{1,0:T(8,128)(2,1)S(1)}, u32[]{:S(2)}, u32[]{:S(2)}) collective-permute-start(bf16[512,512]{1,0:T(8,128)(2,1)S(1)} %collective-permute-done.24.refs_12_), channel_id=1, source_target_pairs={{0,7},{1,0},{2,1},{3,2},{4,3},{5,4},{6,5},{7,6},{16,23},{17,16},{1... | collective-permute-start | bytes 1572872 | tf_op jit(solution)/shard_map/ppermute | solution.py:59
  49.2 7.4 %collective-permute-done.42.refs_14_ = bf16[512,512]{1,0:T(8,128)(2,1)S(1)} collective-permute-done((bf16[512,512]{1,0:T(8,128)(2,1)S(1)}, bf16[512,512]{1,0:T(8,128)(2,1)S(1)}, u32[]{:S(2)}, u32[]{:S(2)}) %collective-permute-start.42) | collective-permute-done | bytes 524320 | tf_op jit(solution)/shard_map/ppermute | solution.py:59
  56.7 2.9 %collective-permute-start.12 = (bf16[512,512]{1,0:T(8,128)(2,1)S(1)}, bf16[512,512]{1,0:T(8,128)(2,1)S(1)}, u32[]{:S(2)}, u32[]{:S(2)}) collective-permute-start(bf16[512,512]{1,0:T(8,128)(2,1)S(1)} %collective-permute-done.8.refs_10_.refs_11_), channel_id=1, source_target_pairs={{0,2},{1,9},{2,4},{3,11},{4,6},{5,13},{6,0},{7,15},{16,18},{17,25}... | collective-permute-start | bytes 1572872 | tf_op jit(solution)/shard_map/ppermute | solution.py:59
  59.6 2.5 %collective-permute-start.28 = (bf16[512,512]{1,0:T(8,128)(2,1)S(1)}, bf16[512,512]{1,0:T(8,128)(2,1)S(1)}, u32[]{:S(2)}, u32[]{:S(2)}) collective-permute-start(bf16[512,512]{1,0:T(8,128)(2,1)S(1)} %collective-permute-done.24.refs_12_), channel_id=1, source_target_pairs={{0,2},{1,9},{2,4},{3,11},{4,6},{5,13},{6,0},{7,15},{16,18},{17,25}... | collective-permute-start | bytes 1572872 | tf_op jit(solution)/shard_map/ppermute | solution.py:59
  62.7 3.9 %collective-permute-done.14.refs_17_.refs_18_ = bf16[512,512]{1,0:T(8,128)(2,1)S(1)} collective-permute-done((bf16[512,512]{1,0:T(8,128)(2,1)S(1)}, bf16[512,512]{1,0:T(8,128)(2,1)S(1)}, u32[]{:S(2)}, u32[]{:S(2)}) %collective-permute-start.14) | collective-permute-done | bytes 524320 | tf_op jit(solution)/shard_map/ppermute | solution.py:59
  71.8 4.3 %collective-permute-start.25 = (bf16[512,512]{1,0:T(8,128)(2,1)S(1)}, bf16[512,512]{1,0:T(8,128)(2,1)S(1)}, u32[]{:S(2)}, u32[]{:S(2)}) collective-permute-start(bf16[512,512]{1,0:T(8,128)(2,1)S(1)} %collective-permute-done.24.refs_12_), channel_id=1, source_target_pairs={{0,1},{1,0},{2,3},{3,2},{4,5},{5,4},{6,7},{7,6},{16,17},{17,16},{1... | collective-permute-start | bytes 1572872 | tf_op jit(solution)/shard_map/ppermute | solution.py:59
  76.1 2.8 %collective-permute-start.44 = (bf16[512,512]{1,0:T(8,128)(2,1)S(1)}, bf16[512,512]{1,0:T(8,128)(2,1)S(1)}, u32[]{:S(2)}, u32[]{:S(2)}) collective-permute-start(bf16[512,512]{1,0:T(8,128)(2,1)S(1)} %collective-permute-done.40.refs_12_), channel_id=1, source_target_pairs={{0,2},{1,9},{2,4},{3,11},{4,6},{5,13},{6,0},{7,15},{16,18},{17,25}... | collective-permute-start | bytes 1572872 | tf_op jit(solution)/shard_map/ppermute | solution.py:59
  87.7 2.8 %collective-permute-done.21.refs_8_ = bf16[256,512]{1,0:T(8,128)(2,1)S(1)} collective-permute-done((bf16[256,512]{1,0:T(8,128)(2,1)S(1)}, bf16[256,512]{1,0:T(8,128)(2,1)S(1)}, u32[]{:S(2)}, u32[]{:S(2)}) %collective-permute-start.21) | collective-permute-done | bytes 262176 | tf_op jit(solution)/shard_map/ppermute | solution.py:59
  96.9 2.3 %collective-permute-start.47 = (bf16[512,512]{1,0:T(8,128)(2,1)S(1)}, bf16[512,512]{1,0:T(8,128)(2,1)S(1)}, u32[]{:S(2)}, u32[]{:S(2)}) collective-permute-start(bf16[512,512]{1,0:T(8,128)(2,1)S(1)} %collective-permute-done.46.refs_19_), channel_id=1, source_target_pairs={{0,1},{1,0},{2,3},{3,2},{4,5},{5,4},{6,7},{7,6},{16,17},{17,16},{1... | collective-permute-start | bytes 1572872 | tf_op jit(solution)/shard_map/ppermute | solution.py:59
  104.1 3.1 %collective-permute-start.37 = (bf16[256,512]{1,0:T(8,128)(2,1)S(1)}, bf16[256,512]{1,0:T(8,128)(2,1)S(1)}, u32[]{:S(2)}, u32[]{:S(2)}) collective-permute-start(bf16[256,512]{1,0:T(8,128)(2,1)S(1)} %shard_map.113.refs_0_.refs_1_.refs_2_), channel_id=1, source_target_pairs={{0,32},{1,33},{2,34},{3,35},{4,36},{5,37},{6,38},{7,39},{16,48},{1... | collective-permute-start | bytes 786440 | tf_op jit(solution)/shard_map/ppermute | solution.py:59
  108.8 2.8 %collective-permute-done.37.refs_7_.refs_8_ = bf16[256,512]{1,0:T(8,128)(2,1)S(1)} collective-permute-done((bf16[256,512]{1,0:T(8,128)(2,1)S(1)}, bf16[256,512]{1,0:T(8,128)(2,1)S(1)}, u32[]{:S(2)}, u32[]{:S(2)}) %collective-permute-start.37) | collective-permute-done | bytes 262176 | tf_op jit(solution)/shard_map/ppermute | solution.py:59
  113.5 2.9 %collective-permute-start.36 = (bf16[256,512]{1,0:T(8,128)(2,1)S(1)}, bf16[256,512]{1,0:T(8,128)(2,1)S(1)}, u32[]{:S(2)}, u32[]{:S(2)}) collective-permute-start(bf16[256,512]{1,0:T(8,128)(2,1)S(1)} %collective-permute-done.32.refs_2_.refs_3_), channel_id=1, source_target_pairs={{0,48},{1,49},{2,50},{3,51},{4,52},{5,53},{6,54},{7,55},{16,0},{17... | collective-permute-start | bytes 786440 | tf_op jit(solution)/shard_map/ppermute | solution.py:59
  119.0 4.0 %collective-permute-done.36.refs_6_.refs_7_ = bf16[256,512]{1,0:T(8,128)(2,1)S(1)} collective-permute-done((bf16[256,512]{1,0:T(8,128)(2,1)S(1)}, bf16[256,512]{1,0:T(8,128)(2,1)S(1)}, u32[]{:S(2)}, u32[]{:S(2)}) %collective-permute-start.36) | collective-permute-done | bytes 262176 | tf_op jit(solution)/shard_map/ppermute | solution.py:59
  124.7 4.6 %collective-permute-start.55 = (bf16[256,512]{1,0:T(8,128)(2,1)S(1)}, bf16[256,512]{1,0:T(8,128)(2,1)S(1)}, u32[]{:S(2)}, u32[]{:S(2)}) collective-permute-start(bf16[256,512]{1,0:T(8,128)(2,1)S(1)} %shard_map.115.refs_1_.refs_9_.refs_0_.refs_2_), channel_id=1, source_target_pairs={{0,1},{1,0},{2,3},{3,2},{4,5},{5,4},{6,7},{7,6},{16,17},{17,16},{1... | collective-permute-start | bytes 786440 | tf_op jit(solution)/shard_map/ppermute | solution.py:59
  134.3 3.7 %collective-permute-start.58 = (bf16[512,512]{1,0:T(8,128)(2,1)S(1)}, bf16[512,512]{1,0:T(8,128)(2,1)S(1)}, u32[]{:S(2)}, u32[]{:S(2)}) collective-permute-start(bf16[512,512]{1,0:T(8,128)(2,1)S(1)} %pad_maximum_fusion), channel_id=1, source_target_pairs={{0,2},{1,7},{2,4},{3,1},{4,6},{5,3},{6,0},{7,5},{16,18},{17,23},{1... | collective-permute-start | bytes 1572872 | tf_op jit(solution)/shard_map/ppermute | solution.py:59
  138.0 2.4 %collective-permute-done.56.refs_11_ = bf16[512,512]{1,0:T(8,128)(2,1)S(1)} collective-permute-done((bf16[512,512]{1,0:T(8,128)(2,1)S(1)}, bf16[512,512]{1,0:T(8,128)(2,1)S(1)}, u32[]{:S(2)}, u32[]{:S(2)}) %collective-permute-start.56) | collective-permute-done | bytes 524320 | tf_op jit(solution)/shard_map/ppermute | solution.py:59
  141.7 2.9 %collective-permute-start.60 = (bf16[512,512]{1,0:T(8,128)(2,1)S(1)}, bf16[512,512]{1,0:T(8,128)(2,1)S(1)}, u32[]{:S(2)}, u32[]{:S(2)}) collective-permute-start(bf16[512,512]{1,0:T(8,128)(2,1)S(1)} %collective-permute-done.56.refs_11_), channel_id=1, source_target_pairs={{0,2},{1,9},{2,4},{3,11},{4,6},{5,13},{6,0},{7,15},{16,18},{17,25}... | collective-permute-start | bytes 1572872 | tf_op jit(solution)/shard_map/ppermute | solution.py:59
  148.2 10.2 %collective-permute-done.48.refs_2_.refs_1_.refs_3_ = bf16[256,512]{1,0:T(8,128)(2,1)S(1)} collective-permute-done((bf16[256,512]{1,0:T(8,128)(2,1)S(1)}, bf16[256,512]{1,0:T(8,128)(2,1)S(1)}, u32[]{:S(2)}, u32[]{:S(2)}) %collective-permute-start.48) | collective-permute-done | bytes 262176 | tf_op jit(solution)/shard_map/ppermute | solution.py:59
  158.4 3.7 %collective-permute-done.54.refs_8_.refs_7_.refs_9_ = bf16[256,512]{1,0:T(8,128)(2,1)S(1)} collective-permute-done((bf16[256,512]{1,0:T(8,128)(2,1)S(1)}, bf16[256,512]{1,0:T(8,128)(2,1)S(1)}, u32[]{:S(2)}, u32[]{:S(2)}) %collective-permute-start.54) | collective-permute-done | bytes 262176 | tf_op jit(solution)/shard_map/ppermute | solution.py:59
  165.5 8.3 %collective-permute-done.51.refs_5_.refs_4_.refs_6_ = bf16[256,512]{1,0:T(8,128)(2,1)S(1)} collective-permute-done((bf16[256,512]{1,0:T(8,128)(2,1)S(1)}, bf16[256,512]{1,0:T(8,128)(2,1)S(1)}, u32[]{:S(2)}, u32[]{:S(2)}) %collective-permute-start.51) | collective-permute-done | bytes 262176 | tf_op jit(solution)/shard_map/ppermute | solution.py:59
  179.3 2.6 %collective-permute-start.67 = (bf16[512,512]{1,0:T(8,128)(2,1)S(1)}, bf16[512,512]{1,0:T(8,128)(2,1)S(1)}, u32[]{:S(2)}, u32[]{:S(2)}) collective-permute-start(bf16[512,512]{1,0:T(8,128)(2,1)S(1)} %pad_maximum_fusion.1), channel_id=1, source_target_pairs={{0,2},{1,7},{2,4},{3,1},{4,6},{5,3},{6,0},{7,5},{16,18},{17,23},{1... | collective-permute-start | bytes 1572872 | tf_op jit(solution)/shard_map/ppermute | solution.py:59
  181.9 8.7 %collective-permute-done.65.refs_10_ = bf16[512,512]{1,0:T(8,128)(2,1)S(1)} collective-permute-done((bf16[512,512]{1,0:T(8,128)(2,1)S(1)}, bf16[512,512]{1,0:T(8,128)(2,1)S(1)}, u32[]{:S(2)}, u32[]{:S(2)}) %collective-permute-start.65) | collective-permute-done | bytes 524320 | tf_op jit(solution)/shard_map/ppermute | solution.py:59
  194.6 5.4 %collective-permute-done.71.refs_13_ = bf16[512,512]{1,0:T(8,128)(2,1)S(1)} collective-permute-done((bf16[512,512]{1,0:T(8,128)(2,1)S(1)}, bf16[512,512]{1,0:T(8,128)(2,1)S(1)}, u32[]{:S(2)}, u32[]{:S(2)}) %collective-permute-start.71) | collective-permute-done | bytes 524320 | tf_op jit(solution)/shard_map/ppermute | solution.py:59
  202.0 2.4 %shard_map.114 = (bf16[256,512]{1,0:T(8,128)(2,1)}, bf16[256,512]{1,0:T(8,128)(2,1)}) custom-call(bf16[256,512]{1,0:T(8,128)(2,1)S(1)} %shard_map.113.refs_0_.refs_1_.refs_2_, bf16[256,512]{1,0:T(8,128)(2,1)S(1)} %shard_map.113.refs_0_.refs_1_.refs_2_, bf16[256,512]{1,0:T(8,128)(2,1)S(1)} %collective-permute-done.32.refs_2_.refs_3_, ...), custom_call_target="tpu_custom_call" | custom-call | tf_op jit(solution)/shard_map/pallas_call | solution.py:254
  (131 shorter events, 77.2 us)
Async XLA Ops:
  10.9 11.5 %collective-permute-start.1 = (bf16[256,512]{1,0:T(8,128)(2,1)S(1)}, bf16[256,512]{1,0:T(8,128)(2,1)S(1)}, u32[]{:S(2)}, u32[]{:S(2)}) collective-permute-start(bf16[256,512]{1,0:T(8,128)(2,1)S(1)} %get-tuple-element.12.refs_0_.refs_1_.refs_10_), channel_id=1, source_target_pairs={{0,16},{1,17},{2,18},{3,19},{4,20},{5,21},{6,22},{7,23},{16,32},{1... | collective-permute-start | bytes 786440 | tf_op jit(solution)/shard_map/ppermute | solution.py:59
  18.7 15.5 %collective-permute-start.26 = (bf16[512,512]{1,0:T(8,128)(2,1)S(1)}, bf16[512,512]{1,0:T(8,128)(2,1)S(1)}, u32[]{:S(2)}, u32[]{:S(2)}) collective-permute-start(bf16[512,512]{1,0:T(8,128)(2,1)S(1)} %constant_dynamic-update-slice_fusion.2), channel_id=1, source_target_pairs={{0,2},{1,7},{2,4},{3,1},{4,6},{5,3},{6,0},{7,5},{16,18},{17,23},{1... | collective-permute-start | bytes 1572872 | tf_op jit(solution)/shard_map/ppermute | solution.py:59
  22.5 14.6 %collective-permute-start.24 = (bf16[512,512]{1,0:T(8,128)(2,1)S(1)}, bf16[512,512]{1,0:T(8,128)(2,1)S(1)}, u32[]{:S(2)}, u32[]{:S(2)}) collective-permute-start(bf16[512,512]{1,0:T(8,128)(2,1)S(1)} %constant_dynamic-update-slice_fusion.2), channel_id=1, source_target_pairs={{0,8},{1,5},{2,10},{3,7},{4,12},{5,1},{6,14},{7,3},{16,24},{17,21}... | collective-permute-start | bytes 1572872 | tf_op jit(solution)/shard_map/ppermute | solution.py:59
  24.3 21.1 %collective-permute-start.10 = (bf16[512,512]{1,0:T(8,128)(2,1)S(1)}, bf16[512,512]{1,0:T(8,128)(2,1)S(1)}, u32[]{:S(2)}, u32[]{:S(2)}) collective-permute-start(bf16[512,512]{1,0:T(8,128)(2,1)S(1)} %constant_dynamic-update-slice_fusion), channel_id=1, source_target_pairs={{0,2},{1,7},{2,4},{3,1},{4,6},{5,3},{6,0},{7,5},{16,18},{17,23},{1... | collective-permute-start | bytes 1572872 | tf_op jit(solution)/shard_map/ppermute | solution.py:59
  24.6 24.5 %collective-permute-start.8 = (bf16[512,512]{1,0:T(8,128)(2,1)S(1)}, bf16[512,512]{1,0:T(8,128)(2,1)S(1)}, u32[]{:S(2)}, u32[]{:S(2)}) collective-permute-start(bf16[512,512]{1,0:T(8,128)(2,1)S(1)} %constant_dynamic-update-slice_fusion), channel_id=1, source_target_pairs={{0,8},{1,5},{2,10},{3,7},{4,12},{5,1},{6,14},{7,3},{16,24},{17,21}... | collective-permute-start | bytes 1572872 | tf_op jit(solution)/shard_map/ppermute | solution.py:59
  29.7 26.9 %collective-permute-start.42 = (bf16[512,512]{1,0:T(8,128)(2,1)S(1)}, bf16[512,512]{1,0:T(8,128)(2,1)S(1)}, u32[]{:S(2)}, u32[]{:S(2)}) collective-permute-start(bf16[512,512]{1,0:T(8,128)(2,1)S(1)} %constant_dynamic-update-slice_fusion.4), channel_id=1, source_target_pairs={{0,2},{1,7},{2,4},{3,1},{4,6},{5,3},{6,0},{7,5},{16,18},{17,23},{1... | collective-permute-start | bytes 1572872 | tf_op jit(solution)/shard_map/ppermute | solution.py:59
  34.2 25.4 %collective-permute-start.40 = (bf16[512,512]{1,0:T(8,128)(2,1)S(1)}, bf16[512,512]{1,0:T(8,128)(2,1)S(1)}, u32[]{:S(2)}, u32[]{:S(2)}) collective-permute-start(bf16[512,512]{1,0:T(8,128)(2,1)S(1)} %constant_dynamic-update-slice_fusion.4), channel_id=1, source_target_pairs={{0,8},{1,5},{2,10},{3,7},{4,12},{5,1},{6,14},{7,3},{16,24},{17,21}... | collective-permute-start | bytes 1572872 | tf_op jit(solution)/shard_map/ppermute | solution.py:59
  37.1 24.9 %collective-permute-start.27 = (bf16[512,512]{1,0:T(8,128)(2,1)S(1)}, bf16[512,512]{1,0:T(8,128)(2,1)S(1)}, u32[]{:S(2)}, u32[]{:S(2)}) collective-permute-start(bf16[512,512]{1,0:T(8,128)(2,1)S(1)} %collective-permute-done.26.refs_14_), channel_id=1, source_target_pairs={{0,1},{1,0},{2,3},{3,2},{4,5},{5,4},{6,7},{7,6},{16,17},{17,16},{1... | collective-permute-start | bytes 1572872 | tf_op jit(solution)/shard_map/ppermute | solution.py:59
  45.4 16.6 %collective-permute-start.30 = (bf16[512,512]{1,0:T(8,128)(2,1)S(1)}, bf16[512,512]{1,0:T(8,128)(2,1)S(1)}, u32[]{:S(2)}, u32[]{:S(2)}) collective-permute-start(bf16[512,512]{1,0:T(8,128)(2,1)S(1)} %collective-permute-done.24.refs_12_), channel_id=1, source_target_pairs={{0,7},{1,0},{2,1},{3,2},{4,3},{5,4},{6,5},{7,6},{16,23},{17,16},{1... | collective-permute-start | bytes 1572872 | tf_op jit(solution)/shard_map/ppermute | solution.py:59
  49.1 17.6 %collective-permute-start.14 = (bf16[512,512]{1,0:T(8,128)(2,1)S(1)}, bf16[512,512]{1,0:T(8,128)(2,1)S(1)}, u32[]{:S(2)}, u32[]{:S(2)}) collective-permute-start(bf16[512,512]{1,0:T(8,128)(2,1)S(1)} %collective-permute-done.8.refs_10_.refs_11_), channel_id=1, source_target_pairs={{0,7},{1,0},{2,1},{3,2},{4,3},{5,4},{6,5},{7,6},{16,23},{17,16},{1... | collective-permute-start | bytes 1572872 | tf_op jit(solution)/shard_map/ppermute | solution.py:59
  56.7 11.6 %collective-permute-start.12 = (bf16[512,512]{1,0:T(8,128)(2,1)S(1)}, bf16[512,512]{1,0:T(8,128)(2,1)S(1)}, u32[]{:S(2)}, u32[]{:S(2)}) collective-permute-start(bf16[512,512]{1,0:T(8,128)(2,1)S(1)} %collective-permute-done.8.refs_10_.refs_11_), channel_id=1, source_target_pairs={{0,2},{1,9},{2,4},{3,11},{4,6},{5,13},{6,0},{7,15},{16,18},{17,25}... | collective-permute-start | bytes 1572872 | tf_op jit(solution)/shard_map/ppermute | solution.py:59
  59.6 12.3 %collective-permute-start.28 = (bf16[512,512]{1,0:T(8,128)(2,1)S(1)}, bf16[512,512]{1,0:T(8,128)(2,1)S(1)}, u32[]{:S(2)}, u32[]{:S(2)}) collective-permute-start(bf16[512,512]{1,0:T(8,128)(2,1)S(1)} %collective-permute-done.24.refs_12_), channel_id=1, source_target_pairs={{0,2},{1,9},{2,4},{3,11},{4,6},{5,13},{6,0},{7,15},{16,18},{17,25}... | collective-permute-start | bytes 1572872 | tf_op jit(solution)/shard_map/ppermute | solution.py:59
  62.0 14.1 %collective-permute-start.11 = (bf16[512,512]{1,0:T(8,128)(2,1)S(1)}, bf16[512,512]{1,0:T(8,128)(2,1)S(1)}, u32[]{:S(2)}, u32[]{:S(2)}) collective-permute-start(bf16[512,512]{1,0:T(8,128)(2,1)S(1)} %collective-permute-done.10.refs_12_.refs_13_), channel_id=1, source_target_pairs={{0,1},{1,0},{2,3},{3,2},{4,5},{5,4},{6,7},{7,6},{16,17},{17,16},{1... | collective-permute-start | bytes 1572872 | tf_op jit(solution)/shard_map/ppermute | solution.py:59
  62.0 14.1 %collective-permute-start.9 = (bf16[512,512]{1,0:T(8,128)(2,1)S(1)}, bf16[512,512]{1,0:T(8,128)(2,1)S(1)}, u32[]{:S(2)}, u32[]{:S(2)}) collective-permute-start(bf16[512,512]{1,0:T(8,128)(2,1)S(1)} %collective-permute-done.8.refs_10_.refs_11_), channel_id=1, source_target_pairs={{0,1},{1,0},{2,3},{3,2},{4,5},{5,4},{6,7},{7,6},{16,17},{17,16},{1... | collective-permute-start | bytes 1572872 | tf_op jit(solution)/shard_map/ppermute | solution.py:59
  66.6 12.4 %collective-permute-start.15 = (bf16[512,512]{1,0:T(8,128)(2,1)S(1)}, bf16[512,512]{1,0:T(8,128)(2,1)S(1)}, u32[]{:S(2)}, u32[]{:S(2)}) collective-permute-start(bf16[512,512]{1,0:T(8,128)(2,1)S(1)} %collective-permute-done.14.refs_17_.refs_18_), channel_id=1, source_target_pairs={{0,1},{1,0},{2,3},{3,2},{4,5},{5,4},{6,7},{7,6},{16,17},{17,16},{1... | collective-permute-start | bytes 1572872 | tf_op jit(solution)/shard_map/ppermute | solution.py:59
  79.0 11.7 %collective-permute-start.29 = (bf16[512,512]{1,0:T(8,128)(2,1)S(1)}, bf16[512,512]{1,0:T(8,128)(2,1)S(1)}, u32[]{:S(2)}, u32[]{:S(2)}) collective-permute-start(bf16[512,512]{1,0:T(8,128)(2,1)S(1)} %collective-permute-done.28.refs_16_), channel_id=1, source_target_pairs={{0,1},{1,0},{2,3},{3,2},{4,5},{5,4},{6,7},{7,6},{16,17},{17,16},{1... | collective-permute-start | bytes 1572872 | tf_op jit(solution)/shard_map/ppermute | solution.py:59
  90.7 16.6 %collective-permute-start.43 = (bf16[512,512]{1,0:T(8,128)(2,1)S(1)}, bf16[512,512]{1,0:T(8,128)(2,1)S(1)}, u32[]{:S(2)}, u32[]{:S(2)}) collective-permute-start(bf16[512,512]{1,0:T(8,128)(2,1)S(1)} %collective-permute-done.42.refs_14_), channel_id=1, source_target_pairs={{0,1},{1,0},{2,3},{3,2},{4,5},{5,4},{6,7},{7,6},{16,17},{17,16},{1... | collective-permute-start | bytes 1572872 | tf_op jit(solution)/shard_map/ppermute | solution.py:59
  93.7 13.6 %collective-permute-start.41 = (bf16[512,512]{1,0:T(8,128)(2,1)S(1)}, bf16[512,512]{1,0:T(8,128)(2,1)S(1)}, u32[]{:S(2)}, u32[]{:S(2)}) collective-permute-start(bf16[512,512]{1,0:T(8,128)(2,1)S(1)} %collective-permute-done.40.refs_12_), channel_id=1, source_target_pairs={{0,1},{1,0},{2,3},{3,2},{4,5},{5,4},{6,7},{7,6},{16,17},{17,16},{1... | collective-permute-start | bytes 1572872 | tf_op jit(solution)/shard_map/ppermute | solution.py:59
  96.9 11.4 %collective-permute-start.47 = (bf16[512,512]{1,0:T(8,128)(2,1)S(1)}, bf16[512,512]{1,0:T(8,128)(2,1)S(1)}, u32[]{:S(2)}, u32[]{:S(2)}) collective-permute-start(bf16[512,512]{1,0:T(8,128)(2,1)S(1)} %collective-permute-done.46.refs_19_), channel_id=1, source_target_pairs={{0,1},{1,0},{2,3},{3,2},{4,5},{5,4},{6,7},{7,6},{16,17},{17,16},{1... | collective-permute-start | bytes 1572872 | tf_op jit(solution)/shard_map/ppermute | solution.py:59
  99.8 16.5 %collective-permute-start.45 = (bf16[512,512]{1,0:T(8,128)(2,1)S(1)}, bf16[512,512]{1,0:T(8,128)(2,1)S(1)}, u32[]{:S(2)}, u32[]{:S(2)}) collective-permute-start(bf16[512,512]{1,0:T(8,128)(2,1)S(1)} %collective-permute-done.44.refs_16_), channel_id=1, source_target_pairs={{0,1},{1,0},{2,3},{3,2},{4,5},{5,4},{6,7},{7,6},{16,17},{17,16},{1... | collective-permute-start | bytes 1572872 | tf_op jit(solution)/shard_map/ppermute | solution.py:59
  132.6 12.5 %collective-permute-start.50 = (bf16[256,512]{1,0:T(8,128)(2,1)S(1)}, bf16[256,512]{1,0:T(8,128)(2,1)S(1)}, u32[]{:S(2)}, u32[]{:S(2)}) collective-permute-start(bf16[256,512]{1,0:T(8,128)(2,1)S(1)} %shard_map.115.refs_1_.refs_9_.refs_0_.refs_2_), channel_id=1, source_target_pairs={{0,48},{1,49},{2,50},{3,51},{4,52},{5,53},{6,54},{7,55},{16,0},{17... | collective-permute-start | bytes 786440 | tf_op jit(solution)/shard_map/ppermute | solution.py:59
  134.3 13.2 %collective-permute-start.49 = (bf16[256,512]{1,0:T(8,128)(2,1)S(1)}, bf16[256,512]{1,0:T(8,128)(2,1)S(1)}, u32[]{:S(2)}, u32[]{:S(2)}) collective-permute-start(bf16[256,512]{1,0:T(8,128)(2,1)S(1)} %shard_map.115.refs_1_.refs_9_.refs_0_.refs_2_), channel_id=1, source_target_pairs={{0,16},{1,17},{2,18},{3,19},{4,20},{5,21},{6,22},{7,23},{16,32},{1... | collective-permute-start | bytes 786440 | tf_op jit(solution)/shard_map/ppermute | solution.py:59
  134.3 27.8 %collective-permute-start.58 = (bf16[512,512]{1,0:T(8,128)(2,1)S(1)}, bf16[512,512]{1,0:T(8,128)(2,1)S(1)}, u32[]{:S(2)}, u32[]{:S(2)}) collective-permute-start(bf16[512,512]{1,0:T(8,128)(2,1)S(1)} %pad_maximum_fusion), channel_id=1, source_target_pairs={{0,2},{1,7},{2,4},{3,1},{4,6},{5,3},{6,0},{7,5},{16,18},{17,23},{1... | collective-permute-start | bytes 1572872 | tf_op jit(solution)/shard_map/ppermute | solution.py:59
  140.4 22.2 %collective-permute-start.62 = (bf16[512,512]{1,0:T(8,128)(2,1)S(1)}, bf16[512,512]{1,0:T(8,128)(2,1)S(1)}, u32[]{:S(2)}, u32[]{:S(2)}) collective-permute-start(bf16[512,512]{1,0:T(8,128)(2,1)S(1)} %collective-permute-done.56.refs_11_), channel_id=1, source_target_pairs={{0,7},{1,0},{2,1},{3,2},{4,3},{5,4},{6,5},{7,6},{16,23},{17,16},{1... | collective-permute-start | bytes 1572872 | tf_op jit(solution)/shard_map/ppermute | solution.py:59
  141.7 21.1 %collective-permute-start.60 = (bf16[512,512]{1,0:T(8,128)(2,1)S(1)}, bf16[512,512]{1,0:T(8,128)(2,1)S(1)}, u32[]{:S(2)}, u32[]{:S(2)}) collective-permute-start(bf16[512,512]{1,0:T(8,128)(2,1)S(1)} %collective-permute-done.56.refs_11_), channel_id=1, source_target_pairs={{0,2},{1,9},{2,4},{3,11},{4,6},{5,13},{6,0},{7,15},{16,18},{17,25}... | collective-permute-start | bytes 1572872 | tf_op jit(solution)/shard_map/ppermute | solution.py:59
  145.1 13.3 %collective-permute-start.48 = (bf16[256,512]{1,0:T(8,128)(2,1)S(1)}, bf16[256,512]{1,0:T(8,128)(2,1)S(1)}, u32[]{:S(2)}, u32[]{:S(2)}) collective-permute-start(bf16[256,512]{1,0:T(8,128)(2,1)S(1)} %shard_map.115.refs_1_.refs_9_.refs_0_.refs_2_), channel_id=1, source_target_pairs={{0,64},{1,65},{2,66},{3,67},{4,68},{5,69},{6,70},{7,71},{16,80},{1... | collective-permute-start | bytes 786440 | tf_op jit(solution)/shard_map/ppermute | solution.py:59
  147.5 14.6 %collective-permute-start.54 = (bf16[256,512]{1,0:T(8,128)(2,1)S(1)}, bf16[256,512]{1,0:T(8,128)(2,1)S(1)}, u32[]{:S(2)}, u32[]{:S(2)}) collective-permute-start(bf16[256,512]{1,0:T(8,128)(2,1)S(1)} %collective-permute-done.53.refs_7_.refs_6_.refs_8_), channel_id=1, source_target_pairs={{0,64},{1,65},{2,66},{3,67},{4,68},{5,69},{6,70},{7,71},{16,80},{1... | collective-permute-start | bytes 786440 | tf_op jit(solution)/shard_map/ppermute | solution.py:59
  162.1 11.6 %collective-permute-start.57 = (bf16[512,512]{1,0:T(8,128)(2,1)S(1)}, bf16[512,512]{1,0:T(8,128)(2,1)S(1)}, u32[]{:S(2)}, u32[]{:S(2)}) collective-permute-start(bf16[512,512]{1,0:T(8,128)(2,1)S(1)} %collective-permute-done.56.refs_11_), channel_id=1, source_target_pairs={{0,1},{1,0},{2,3},{3,2},{4,5},{5,4},{6,7},{7,6},{16,17},{17,16},{1... | collective-permute-start | bytes 1572872 | tf_op jit(solution)/shard_map/ppermute | solution.py:59
  162.2 11.6 %collective-permute-start.59 = (bf16[512,512]{1,0:T(8,128)(2,1)S(1)}, bf16[512,512]{1,0:T(8,128)(2,1)S(1)}, u32[]{:S(2)}, u32[]{:S(2)}) collective-permute-start(bf16[512,512]{1,0:T(8,128)(2,1)S(1)} %collective-permute-done.58.refs_13_), channel_id=1, source_target_pairs={{0,1},{1,0},{2,3},{3,2},{4,5},{5,4},{6,7},{7,6},{16,17},{17,16},{1... | collective-permute-start | bytes 1572872 | tf_op jit(solution)/shard_map/ppermute | solution.py:59
  178.2 12.4 %collective-permute-start.65 = (bf16[512,512]{1,0:T(8,128)(2,1)S(1)}, bf16[512,512]{1,0:T(8,128)(2,1)S(1)}, u32[]{:S(2)}, u32[]{:S(2)}) collective-permute-start(bf16[512,512]{1,0:T(8,128)(2,1)S(1)} %pad_maximum_fusion.1), channel_id=1, source_target_pairs={{0,8},{1,5},{2,10},{3,7},{4,12},{5,1},{6,14},{7,3},{16,24},{17,21}... | collective-permute-start | bytes 1572872 | tf_op jit(solution)/shard_map/ppermute | solution.py:59
  179.3 15.4 %collective-permute-start.67 = (bf16[512,512]{1,0:T(8,128)(2,1)S(1)}, bf16[512,512]{1,0:T(8,128)(2,1)S(1)}, u32[]{:S(2)}, u32[]{:S(2)}) collective-permute-start(bf16[512,512]{1,0:T(8,128)(2,1)S(1)} %pad_maximum_fusion.1), channel_id=1, source_target_pairs={{0,2},{1,7},{2,4},{3,1},{4,6},{5,3},{6,0},{7,5},{16,18},{17,23},{1... | collective-permute-start | bytes 1572872 | tf_op jit(solution)/shard_map/ppermute | solution.py:59
  190.9 13.5 %collective-permute-start.66 = (bf16[512,512]{1,0:T(8,128)(2,1)S(1)}, bf16[512,512]{1,0:T(8,128)(2,1)S(1)}, u32[]{:S(2)}, u32[]{:S(2)}) collective-permute-start(bf16[512,512]{1,0:T(8,128)(2,1)S(1)} %collective-permute-done.65.refs_10_), channel_id=1, source_target_pairs={{0,1},{1,0},{2,3},{3,2},{4,5},{5,4},{6,7},{7,6},{16,17},{17,16},{1... | collective-permute-start | bytes 1572872 | tf_op jit(solution)/shard_map/ppermute | solution.py:59
  (41 other events, 349.0 us)
